TPU v7x, 512 devices: a whole 4x4x16 slice. The times are simulated.
512 devices in a mesh: rep: 64 (over x, z), tp: 8 (over y, core).
Axes of the slice: x: 4, y: 4, z: 16, core: 2. Of those that a mesh axis runs over, the one named last changes fastest.
Arguments:
- queries: bfloat16 [8192, 4096], P(('rep', 'tp')), may hold values from -120 to 120
- fresh_kv: bfloat16 [8192, 2048], P(('rep', 'tp')), may hold values from -8 to 8
- kv_pool: bfloat16 [8192, 16, 2048], P('rep', None, 'tp'), may hold values from -6 to 6
- residual: bfloat16 [8192, 4096], P('rep', 'tp'), may hold values from -6 to 6
- norm_gain: float32 [4096], P('tp'), may hold values from 0.1 to 1.9
- gate_up: bfloat16 [64, 4096, 2048], P('rep', None, 'tp'), may hold values from -0.09375 to 0.09375
- down_proj: bfloat16 [64, 1024, 4096], P('rep', None, 'tp'), may hold values from -0.0625 to 0.0625
- prior_len: int32 [256], replicated, may hold values from 1 to 512, as said below
- new_len: int32 [256], replicated, may hold values from 16 to 32, as said below
- page_table: int32 [64, 128], P('rep'), may hold values from 0 to 127, each once within a row
- leaving: int32 [64], replicated, may hold values from 0 to 3
- expert_ids: int32 [8192, 2], P('rep'), may hold values from 0 to 7, all different within a row; in each aligned block of 128 rows (0 to 127, 128 to 255, ...) at most 40 rows name the same one
- route_logits: float32 [8192, 2], P('rep'), may hold values from -6 to 6
Outputs:
- output: bfloat16 [8192, 4096], P('rep', 'tp')
Inputs may be any that keep to these rules, and one draw needn't show every extreme that they name: `prior_len`: some request has exactly 512 earlier tokens. `new_len`: some request has exactly 32 live new tokens. `page_table`: each group's row names each of its 128 pages once. `expert_ids`: the two experts of a slot differ; among the 128 slots of one group no expert is named more than 40 times, and in some group one is named exactly 40 times.
All inputs are finite; a program needn't handle non-finite values.
Results may differ from a plain program's by a relative error of at most 0.0042.
Values may be sent and summed in bfloat16 or wider, within the bound.
No kernel may reach another device: no remote copies, remote signals or barrier semaphores. Data moves between devices by JAX's collectives and lax.ppermute only.
A program may use at most 128 MiB of HBM per device.

v0:
```python
import jax
import jax.numpy as jnp
from jax import lax
from jax.sharding import PartitionSpec as P

D = 4096
HD = 128
EXPERTS = 8
REQ = 4
FRESH = 32
PRIOR = 512
PAGE = 16
CAP = 40


epsilon = 1e-05


def shifted(value, axis, by):
    length = lax.axis_size(axis)
    return lax.ppermute(value, axis, [(i, (i + by) % length) for i in range(length)])


def attend_slots(query_rows, earlier, newer, prior_count, new_count):
    requests, fresh_len, q_width = query_rows.shape
    kv_heads = earlier.shape[2] // (2 * HD)
    group_size = q_width // HD // kv_heads
    keys_all = jnp.concatenate([earlier, newer], axis=1)
    span_len = keys_all.shape[1]
    prior_span = earlier.shape[1]
    paired = keys_all.reshape(requests, span_len, kv_heads, 2, HD)
    key_part = paired[:, :, :, 0]
    value_part = paired[:, :, :, 1]
    grouped = query_rows.reshape(requests, fresh_len, kv_heads, group_size, HD)
    scores = jnp.einsum(
        "rcgjd,rkgd->rgjck", grouped, key_part, preferred_element_type=jnp.float32
    ) * HD ** (-0.5)
    key_pos = jnp.arange(span_len, dtype=jnp.int32)
    key_offset = key_pos - prior_span
    query_pos = jnp.arange(fresh_len, dtype=jnp.int32)
    visible = jnp.where(
        key_pos[None, None, :] < prior_span,
        key_pos[None, None, :] < prior_count[:, None, None],
        (key_offset[None, None, :] <= query_pos[None, :, None])
        & (key_offset[None, None, :] < new_count[:, None, None]),
    )
    visible = visible[:, None, None]
    masked = jnp.where(visible, scores, -1e30)
    highest = jnp.max(masked, axis=-1, keepdims=True)
    expo = jnp.where(visible, jnp.exp(masked - highest), 0.0)
    totals = jnp.sum(expo, axis=-1, keepdims=True)
    weights = (expo / totals).astype(jnp.bfloat16)
    mixed = jnp.einsum("rgjck,rkgd->rcgjd", weights, value_part, preferred_element_type=jnp.float32)
    mixed = mixed.reshape(requests, fresh_len, q_width)
    return jnp.where(query_pos[None, :, None] < new_count[:, None, None], mixed, 0.0).astype(
        jnp.bfloat16
    )


def pick_slot(values, position):
    return lax.dynamic_index_in_dim(values, position, 0, keepdims=False)


def put_slot(values, update, position):
    return lax.dynamic_update_index_in_dim(values, update, position, 0)


def per_device(
    queries,
    fresh_kv,
    kv_pool,
    residual,
    norm_gain,
    gate_up,
    down_proj,
    prior_len,
    new_len,
    page_table,
    leaving,
    expert_ids,
    route_logits,
):
    replicas = lax.axis_size("rep")
    my_group = lax.axis_index("rep")
    prev_group = (my_group + replicas - 1) % replicas
    leave_slot = leaving[my_group]
    anchor_index = prev_group * REQ + leaving[prev_group]
    query_heads, kv_heads_rows = (
        lax.all_to_all(queries, "tp", split_axis=1, concat_axis=0, tiled=True),
        lax.all_to_all(fresh_kv, "tp", split_axis=1, concat_axis=0, tiled=True),
    )
    query_heads = query_heads.reshape(REQ, FRESH, -1)
    kv_heads_rows = kv_heads_rows.reshape(REQ, FRESH, -1)
    tables = page_table[0].reshape(REQ, PRIOR // PAGE)
    earlier = kv_pool[tables].reshape(REQ, PRIOR, -1)
    resid_slots = residual.reshape(REQ, FRESH, -1)
    own_prior = lax.dynamic_slice_in_dim(prior_len, my_group * REQ, REQ, 0)
    own_new = lax.dynamic_slice_in_dim(new_len, my_group * REQ, REQ, 0)
    arrived = shifted(
        (
            pick_slot(earlier, leave_slot),
            pick_slot(query_heads, leave_slot),
            pick_slot(kv_heads_rows, leave_slot),
            pick_slot(resid_slots, leave_slot),
        ),
        "rep",
        1,
    )
    earlier = put_slot(earlier, arrived[0], leave_slot)
    query_heads = put_slot(query_heads, arrived[1], leave_slot)
    kv_heads_rows = put_slot(kv_heads_rows, arrived[2], leave_slot)
    resid_slots = put_slot(resid_slots, arrived[3], leave_slot)
    counts_prior = own_prior.at[leave_slot].set(prior_len[anchor_index])
    counts_new = own_new.at[leave_slot].set(new_len[anchor_index])
    attention = attend_slots(query_heads, earlier, kv_heads_rows, counts_prior, counts_new)
    token_count = REQ * FRESH
    hidden = resid_slots.reshape(token_count, -1).astype(jnp.float32) + attention.reshape(
        token_count, -1
    ).astype(jnp.float32)
    squares = lax.psum(jnp.sum(hidden * hidden, axis=1), "tp")
    normed = (hidden * lax.rsqrt(squares / D + epsilon)[:, None] * norm_gain[None, :]).astype(
        jnp.bfloat16
    )
    per_expert = replicas // EXPERTS
    struck = (expert_ids[:, :, None] == jnp.arange(EXPERTS, dtype=jnp.int32)[None, None, :]).astype(
        jnp.int32
    )
    loads = jnp.sum(struck, axis=1)
    ahead = jnp.cumsum(loads, axis=0) - loads
    slot_of = jnp.sum(struck * ahead[:, None, :], axis=2)
    target = expert_ids * CAP + slot_of
    placing = jnp.any(
        target[:, :, None] == jnp.arange(EXPERTS * CAP, dtype=jnp.int32)[None, None, :], axis=1
    )
    placing = placing.astype(jnp.bfloat16)
    row_total = replicas * CAP
    hidden_dev = gate_up.shape[2] // 2
    local_in = gate_up[0]
    local_down = down_proj[0]
    whole = lax.all_gather(normed, "tp", axis=1, tiled=True)
    packed = jnp.einsum("te,tc->ec", placing, whole, preferred_element_type=jnp.float32).astype(
        jnp.bfloat16
    )
    packed = packed.reshape(EXPERTS, 1, CAP, packed.shape[-1])
    packed = jnp.broadcast_to(packed, (EXPERTS, per_expert, CAP, packed.shape[-1]))
    landed = lax.all_to_all(
        packed.reshape(replicas, CAP, -1), "rep", split_axis=0, concat_axis=0, tiled=True
    )
    gate_both = jnp.dot(landed.reshape(row_total, -1), local_in, preferred_element_type=jnp.float32)
    active = (jax.nn.silu(gate_both[:, :hidden_dev]) * gate_both[:, hidden_dev:]).astype(
        jnp.bfloat16
    )
    partial_value = jnp.dot(
        lax.all_gather(active, "tp", axis=1, tiled=True),
        local_down,
        preferred_element_type=jnp.float32,
    )
    returned = lax.all_to_all(
        partial_value.reshape(replicas, CAP, -1), "rep", split_axis=0, concat_axis=0, tiled=True
    )
    summed = jnp.sum(returned.reshape(EXPERTS, per_expert, CAP, -1), axis=1).reshape(
        EXPERTS * CAP, -1
    )
    shares = jax.nn.softmax(route_logits, axis=-1)
    moe_out = shares[:, 0:1] * summed[target[:, 0]] + shares[:, 1:2] * summed[target[:, 1]]
    return (hidden + moe_out).astype(jnp.bfloat16)


def solution(mesh):
    in_specs = (
        P(("rep", "tp"), None),
        P(("rep", "tp"), None),
        P("rep", None, "tp"),
        P("rep", "tp"),
        P("tp"),
        P("rep", None, "tp"),
        P("rep", None, "tp"),
        P(),
        P(),
        P("rep", None),
        P(),
        P("rep", None),
        P("rep", None),
    )
    out_specs = P("rep", "tp")
    return jax.shard_map(
        per_device, mesh=mesh, in_specs=in_specs, out_specs=out_specs, check_vma=False
    )
```

profile of v0, /device:TPU:1, one launch (start us, length us, event | category | flops | bytes accessed | tf_op | source)
XLA Modules:
  0.0 1347.5 jit_solution(16548631553993277854)
XLA Ops:
  6.5 1.1 copy.97
  7.6 1.3 fusion.20
  10.0 0.5 broadcast.190
  10.6 1.3 reduce.10
  12.7 1.9 gather_fusion
  14.6 0.7 dynamic-slice_bitcast_fusion
  15.3 4.4 collective-permute-start.1
  19.7 0.6 copy.89
  20.3 7.7 all-to-all-start
  28.0 0.6 dynamic-slice_bitcast_fusion.2
  28.6 1.9 collective-permute-start
  31.2 0.6 iota_compare_fusion.4
  32.0 0.6 iota_compare_fusion.1
  33.4 0.8 and_select_fusion
  34.2 1.3 iota_compare_fusion.5
  35.4 0.7 copy.88
  36.1 1.3 lt.140
  37.4 4.8 all-to-all-start.1
  42.3 0.8 bitcast_dynamic-update-slice_fusion.2
  43.0 0.6 dynamic-slice_bitcast_fusion.3
  43.6 3.2 collective-permute-start.2
  46.8 0.7 all-to-all-done.1
  47.5 4.1 collective-permute-start.3
  51.6 2.6 collective-permute-done.2
  54.2 0.7 bitcast_dynamic-update-slice_fusion.3
  54.9 3.0 collective-permute-done.3
  58.0 1.0 bitcast_dynamic-update-slice_fusion
  58.9 1.1 pad_maximum_fusion
  60.0 2.6 reshape.326
  62.6 1.6 fusion.19
  64.2 0.5 fusion.21
  65.2 0.5 convolution_bitcast_fusion
  66.1 13.5 %psum.7 = f32[128]{0:T(128)S(1)} all-reduce(f32[128]{0:T(128)S(1)} %reduce_sum.61), channel_id=1, replica_groups=mesh['rep'=64,'tp'=8] {'tp'}, use_global_device_ids=true, to_apply=%region_9.10 | all-reduce | flops 128 | bytes 1024 | tf_op jit(solution)/shard_map/psum | solution.py:120
  79.7 0.8 multiply_convert_fusion
  81.0 26.7 %all-gather.3.cloned.1.call-done = bf16[128,4096]{1,0:T(8,128)(2,1)} async-done(((bf16[128,512]{1,0:T(8,128)(2,1)}), bf16[128,4096]{1,0:T(8,128)(2,1)}) %all-gather.3.cloned.1.call-update) | async-done | bytes 1048592 | tf_op jit(solution)/shard_map/all_gather | solution.py:140
  107.7 2.1 convolution_convert_fusion
  109.7 2.5 broadcast_in_dim.112
  112.2 915.9 %all_to_all.42 = bf16[64,40,4096]{2,1,0:T(8,128)(2,1)S(1)} all-to-all(bf16[64,40,4096]{2,1,0:T(8,128)(2,1)S(1)} %bitcast.120), channel_id=1, replica_groups=mesh['rep'=64,'tp'=8] {'rep'}, dimensions={0} | all-to-all | bytes 41943040 | tf_op jit(solution)/shard_map/all_to_all | solution.py:146
  1028.1 6.2 fusion
  1034.3 1.2 fusion.3
  1035.6 47.0 %all-gather.5.cloned.1.call-done = bf16[2560,1024]{1,0:T(8,128)(2,1)} async-done(((bf16[2560,128]{1,0:T(8,128)(2,1)}), bf16[2560,1024]{1,0:T(8,128)(2,1)}) %all-gather.5.cloned.1.call-update) | async-done | bytes 5242896 | tf_op jit(solution)/shard_map/all_gather | solution.py:154
  1082.5 7.3 fusion.6
  1089.8 15.7 %all-to-all-start.3 = ((f32[64,40,512]{2,1,0:T(8,128)}), f32[64,40,512]{2,1,0:T(8,128)}, u32[]{:S(2)}, u32[]{:S(2)}) async-start(f32[64,40,512]{2,1,0:T(8,128)} %fusion.6), calls=%async_computation.3 | async-start | bytes 10485760 | tf_op jit(solution)/shard_map/all_to_all | solution.py:158
  1105.6 227.9 %all-to-all-done.3 = f32[64,40,512]{2,1,0:T(8,128)} async-done(((f32[64,40,512]{2,1,0:T(8,128)}), f32[64,40,512]{2,1,0:T(8,128)}, u32[]{:S(2)}, u32[]{:S(2)}) %all-to-all-start.3) | async-done | bytes 5242912 | tf_op jit(solution)/shard_map/all_to_all | solution.py:158
  1333.5 3.2 bitcast_reduce_fusion
  1336.7 0.8 gather_fusion.1
  1337.5 1.4 gather_fusion.2
  1338.9 1.8 add_convert_fusion
  (65 shorter events, 2.6 us)
Async XLA Ops:
  6.5 1021.6 %copy-start = (bf16[1,4096,256]{2,1,0:T(8,128)(2,1)S(1)}, bf16[1,4096,256]{2,1,0:T(8,128)(2,1)}, u32[]{:S(2)}) copy-start(bf16[1,4096,256]{2,1,0:T(8,128)(2,1)} %param.22) | copy-start | bytes 6291460
  12.6 7.1 copy-start.3
  12.6 19.2 %copy-start.9 = (s32[256]{0:T(256)S(1)}, s32[256]{0:T(256)}, u32[]{:S(2)}) copy-start(s32[256]{0:T(256)} %param.25) | copy-start | bytes 3076
  12.7 19.2 %copy-start.8 = (s32[256]{0:T(256)S(1)}, s32[256]{0:T(256)}, u32[]{:S(2)}) copy-start(s32[256]{0:T(256)} %param.24) | copy-start | bytes 3076
  12.7 22.8 %copy-start.2 = (bf16[16,4096]{1,0:T(8,128)(2,1)S(1)}, bf16[16,4096]{1,0:T(8,128)(2,1)}, u32[]{:S(2)}) copy-start(bf16[16,4096]{1,0:T(8,128)(2,1)} %param.17) | copy-start | bytes 393220
  15.3 42.6 %collective-permute-start.1 = (bf16[512,256]{1,0:T(8,128)(2,1)}, bf16[512,256]{1,0:T(8,128)(2,1)}, u32[]{:S(2)}, u32[]{:S(2)}) collective-permute-start(bf16[512,256]{1,0:T(8,128)(2,1)} %dynamic-slice_bitcast_fusion), channel_id=1, source_target_pairs={{0,8},{8,16},{16,24},{24,32},{32,40},{40,48},{48,56},{56,64},{64,7... | collective-permute-start | bytes 786440 | tf_op jit(solution)/shard_map/ppermute | solution.py:21
  20.3 17.1 %all-to-all-start = ((bf16[16,8,256]{2,0,1:T(8,128)(2,1)}), bf16[16,8,256]{2,0,1:T(8,128)(2,1)S(1)}, u32[]{:S(2)}, u32[]{:S(2)}) async-start(bf16[16,8,256]{2,0,1:T(8,128)(2,1)} %bitcast.119), calls=%async_computation | async-start | bytes 131072 | tf_op jit(solution)/shard_map/all_to_all | solution.py:90
  28.6 13.6 %collective-permute-start = (bf16[32,512]{1,0:T(8,128)(2,1)}, bf16[32,512]{1,0:T(8,128)(2,1)}, u32[]{:S(2)}, u32[]{:S(2)}) collective-permute-start(bf16[32,512]{1,0:T(8,128)(2,1)} %dynamic-slice_bitcast_fusion.2), channel_id=1, source_target_pairs={{0,8},{8,16},{16,24},{24,32},{32,40},{40,48},{48,56},{56,64},{64,7... | collective-permute-start | bytes 98312 | tf_op jit(solution)/shard_map/ppermute | solution.py:21
  32.7 0.5 copy-start.11
  37.4 10.1 all-to-all-start.1
  42.2 65.4 %all-gather.3.cloned.1.call-start = ((), (), s32[]{:S(2)}) async-start(), calls=%async_computation.4 | async-start | bytes 1179648 | tf_op jit(solution)/shard_map/all_gather | solution.py:140
  43.6 10.6 collective-permute-start.2
  47.5 10.4 collective-permute-start.3
  65.1 0.7 copy-start.10
  65.1 14.5 %copy-start.6 = (f32[512]{0:T(512)S(1)}, f32[512]{0:T(512)}, u32[]{:S(2)}) copy-start(f32[512]{0:T(512)} %param.21) | copy-start | bytes 6148
  65.2 14.5 %copy-start.7 = (pred[128]{0:T(512)(128)(4,1)S(1)}, pred[128]{0:T(512)(128)(4,1)}, u32[]{:S(2)}) copy-start(pred[128]{0:T(512)(128)(4,1)} %lt.140) | copy-start | bytes 388
  65.7 14.8 %copy-start.4 = (s32[128,2]{0,1:T(2,128)S(1)}, s32[128,2]{0,1:T(2,128)}, u32[]{:S(2)}) copy-start(s32[128,2]{0,1:T(2,128)} %param.28) | copy-start | bytes 3076
  80.5 1002.1 %all-gather.5.cloned.1.call-start = ((), (), s32[]{:S(2)}) async-start(), calls=%async_computation.5 | async-start | bytes 5898240 | tf_op jit(solution)/shard_map/all_gather | solution.py:154
  1034.3 48.2 %copy-start.12 = (bf16[1,1024,512]{2,1,0:T(8,128)(2,1)S(1)}, bf16[1,1024,512]{2,1,0:T(8,128)(2,1)}, u32[]{:S(2)}) copy-start(bf16[1,1024,512]{2,1,0:T(8,128)(2,1)} %param.23) | copy-start | bytes 3145732
  1089.8 15.7 %copy-start.5 = (f32[128,2]{0,1:T(2,128)S(1)}, f32[128,2]{0,1:T(2,128)}, u32[]{:S(2)}) copy-start(f32[128,2]{0,1:T(2,128)} %param.29) | copy-start | bytes 3076
  1089.8 243.7 %all-to-all-start.3 = ((f32[64,40,512]{2,1,0:T(8,128)}), f32[64,40,512]{2,1,0:T(8,128)}, u32[]{:S(2)}, u32[]{:S(2)}) async-start(f32[64,40,512]{2,1,0:T(8,128)} %fusion.6), calls=%async_computation.3 | async-start | bytes 10485760 | tf_op jit(solution)/shard_map/all_to_all | solution.py:158
  1337.5 3.2 copy-start.1
Sparse Core Ops, SparseCore 0:
  80.6 27.0 all-gather.2
  1035.7 46.7 all-gather.4
where the time goes:
time: 1350 us
  blocking collectives  929 us (69%)
  waiting for transfers between devices  308 us (23%)
  starting transfers between devices  41.7 us (3%)
  local copies, waits for them, and re-layouts  22 us (2%)
  matrix products  16.5 us (1%)
  between operations  16.1 us (1%)
  other arithmetic  13.9 us (1%)
    all_to_all x1, blocking collectives, per_device(): lax.all_to_all(packed.reshape(replicas, CAP, -1), 'rep', split_axis=0, co...  916 us
    all_to_all x1, waiting for transfers between devices, per_device(): lax.all_to_all(partial_value.reshape(replicas, CAP, -1), 'rep', split_axi...  228 us
    all_gather x1, waiting for transfers between devices, per_device(): lax.all_gather(active, 'tp', axis=1, tiled=True)  47 us
  transfers between devices with their start and end apart: 9, of which 6 were waited for; matrix products, arithmetic and copies ran while one was open for 1% of the time, Pallas kernels for 0%

commit v1 on v0

v1 whole, which is shorter than its diff:
```python
import functools

import jax
import jax.numpy as jnp
from jax import lax
from jax.experimental import pallas as pl
from jax.experimental.pallas import tpu as pltpu
from jax.sharding import Mesh
from jax.sharding import PartitionSpec as P

D = 4096
HD = 128
EXPERTS = 8
REQ = 4
FRESH = 32
PRIOR = 512
PAGE = 16
CAP = 40

NX, NZ, NY, NC = 4, 16, 4, 2
N_REP = NX * NZ
N_TP = NY * NC
REP = ("x", "z")
TP = ("y", "c")
SPREAD = ("x", "y", "c")
SHARE = CAP // N_TP
PIECE = 2 * SHARE
ROWS = NX * PIECE
ALL_ROWS = NZ * ROWS
OWN_ROWS = ALL_ROWS // 2
WIDE = 640

epsilon = 1e-05


def attend_slots(query_rows, earlier, newer, prior_count, new_count):
    requests, fresh_len, q_width = query_rows.shape
    group_size = q_width // HD
    keys_all = jnp.concatenate([earlier, newer], axis=1)
    span_len = keys_all.shape[1]
    prior_span = earlier.shape[1]
    key_part = keys_all[:, :, :HD]
    value_part = keys_all[:, :, HD:]
    grouped = query_rows.reshape(requests, fresh_len, group_size, HD)
    scores = jnp.einsum(
        "rcjd,rkd->rjck", grouped, key_part, preferred_element_type=jnp.float32
    ) * HD ** (-0.5)
    key_pos = jnp.arange(span_len, dtype=jnp.int32)
    key_offset = key_pos - prior_span
    query_pos = jnp.arange(fresh_len, dtype=jnp.int32)
    visible = jnp.where(
        key_pos[None, None, :] < prior_span,
        key_pos[None, None, :] < prior_count[:, None, None],
        (key_offset[None, None, :] <= query_pos[None, :, None])
        & (key_offset[None, None, :] < new_count[:, None, None]),
    )
    visible = visible[:, None]
    masked = jnp.where(visible, scores, -1e30)
    highest = jnp.max(masked, axis=-1, keepdims=True)
    expo = jnp.where(visible, jnp.exp(masked - highest), 0.0)
    totals = jnp.sum(expo, axis=-1, keepdims=True)
    weights = (expo / totals).astype(jnp.bfloat16)
    mixed = jnp.einsum("rjck,rkd->rcjd", weights, value_part, preferred_element_type=jnp.float32)
    mixed = mixed.reshape(requests, fresh_len, q_width)
    return jnp.where(query_pos[None, :, None] < new_count[:, None, None], mixed, 0.0).astype(
        jnp.bfloat16
    )


def norm_kernel(recv_ref, out_ref, rows):
    for xs in range(NX):
        total = jnp.zeros((PIECE, 128), jnp.float32)
        for ts in range(N_TP):
            piece = recv_ref[xs * N_TP + ts].astype(jnp.float32)
            rows[xs * PIECE : (xs + 1) * PIECE, ts * 512 : (ts + 1) * 512] = piece[:, :512]
            total = total + piece[:, 512:]
        square = jnp.sum(total, axis=1, keepdims=True)
        scale = lax.rsqrt(square * (1.0 / D) + epsilon)
        here = slice(xs * PIECE, (xs + 1) * PIECE)
        rows[here, :] = rows[here, :] * scale
    out_ref[...] = rows[...].astype(jnp.bfloat16)


def norm_rows(received):
    return pl.pallas_call(
        norm_kernel,
        out_shape=jax.ShapeDtypeStruct((ROWS, D), jnp.bfloat16),
        scratch_shapes=[pltpu.VMEM((ROWS, D), jnp.float32)],
        name="norm_rows",
    )(received)


def expert_kernel(all_ref, take_ref, put_ref, in_ref, down_ref, out_ref, rows, active):
    step = pl.program_id(0)

    @pl.when(step == 0)
    def _():
        for n in range(8):
            part = slice(n * 512, (n + 1) * 512)
            rows[:, part] = jnp.dot(
                take_ref[...], all_ref[:, part], preferred_element_type=jnp.float32
            ).astype(jnp.bfloat16)

    @pl.when(step < N_TP)
    def _():
        both = jnp.dot(rows[...], in_ref[0], preferred_element_type=jnp.float32)
        gate = both[:, :128]
        value = (gate / (1.0 + jnp.exp(-gate)) * both[:, 128:]).astype(jnp.bfloat16)
        for t in range(N_TP):

            @pl.when(step == t)
            def _():
                active[:, t * 128 : (t + 1) * 128] = value

    @pl.when(step >= N_TP)
    def _():
        part = jnp.dot(active[...], down_ref[0], preferred_element_type=jnp.float32)
        out_ref[...] = jnp.dot(
            put_ref[...], part.astype(jnp.bfloat16), preferred_element_type=jnp.float32
        ).astype(jnp.bfloat16)


def run_experts(all_rows, take, put, weights_in, weights_down):
    last = N_TP - 1
    return pl.pallas_call(
        expert_kernel,
        out_shape=jax.ShapeDtypeStruct((ALL_ROWS, D), jnp.bfloat16),
        grid=(2 * N_TP,),
        in_specs=[
            pl.BlockSpec((ALL_ROWS, D), lambda j: (0, 0), pipeline_mode=pl.Buffered(1)),
            pl.BlockSpec((OWN_ROWS, ALL_ROWS), lambda j: (0, 0), pipeline_mode=pl.Buffered(1)),
            pl.BlockSpec((ALL_ROWS, OWN_ROWS), lambda j: (0, 0), pipeline_mode=pl.Buffered(1)),
            pl.BlockSpec((1, D, 256), lambda j: (jnp.minimum(j, last), 0, 0)),
            pl.BlockSpec((1, 1024, 512), lambda j: (jnp.maximum(j - N_TP, 0), 0, 0)),
        ],
        out_specs=pl.BlockSpec((ALL_ROWS, 512), lambda j: (0, jnp.maximum(j - N_TP, 0))),
        scratch_shapes=[
            pltpu.VMEM((OWN_ROWS, D), jnp.bfloat16),
            pltpu.VMEM((OWN_ROWS, 1024), jnp.bfloat16),
        ],
        compiler_params=pltpu.CompilerParams(
            dimension_semantics=("arbitrary",), vmem_limit_bytes=40 << 20
        ),
        name="experts",
    )(all_rows, take, put, weights_in, weights_down)


def three_parts(values):
    parts = []
    for _ in range(3):
        head = lax.reduce_precision(values, 8, 7)
        parts.append(head.astype(jnp.bfloat16))
        values = values - head
    return parts


def per_device(
    queries,
    fresh_kv,
    kv_pool,
    residual,
    norm_gain,
    gate_up,
    down_proj,
    prior_len,
    new_len,
    page_table,
    leaving,
    expert_ids,
    route_logits,
):
    my_z = lax.axis_index("z")
    my_group = lax.axis_index("x") * NZ + my_z
    leave_slot = leaving[my_group]
    handing = [(i, (i + 1) % N_REP) for i in range(N_REP)]

    weights_down = lax.all_gather(down_proj[0], TP)
    weights_in = lax.all_gather(gate_up[0], TP)

    query_heads = lax.all_to_all(queries, TP, split_axis=1, concat_axis=0, tiled=True)
    kv_rows = lax.all_to_all(fresh_kv, TP, split_axis=1, concat_axis=0, tiled=True)
    resid_slots = residual.reshape(REQ, FRESH, -1)
    resid_came = lax.ppermute(
        lax.dynamic_index_in_dim(resid_slots, leave_slot, 0, keepdims=False), REP, handing
    )
    tables = page_table[0].reshape(REQ, PRIOR // PAGE)
    earlier = kv_pool[tables].reshape(REQ, PRIOR, -1)
    own_prior = lax.dynamic_slice_in_dim(prior_len, my_group * REQ, REQ, 0)
    own_new = lax.dynamic_slice_in_dim(new_len, my_group * REQ, REQ, 0)
    attention = attend_slots(
        query_heads.reshape(REQ, FRESH, -1),
        earlier,
        kv_rows.reshape(REQ, FRESH, -1),
        own_prior,
        own_new,
    )
    attention_came = lax.ppermute(
        lax.dynamic_index_in_dim(attention, leave_slot, 0, keepdims=False), REP, handing
    )
    is_new = (jnp.arange(REQ, dtype=jnp.int32) == leave_slot)[:, None, None]
    resid_new = jnp.where(is_new, resid_came[None], resid_slots).astype(jnp.float32)
    attention_new = jnp.where(is_new, attention_came[None], attention).astype(jnp.float32)
    token_count = REQ * FRESH
    hidden = (resid_new + attention_new).reshape(token_count, -1)

    struck = (
        expert_ids[:, :, None] == jnp.arange(EXPERTS, dtype=jnp.int32)[None, None, :]
    ).astype(jnp.bfloat16)
    loads = struck[:, 0] + struck[:, 1]
    earlier_rows = (
        jnp.arange(token_count, dtype=jnp.int32)[:, None]
        > jnp.arange(token_count, dtype=jnp.int32)[None, :]
    ).astype(jnp.bfloat16)
    ahead = jnp.dot(earlier_rows, loads, preferred_element_type=jnp.float32)
    place = jnp.sum(struck.astype(jnp.float32) * ahead[:, None, :], axis=2).astype(jnp.int32)
    target = (
        ((expert_ids // 2) * N_TP + place // SHARE) * PIECE + (expert_ids % 2) * SHARE + place % SHARE
    )
    slots = jnp.arange(EXPERTS * CAP, dtype=jnp.int32)
    placing = (
        (target[:, 0][None, :] == slots[:, None]) | (target[:, 1][None, :] == slots[:, None])
    ).astype(jnp.bfloat16)

    squares = three_parts(jnp.sum(hidden * hidden, axis=1))
    extra = jnp.stack(squares + [jnp.zeros_like(squares[0])], axis=1)
    extra = jnp.pad(extra, ((0, 0), (0, WIDE - 512 - 4)))
    payload = jnp.concatenate(
        [(hidden * norm_gain[None, :]).astype(jnp.bfloat16), extra], axis=1
    )
    packed = jnp.dot(placing, payload, preferred_element_type=jnp.float32).astype(jnp.bfloat16)
    received = lax.all_to_all(packed.reshape(NX * N_TP, PIECE, WIDE), SPREAD, 0, 0)
    normed = norm_rows(received.reshape(NX * N_TP, PIECE, WIDE))
    all_rows = lax.all_gather(normed, "z", tiled=True)

    index = jnp.arange(ALL_ROWS, dtype=jnp.int32)
    own = (index // SHARE) % 2 == my_z // 8
    compact = jnp.where(own, (index // PIECE) * SHARE + index % SHARE, -1)
    own_index = jnp.arange(OWN_ROWS, dtype=jnp.int32)
    take = (own_index[:, None] == compact[None, :]).astype(jnp.bfloat16)
    put = (compact[:, None] == own_index[None, :]).astype(jnp.bfloat16)
    partial_rows = run_experts(all_rows, take, put, weights_in, weights_down)
    summed = lax.psum_scatter(partial_rows, "z", scatter_dimension=0, tiled=True)
    back = summed.reshape(NX, PIECE, N_TP, 512).transpose(0, 2, 1, 3)
    returned = lax.all_to_all(back.reshape(NX * N_TP, PIECE, 512), SPREAD, 0, 0)
    returned = returned.reshape(EXPERTS * CAP, 512)
    shares = jax.nn.softmax(route_logits, axis=-1)
    first = (target[:, 0][:, None] == slots[None, :]).astype(jnp.bfloat16)
    second = (target[:, 1][:, None] == slots[None, :]).astype(jnp.bfloat16)
    moe_out = shares[:, 0:1] * jnp.dot(
        first, returned, preferred_element_type=jnp.float32
    ) + shares[:, 1:2] * jnp.dot(second, returned, preferred_element_type=jnp.float32)
    return (hidden + moe_out).astype(jnp.bfloat16)


def solution(mesh):
    inner = Mesh(mesh.devices.reshape(NX, NZ, NY, NC), ("x", "z", "y", "c"))
    every = ("x", "z", "y", "c")
    in_specs = (
        P(every, None),
        P(every, None),
        P(REP, None, TP),
        P(REP, TP),
        P(TP),
        P(REP, None, TP),
        P(REP, None, TP),
        P(),
        P(),
        P(REP, None),
        P(),
        P(REP, None),
        P(REP, None),
    )
    return jax.shard_map(
        per_device, mesh=inner, in_specs=in_specs, out_specs=P(REP, TP), check_vma=False
    )
```

time: 1350 us -> 445 us (0.33)
  blocking collectives: 929 us -> 18 us
  Pallas kernels: 0 us -> 24.9 us
  waiting for transfers between devices: 308 us -> 324 us
    all_to_all x1, blocking collectives: 916 us -> 18 us  [per_device(): lax.all_to_all(packed.reshape(NX * N_TP, PIECE, WIDE), SPREAD, 0, 0)]
    all_to_all x3, waiting for transfers between devices: 229 us -> 16.4 us  [the longest x1 11.6 us: per_device(): returned = lax.all_to_all(back.reshape(NX * N_TP, PIECE, 512), SPREAD, 0, 0)]
    all_gather x2 -> x3, waiting for transfers between devices: 73.6 us -> 225 us  [the longest x1 95.1 us: per_device(): weights_in = lax.all_gather(gate_up[0], TP)]
    reduce_scatter x0 -> x1, waiting for transfers between devices: none -> 73.4 us  [per_device(): lax.psum_scatter(partial_rows, 'z', scatter_dimension=0, tiled=True)]
    pallas_call x0 -> x2, Pallas kernels: none -> 24.9 us  [the longest x1 22.9 us: run_experts(): pl.pallas_call(expert_kernel, out_shape=jax.ShapeDtypeStruct((ALL_ROWS, D...]
  transfers between devices with their start and end apart: 9 -> 9, of which waited for: 6 -> 7; matrix products, arithmetic and copies ran while one was open for 1% -> 3% of each run, Pallas kernels for 0% -> 0%
where the time goes in v1:
time: 445 us; the launch traced here: 444 us
  waiting for transfers between devices  324 us (73%)
  starting transfers between devices  35.4 us (8%)
  Pallas kernels  24.9 us (6%)
  blocking collectives  18 us (4%)
  local copies, waits for them, and re-layouts  16.5 us (4%)
  between operations  15.3 us (3%)
  other arithmetic  5.1 us (1%)
  matrix products  5.08 us (1%)
    all_gather x1, waiting for transfers between devices, per_device(): weights_in = lax.all_gather(gate_up[0], TP)  95.1 us
    reduce_scatter x1, waiting for transfers between devices, per_device(): lax.psum_scatter(partial_rows, 'z', scatter_dimension=0, tiled=True)  73.4 us
    all_gather x1, waiting for transfers between devices, per_device(): all_rows = lax.all_gather(normed, 'z', tiled=True)  67.5 us
    all_gather x1, waiting for transfers between devices, per_device(): weights_down = lax.all_gather(down_proj[0], TP)  62.6 us
    pallas_call x1, Pallas kernels, run_experts(): pl.pallas_call(expert_kernel, out_shape=jax.ShapeDtypeStruct((ALL_ROWS, D...  22.9 us
    all_to_all x1, blocking collectives, per_device(): lax.all_to_all(packed.reshape(NX * N_TP, PIECE, WIDE), SPREAD, 0, 0)  18 us
    all_to_all x1, starting transfers between devices, per_device(): returned = lax.all_to_all(back.reshape(NX * N_TP, PIECE, 512), SPREAD, 0, 0)  16.5 us
    all_to_all x1, waiting for transfers between devices, per_device(): returned = lax.all_to_all(back.reshape(NX * N_TP, PIECE, 512), SPREAD, 0, 0)  11.6 us
  transfers between devices with their start and end apart: 9, of which 7 were waited for; matrix products, arithmetic and copies ran while one was open for 3% of the time, Pallas kernels for 0%

profile of v1, /device:TPU:1, one launch (start us, length us, event | category | flops | bytes accessed | tf_op | source)
XLA Modules:
  0.0 444.1 jit_solution(17505133824203455861)
XLA Ops:
  6.5 1.7 copy.61
  8.2 10.2 %all-to-all-start.1 = ((bf16[16,8,512]{2,0,1:T(8,128)(2,1)}), bf16[16,8,512]{2,0,1:T(8,128)(2,1)S(1)}, u32[]{:S(2)}, u32[]{:S(2)}) async-start(bf16[16,8,512]{2,0,1:T(8,128)(2,1)} %bitcast.95), calls=%async_computation.1 | async-start | bytes 262144 | tf_op jit(solution)/shard_map/all_to_all | solution.py:180
  18.3 1.3 dynamic_slice.16
  21.6 0.8 dynamic-slice_bitcast_fusion
  22.3 1.9 collective-permute-start
  24.3 0.8 dynamic_slice.18
  25.0 0.8 dynamic_slice.19
  25.8 0.6 broadcast.333
  26.4 1.4 reduce.3
  27.9 1.5 copy.62
  29.4 0.7 fusion.50
  30.1 0.1 fusion.44
  30.2 0.7 multiply_reduce_fusion.1
  30.9 0.7 fusion.66
  31.7 0.6 gather_fusion
  32.5 4.8 %all-to-all-start = ((bf16[16,8,256]{2,0,1:T(8,128)(2,1)}), bf16[16,8,256]{2,0,1:T(8,128)(2,1)S(1)}, u32[]{:S(2)}, u32[]{:S(2)}) async-start(bf16[16,8,256]{2,0,1:T(8,128)(2,1)} %bitcast.96), calls=%async_computation | async-start | bytes 131072 | tf_op jit(solution)/shard_map/all_to_all | solution.py:181
  37.4 4.8 %all-to-all-done = bf16[16,8,256]{2,0,1:T(8,128)(2,1)S(1)} async-done(((bf16[16,8,256]{2,0,1:T(8,128)(2,1)}), bf16[16,8,256]{2,0,1:T(8,128)(2,1)S(1)}, u32[]{:S(2)}, u32[]{:S(2)}) %all-to-all-start) | async-done | bytes 65568 | tf_op jit(solution)/shard_map/all_to_all | solution.py:181
  42.2 1.7 fusion.81
  43.9 1.7 fusion.11
  45.8 1.9 collective-permute-start.1
  47.7 0.6 iota_compare_fusion.17
  48.8 7.4 %collective-permute-done.1 = bf16[32,512]{1,0:T(8,128)(2,1)S(1)} collective-permute-done((bf16[32,512]{1,0:T(8,128)(2,1)S(1)}, bf16[32,512]{1,0:T(8,128)(2,1)S(1)}, u32[]{:S(2)}, u32[]{:S(2)}) %collective-permute-start.1) | collective-permute-done | bytes 32800 | tf_op jit(solution)/shard_map/ppermute | solution.py:197
  56.2 0.2 multiply_convert_fusion
  56.4 0.1 multiply_reduce_fusion
  56.6 0.1 copy.33
  56.7 0.3 convolution_convert_fusion
  57.0 0.1 reshape.316
  57.1 18.0 %all_to_all.42.recv_ref = bf16[32,10,640]{2,1,0:T(8,128)(2,1)} all-to-all(bf16[32,10,640]{2,1,0:T(8,128)(2,1)S(1)} %reshape.316), channel_id=1, replica_groups=mesh['x'=4,'z'=16,'y'=4,'c'=2] {'x','y','c'}, dimensions={0} | all-to-all | bytes 819200 | tf_op jit(solution)/shard_map/all_to_all | solution.py:231
  75.1 2.0 norm_rows.1
  77.2 0.7 all-gather.8.cloned.1.call-update
  78.0 0.7 all-gather.6.cloned.1.call-update
  78.7 0.1 fusion.10.take_ref
  78.8 0.2 fusion.9.put_ref
  79.0 67.5 %all-gather.4.cloned.1.call-done.all_ref = bf16[640,4096]{1,0:T(8,128)(2,1)} async-done(((bf16[40,4096]{1,0:T(8,128)(2,1)}), bf16[640,4096]{1,0:T(8,128)(2,1)}) %all-gather.4.cloned.1.call-update) | async-done | bytes 5242896 | tf_op jit(solution)/shard_map/all_gather | solution.py:233
  146.5 62.6 %all-gather.8.cloned.1.call-done.down_ref = bf16[8,1024,512]{2,1,0:T(8,128)(2,1)} async-done(((bf16[1,1024,512]{2,1,0:T(8,128)(2,1)}), bf16[8,1024,512]{2,1,0:T(8,128)(2,1)}) %all-gather.8.cloned.1.call-update) | async-done | bytes 8388624 | tf_op jit(solution)/shard_map/all_gather | solution.py:177
  209.0 95.1 %all-gather.6.cloned.1.call-done.in_ref = bf16[8,4096,256]{2,1,0:T(8,128)(2,1)} async-done(((bf16[1,4096,256]{2,1,0:T(8,128)(2,1)}), bf16[8,4096,256]{2,1,0:T(8,128)(2,1)}) %all-gather.6.cloned.1.call-update) | async-done | bytes 16777232 | tf_op jit(solution)/shard_map/all_gather | solution.py:178
  304.1 2.5 copy-done.2
  306.6 22.9 %experts.1 = bf16[640,4096]{1,0:T(8,128)(2,1)S(1)} custom-call(bf16[640,4096]{1,0:T(8,128)(2,1)S(1)} %copy-done.2, bf16[320,640]{1,0:T(8,128)(2,1)S(1)} %fusion.10.take_ref, bf16[640,320]{1,0:T(8,128)(2,1)S(1)} %fusion.9.put_ref, bf16[8,4096,256]{2,1,0:T(8,128)(2,1)} %all-gather.6.cloned.1.call-done.in_ref, ...), custom_call_target="tpu_custom_call" | custom-call | tf_op jit(solution)/shard_map/experts/pallas_call | solution.py:125
  329.5 2.3 copy-done.1
  331.9 0.7 copy-done.4
  332.6 73.4 %reduce-scatter.2.cloned.1.call-done = bf16[40,4096]{1,0:T(8,128)(2,1)} async-done(((bf16[640,4096]{1,0:T(8,128)(2,1)}), bf16[40,4096]{1,0:T(8,128)(2,1)}) %reduce-scatter.2.cloned.1.call-update) | async-done | bytes 327696 | tf_op jit(solution)/shard_map/reduce_scatter | solution.py:242
  406.0 1.1 copy.42
  407.1 1.0 copy.35
  408.1 16.5 %all-to-all-start.3 = ((bf16[32,10,512]{2,1,0:T(8,128)(2,1)}), bf16[32,10,512]{2,1,0:T(8,128)(2,1)S(1)}, u32[]{:S(2)}, u32[]{:S(2)}) async-start(bf16[32,10,512]{2,1,0:T(8,128)(2,1)} %copy.35), calls=%async_computation.4 | async-start | bytes 1048576 | tf_op jit(solution)/shard_map/all_to_all | solution.py:244
  424.7 11.6 %all-to-all-done.3 = bf16[32,10,512]{2,1,0:T(8,128)(2,1)S(1)} async-done(((bf16[32,10,512]{2,1,0:T(8,128)(2,1)}), bf16[32,10,512]{2,1,0:T(8,128)(2,1)S(1)}, u32[]{:S(2)}, u32[]{:S(2)}) %all-to-all-start.3) | async-done | bytes 327712 | tf_op jit(solution)/shard_map/all_to_all | solution.py:244
  436.2 0.1 reshape.319
  436.4 0.3 convolution_multiply_fusion.2
  436.6 0.9 fusion.8
  (45 shorter events, 1.3 us)
Async XLA Ops:
  6.5 25.2 %copy-start = (bf16[128,16,256]{2,1,0:T(8,128)(2,1)S(1)}, bf16[128,16,256]{2,1,0:T(8,128)(2,1)}, u32[]{:S(2)}) copy-start(bf16[128,16,256]{2,1,0:T(8,128)(2,1)} %param.15) | copy-start | bytes 3145732
  8.2 24.3 %all-to-all-start.1 = ((bf16[16,8,512]{2,0,1:T(8,128)(2,1)}), bf16[16,8,512]{2,0,1:T(8,128)(2,1)S(1)}, u32[]{:S(2)}, u32[]{:S(2)}) async-start(bf16[16,8,512]{2,0,1:T(8,128)(2,1)} %bitcast.95), calls=%async_computation.1 | async-start | bytes 262144 | tf_op jit(solution)/shard_map/all_to_all | solution.py:180
  22.3 26.4 %collective-permute-start = (bf16[32,512]{1,0:T(8,128)(2,1)S(1)}, bf16[32,512]{1,0:T(8,128)(2,1)S(1)}, u32[]{:S(2)}, u32[]{:S(2)}) collective-permute-start(bf16[32,512]{1,0:T(8,128)(2,1)S(1)} %dynamic-slice_bitcast_fusion), channel_id=1, source_target_pairs={{0,8},{8,16},{16,24},{24,32},{32,40},{40,48},{48,56},{56,64},{64,7... | collective-permute-start | bytes 98312 | tf_op jit(solution)/shard_map/ppermute | solution.py:183
  32.5 9.7 %all-to-all-start = ((bf16[16,8,256]{2,0,1:T(8,128)(2,1)}), bf16[16,8,256]{2,0,1:T(8,128)(2,1)S(1)}, u32[]{:S(2)}, u32[]{:S(2)}) async-start(bf16[16,8,256]{2,0,1:T(8,128)(2,1)} %bitcast.96), calls=%async_computation | async-start | bytes 131072 | tf_op jit(solution)/shard_map/all_to_all | solution.py:181
  37.3 109.1 %all-gather.4.cloned.1.call-start = ((), (), s32[]{:S(2)}) async-start(), calls=%async_computation.5 | async-start | bytes 5570560 | tf_op jit(solution)/shard_map/all_gather | solution.py:233
  43.9 12.3 %copy-start.3 = (bf16[128,512]{1,0:T(8,128)(2,1)S(1)}, bf16[128,512]{1,0:T(8,128)(2,1)}, u32[]{:S(2)}) copy-start(bf16[128,512]{1,0:T(8,128)(2,1)} %param.16) | copy-start | bytes 393220
  43.9 12.3 %copy-start.5 = (f32[512]{0:T(512)S(1)}, f32[512]{0:T(512)}, u32[]{:S(2)}) copy-start(f32[512]{0:T(512)} %param.17) | copy-start | bytes 6148
  45.8 10.4 %collective-permute-start.1 = (bf16[32,512]{1,0:T(8,128)(2,1)S(1)}, bf16[32,512]{1,0:T(8,128)(2,1)S(1)}, u32[]{:S(2)}, u32[]{:S(2)}) collective-permute-start(bf16[32,512]{1,0:T(8,128)(2,1)S(1)} %fusion.45), channel_id=1, source_target_pairs={{0,8},{8,16},{16,24},{24,32},{32,40},{40,48},{48,56},{56,64},{64,7... | collective-permute-start | bytes 98312 | tf_op jit(solution)/shard_map/ppermute | solution.py:197
  77.2 131.9 %all-gather.8.cloned.1.call-start = ((), (), s32[]{:S(2)}) async-start(), calls=%async_computation.7 | async-start | bytes 9437184 | tf_op jit(solution)/shard_map/all_gather | solution.py:177
  77.9 226.2 %all-gather.6.cloned.1.call-start = ((), (), s32[]{:S(2)}) async-start(), calls=%async_computation.6 | async-start | bytes 18874368 | tf_op jit(solution)/shard_map/all_gather | solution.py:178
  78.7 327.3 %reduce-scatter.2.cloned.1.call-start = ((), (), s32[]{:S(2)}) async-start(), calls=%async_computation.8 | async-start | bytes 5570560 | tf_op jit(solution)/shard_map/reduce_scatter | solution.py:242
  304.1 2.5 copy-start.2
  329.5 2.3 copy-start.1
  331.8 0.7 copy-start.4
  408.1 28.2 %all-to-all-start.3 = ((bf16[32,10,512]{2,1,0:T(8,128)(2,1)}), bf16[32,10,512]{2,1,0:T(8,128)(2,1)S(1)}, u32[]{:S(2)}, u32[]{:S(2)}) async-start(bf16[32,10,512]{2,1,0:T(8,128)(2,1)} %copy.35), calls=%async_computation.4 | async-start | bytes 1048576 | tf_op jit(solution)/shard_map/all_to_all | solution.py:244
Sparse Core Ops, SparseCore 0:
  77.3 69.1 all-gather.3
  148.6 60.3 all-gather.7
  211.2 92.8 all-gather.5
  332.0 73.9 reduce-scatter.1

commit v2 on v1

--- a/solution.py
+++ b/solution.py
@@ -90,59 +90,96 @@
     )(received)
 
 
-def expert_kernel(all_ref, take_ref, put_ref, in_ref, down_ref, out_ref, rows, active):
-    step = pl.program_id(0)
-
-    @pl.when(step == 0)
-    def _():
-        for n in range(8):
-            part = slice(n * 512, (n + 1) * 512)
-            rows[:, part] = jnp.dot(
-                take_ref[...], all_ref[:, part], preferred_element_type=jnp.float32
-            ).astype(jnp.bfloat16)
-
-    @pl.when(step < N_TP)
-    def _():
-        both = jnp.dot(rows[...], in_ref[0], preferred_element_type=jnp.float32)
+def expert_kernel(order_ref, all_ref, take_ref, put_ref, *refs):
+    in_refs, down_refs = refs[:10], refs[10:20]
+    out_ref, gathered, rows, in_buf, down_buf, active, whole, parts, sems = refs[20:]
+    copies = [[pltpu.make_async_copy(all_ref, gathered, sems.at[0])]]
+    count = 1
+    for pieces, buf in ((in_refs, in_buf), (down_refs, down_buf)):
+        for core in range(2):
+            for k in range(4):
+                chunk = buf.at[core * 4 + k]
+                found = []
+                if k < 3:
+                    found.append((pieces[core * 5 + k], chunk))
+                else:
+                    half = chunk.shape[0] // 2
+                    found.append((pieces[core * 5 + 3], chunk.at[pl.ds(0, half)]))
+                    found.append((pieces[core * 5 + 4], chunk.at[pl.ds(half, half)]))
+                group = []
+                for source, target in found:
+                    group.append(pltpu.make_async_copy(source, target, sems.at[count]))
+                    count += 1
+                copies.append(group)
+    for group in copies:
+        for copy in group:
+            copy.start()
+    copies[0][0].wait()
+    for n in range(8):
+        part = slice(n * 512, (n + 1) * 512)
+        rows[:, part] = jnp.dot(
+            take_ref[...], gathered[:, part], preferred_element_type=jnp.float32
+        ).astype(jnp.bfloat16)
+    for k in range(N_TP):
+        for copy in copies[1 + k]:
+            copy.wait()
+        both = jnp.dot(rows[...], in_buf[k], preferred_element_type=jnp.float32)
         gate = both[:, :128]
-        value = (gate / (1.0 + jnp.exp(-gate)) * both[:, 128:]).astype(jnp.bfloat16)
-        for t in range(N_TP):
-
-            @pl.when(step == t)
-            def _():
-                active[:, t * 128 : (t + 1) * 128] = value
-
-    @pl.when(step >= N_TP)
-    def _():
-        part = jnp.dot(active[...], down_ref[0], preferred_element_type=jnp.float32)
-        out_ref[...] = jnp.dot(
+        active[order_ref[k]] = (gate / (1.0 + jnp.exp(-gate)) * both[:, 128:]).astype(jnp.bfloat16)
+    for t in range(N_TP):
+        whole[:, t * 128 : (t + 1) * 128] = active[t]
+    outs = []
+    for k in range(N_TP):
+        for copy in copies[1 + N_TP + k]:
+            copy.wait()
+        part = jnp.dot(whole[...], down_buf[k], preferred_element_type=jnp.float32)
+        parts[k] = jnp.dot(
             put_ref[...], part.astype(jnp.bfloat16), preferred_element_type=jnp.float32
         ).astype(jnp.bfloat16)
-
-
-def run_experts(all_rows, take, put, weights_in, weights_down):
-    last = N_TP - 1
+        lanes = pl.ds(pl.multiple_of(order_ref[k] * 512, 512), 512)
+        copy = pltpu.make_async_copy(parts.at[k], out_ref.at[:, lanes], sems.at[count])
+        count += 1
+        copy.start()
+        outs.append(copy)
+    for copy in outs:
+        copy.wait()
+
+
+def run_experts(order, all_rows, take, put, weights_in, weights_down):
+    anywhere = pl.BlockSpec(memory_space=pl.ANY)
+    local = pl.BlockSpec(memory_space=pltpu.VMEM)
     return pl.pallas_call(
         expert_kernel,
         out_shape=jax.ShapeDtypeStruct((ALL_ROWS, D), jnp.bfloat16),
-        grid=(2 * N_TP,),
-        in_specs=[
-            pl.BlockSpec((ALL_ROWS, D), lambda j: (0, 0), pipeline_mode=pl.Buffered(1)),
-            pl.BlockSpec((OWN_ROWS, ALL_ROWS), lambda j: (0, 0), pipeline_mode=pl.Buffered(1)),
-            pl.BlockSpec((ALL_ROWS, OWN_ROWS), lambda j: (0, 0), pipeline_mode=pl.Buffered(1)),
-            pl.BlockSpec((1, D, 256), lambda j: (jnp.minimum(j, last), 0, 0)),
-            pl.BlockSpec((1, 1024, 512), lambda j: (jnp.maximum(j - N_TP, 0), 0, 0)),
+        in_specs=[pl.BlockSpec(memory_space=pltpu.SMEM), anywhere, local, local] + [anywhere] * 20,
+        out_specs=anywhere,
+        scratch_shapes=[
+            pltpu.VMEM((ALL_ROWS, D), jnp.bfloat16),
+            pltpu.VMEM((OWN_ROWS, D), jnp.bfloat16),
+            pltpu.VMEM((N_TP, D, 256), jnp.bfloat16),
+            pltpu.VMEM((N_TP, 1024, 512), jnp.bfloat16),
+            pltpu.VMEM((N_TP, OWN_ROWS, 128), jnp.bfloat16),
+            pltpu.VMEM((OWN_ROWS, 1024), jnp.bfloat16),
+            pltpu.VMEM((N_TP, ALL_ROWS, 512), jnp.bfloat16),
+            pltpu.SemaphoreType.DMA((29,)),
         ],
-        out_specs=pl.BlockSpec((ALL_ROWS, 512), lambda j: (0, jnp.maximum(j - N_TP, 0))),
-        scratch_shapes=[
-            pltpu.VMEM((OWN_ROWS, D), jnp.bfloat16),
-            pltpu.VMEM((OWN_ROWS, 1024), jnp.bfloat16),
-        ],
-        compiler_params=pltpu.CompilerParams(
-            dimension_semantics=("arbitrary",), vmem_limit_bytes=40 << 20
-        ),
+        compiler_params=pltpu.CompilerParams(vmem_limit_bytes=50 << 20),
         name="experts",
-    )(all_rows, take, put, weights_in, weights_down)
+    )(order, all_rows, take, put, *weights_in, *weights_down)
+
+
+def by_y(value, step):
+    return lax.ppermute(value, "y", [(i, (i + step) % NY) for i in range(NY)])
+
+
+def other_core(value):
+    return lax.ppermute(value, "c", [(0, 1), (1, 0)])
+
+
+def gather_rest(own, below, above):
+    half = own.shape[0] // 2
+    pieces = [own, below, above, by_y(below[:half], 1), by_y(above[half:], -1)]
+    return pieces + [other_core(piece) for piece in pieces]
 
 
 def three_parts(values):
@@ -174,11 +211,13 @@
     leave_slot = leaving[my_group]
     handing = [(i, (i + 1) % N_REP) for i in range(N_REP)]
 
-    weights_down = lax.all_gather(down_proj[0], TP)
-    weights_in = lax.all_gather(gate_up[0], TP)
-
-    query_heads = lax.all_to_all(queries, TP, split_axis=1, concat_axis=0, tiled=True)
-    kv_rows = lax.all_to_all(fresh_kv, TP, split_axis=1, concat_axis=0, tiled=True)
+    in_own, down_own = gate_up[0], down_proj[0]
+    mixed = jnp.concatenate(
+        [queries.reshape(-1, N_TP, 512), fresh_kv.reshape(-1, N_TP, 256)], axis=2
+    )
+    heads = lax.all_to_all(mixed, TP, split_axis=1, concat_axis=0, tiled=True)[:, 0]
+    query_heads, kv_rows = heads[:, :512], heads[:, 512:]
+    in_below, in_above = by_y(in_own, 1), by_y(in_own, -1)
     resid_slots = residual.reshape(REQ, FRESH, -1)
     resid_came = lax.ppermute(
         lax.dynamic_index_in_dim(resid_slots, leave_slot, 0, keepdims=False), REP, handing
@@ -230,7 +269,17 @@
     packed = jnp.dot(placing, payload, preferred_element_type=jnp.float32).astype(jnp.bfloat16)
     received = lax.all_to_all(packed.reshape(NX * N_TP, PIECE, WIDE), SPREAD, 0, 0)
     normed = norm_rows(received.reshape(NX * N_TP, PIECE, WIDE))
+    normed, in_own, in_below, in_above, down_own = lax.optimization_barrier(
+        (normed, in_own, in_below, in_above, down_own)
+    )
     all_rows = lax.all_gather(normed, "z", tiled=True)
+    weights_in = gather_rest(in_own, in_below, in_above)
+    weights_down = gather_rest(down_own, by_y(down_own, 1), by_y(down_own, -1))
+    my_y, my_core = lax.axis_index("y"), lax.axis_index("c")
+    piece = jnp.arange(N_TP, dtype=jnp.int32)
+    step = piece % 4
+    step = jnp.where(step == 1, NY - 1, jnp.where(step == 2, 1, jnp.where(step == 3, 2, 0)))
+    order = (my_y + step) % NY * NC + (my_core + piece // 4) % NC
 
     index = jnp.arange(ALL_ROWS, dtype=jnp.int32)
     own = (index // SHARE) % 2 == my_z // 8
@@ -238,7 +287,7 @@
     own_index = jnp.arange(OWN_ROWS, dtype=jnp.int32)
     take = (own_index[:, None] == compact[None, :]).astype(jnp.bfloat16)
     put = (compact[:, None] == own_index[None, :]).astype(jnp.bfloat16)
-    partial_rows = run_experts(all_rows, take, put, weights_in, weights_down)
+    partial_rows = run_experts(order, all_rows, take, put, weights_in, weights_down)
     summed = lax.psum_scatter(partial_rows, "z", scatter_dimension=0, tiled=True)
     back = summed.reshape(NX, PIECE, N_TP, 512).transpose(0, 2, 1, 3)
     returned = lax.all_to_all(back.reshape(NX * N_TP, PIECE, 512), SPREAD, 0, 0)

time: 445 us -> 337 us (0.76)
  waiting for transfers between devices: 324 us -> 156 us
  starting transfers between devices: 35.4 us -> 79.8 us
  local copies, waits for them, and re-layouts: 16.5 us -> 24.5 us
    all_gather x2 -> x0, waiting for transfers between devices: 158 us -> none  [the longest x1 95.1 us: per_device(): weights_in = lax.all_gather(gate_up[0], TP)]
    all_gather x1, waiting for transfers between devices: 67.5 us -> 0.02 us  [per_device(): all_rows = lax.all_gather(normed, 'z', tiled=True)]
    ppermute x0 -> x18, starting transfers between devices: none -> 47.8 us  [the longest x8 25.8 us: by_y(): return lax.ppermute(value, 'y', [(i, (i + step) % NY) for i in range(NY)])]
    ppermute x0 -> x18, waiting for transfers between devices: none -> 40.1 us  [the longest x8 37.8 us: by_y(): return lax.ppermute(value, 'y', [(i, (i + step) % NY) for i in range(NY)])]
    all_to_all x2 -> x1, waiting for transfers between devices: 4.8 us -> 25 us  [per_device(): lax.all_to_all(mixed, TP, split_axis=1, concat_axis=0, tiled=True)[:, 0]]
    all_to_all x2 -> x1, starting transfers between devices: 15 us -> 9.83 us  [per_device(): lax.all_to_all(mixed, TP, split_axis=1, concat_axis=0, tiled=True)[:, 0]]
    unnamed x14 -> x64, local copies, waits for them, and re-layouts: 7.1 us -> 11.3 us
  transfers between devices with their start and end apart: 9 -> 24, of which waited for: 7 -> 8; matrix products, arithmetic and copies ran while one was open for 3% -> 7% of each run, Pallas kernels for 0% -> 1%
where the time goes in v2:
time: 337 us; the launch traced here: 336 us
  waiting for transfers between devices  156 us (46%)
  starting transfers between devices  79.8 us (24%)
  Pallas kernels  28.4 us (8%)
  local copies, waits for them, and re-layouts  24.5 us (7%)
  blocking collectives  19.7 us (6%)
  between operations  15.7 us (5%)
  matrix products  7.88 us (2%)
  other arithmetic  3.72 us (1%)
    reduce_scatter x1, waiting for transfers between devices, per_device(): lax.psum_scatter(partial_rows, 'z', scatter_dimension=0, tiled=True)  69.1 us
    ppermute x8, waiting for transfers between devices, by_y(): return lax.ppermute(value, 'y', [(i, (i + step) % NY) for i in range(NY)])  37.8 us
    pallas_call x1, Pallas kernels, run_experts(): pl.pallas_call(expert_kernel, out_shape=jax.ShapeDtypeStruct((ALL_ROWS, D...  26.4 us
    ppermute x8, starting transfers between devices, by_y(): return lax.ppermute(value, 'y', [(i, (i + step) % NY) for i in range(NY)])  25.8 us
    all_to_all x1, waiting for transfers between devices, per_device(): lax.all_to_all(mixed, TP, split_axis=1, concat_axis=0, tiled=True)[:, 0]  25 us
    ppermute x10, starting transfers between devices, other_core(): return lax.ppermute(value, 'c', [(0, 1), (1, 0)])  22 us
    all_to_all x1, blocking collectives, per_device(): lax.all_to_all(packed.reshape(NX * N_TP, PIECE, WIDE), SPREAD, 0, 0)  19.7 us
    all_to_all x1, starting transfers between devices, per_device(): returned = lax.all_to_all(back.reshape(NX * N_TP, PIECE, 512), SPREAD, 0, 0)  16.6 us
  transfers between devices with their start and end apart: 24, of which 8 were waited for; matrix products, arithmetic and copies ran while one was open for 7% of the time, Pallas kernels for 1%

profile of v2, /device:TPU:1, one launch (start us, length us, event | category | flops | bytes accessed | tf_op | source)
XLA Modules:
  0.0 335.7 jit_solution(1770923550394272071)
XLA Ops:
  6.6 4.2 %collective-permute-start.2 = (bf16[4096,256]{1,0:T(8,128)(2,1)}, bf16[4096,256]{1,0:T(8,128)(2,1)S(1)}, u32[]{:S(2)}, u32[]{:S(2)}) collective-permute-start(bf16[4096,256]{1,0:T(8,128)(2,1)} %bitcast.24.refs_0_), channel_id=1, source_target_pairs={{0,2},{2,4},{4,6},{6,0},{1,3},{3,5},{5,7},{7,1},{8,10},{10,12},{12... | collective-permute-start | bytes 6291464 | tf_op jit(solution)/shard_map/ppermute | solution.py:172
  10.7 3.4 %collective-permute-start.3 = (bf16[4096,256]{1,0:T(8,128)(2,1)}, bf16[4096,256]{1,0:T(8,128)(2,1)}, u32[]{:S(2)}, u32[]{:S(2)}) collective-permute-start(bf16[4096,256]{1,0:T(8,128)(2,1)} %bitcast.24.refs_0_), channel_id=1, source_target_pairs={{0,6},{2,0},{4,2},{6,4},{1,7},{3,1},{5,3},{7,5},{8,14},{10,8},{12,... | collective-permute-start | bytes 6291464 | tf_op jit(solution)/shard_map/ppermute | solution.py:172
  16.6 9.8 %all-to-all-start = ((bf16[16,8,768]{2,0,1:T(8,128)(2,1)}), bf16[16,8,768]{2,0,1:T(8,128)(2,1)S(1)}, u32[]{:S(2)}, u32[]{:S(2)}) async-start(bf16[16,8,768]{2,0,1:T(8,128)(2,1)} %copy.33), calls=%async_computation | async-start | bytes 393216 | tf_op jit(solution)/shard_map/all_to_all | solution.py:218
  28.7 1.4 dynamic-slice_bitcast_fusion
  30.1 1.9 collective-permute-start
  34.5 1.6 gather_fusion
  36.8 25.0 %all-to-all-done = bf16[16,8,768]{2,0,1:T(8,128)(2,1)S(1)} async-done(((bf16[16,8,768]{2,0,1:T(8,128)(2,1)}), bf16[16,8,768]{2,0,1:T(8,128)(2,1)S(1)}, u32[]{:S(2)}, u32[]{:S(2)}) %all-to-all-start) | async-done | bytes 196640 | tf_op jit(solution)/shard_map/all_to_all | solution.py:218
  62.5 3.5 %fusion.87 = (f32[4,4,32]{2,1,0:T(4,128)}, f32[4,4,32,544]{3,2,1,0:T(8,128)}) fusion(pred[4,32,544]{2,1,0:T(8,128)(4,1)S(1)} %and_select_fusion, bf16[4,32,256]{2,1,0:T(8,128)(2,1)} %bitcast.115, bf16[4,512,256]{2,1,0:T(8,128)(2,1)} %bitcast.99, bf16[4,32,4,128]{3,2,1,0:T(4,128)(2,1)S(1)} %reshape_reshape.3), kind=kOutput, calls=%fused_computation.154 | convolution fusion | flops 73810464 | bytes 2430976 | tf_op jit(solution)/shard_map/sub | solution.py:60
  66.0 1.9 fusion.11
  68.0 3.5 %collective-permute-start.1 = (bf16[32,512]{1,0:T(8,128)(2,1)S(1)}, bf16[32,512]{1,0:T(8,128)(2,1)S(1)}, u32[]{:S(2)}, u32[]{:S(2)}) collective-permute-start(bf16[32,512]{1,0:T(8,128)(2,1)S(1)} %fusion.45), channel_id=1, source_target_pairs={{0,8},{8,16},{16,24},{24,32},{32,40},{40,48},{48,56},{56,64},{64,7... | collective-permute-start | bytes 98312 | tf_op jit(solution)/shard_map/ppermute | solution.py:236
  72.5 10.1 %collective-permute-done.1 = bf16[32,512]{1,0:T(8,128)(2,1)S(1)} collective-permute-done((bf16[32,512]{1,0:T(8,128)(2,1)S(1)}, bf16[32,512]{1,0:T(8,128)(2,1)S(1)}, u32[]{:S(2)}, u32[]{:S(2)}) %collective-permute-start.1) | collective-permute-done | bytes 32800 | tf_op jit(solution)/shard_map/ppermute | solution.py:236
  82.6 1.6 multiply_convert_fusion
  85.8 1.2 convolution_convert_fusion
  87.0 1.0 reshape.317
  88.0 19.7 %all_to_all.25.recv_ref = bf16[32,10,640]{2,1,0:T(8,128)(2,1)} all-to-all(bf16[32,10,640]{2,1,0:T(8,128)(2,1)} %reshape.317), channel_id=1, replica_groups=mesh['x'=4,'z'=16,'y'=4,'c'=2] {'x','y','c'}, dimensions={0} | all-to-all | bytes 819200 | tf_op jit(solution)/shard_map/all_to_all | solution.py:270
  107.7 2.0 norm_rows.1
  109.8 1.9 collective-permute-start.11
  111.8 4.6 %collective-permute-start.12 = (bf16[1024,512]{1,0:T(8,128)(2,1)}, bf16[1024,512]{1,0:T(8,128)(2,1)}, u32[]{:S(2)}, u32[]{:S(2)}) collective-permute-start(bf16[1024,512]{1,0:T(8,128)(2,1)} %bitcast.102), channel_id=1, source_target_pairs={{0,6},{2,0},{4,2},{6,4},{1,7},{3,1},{5,3},{7,5},{8,14},{10,8},{12,... | collective-permute-start | bytes 3145736 | tf_op jit(solution)/shard_map/ppermute | solution.py:172
  116.4 2.3 collective-permute-start.15
  118.7 1.3 slice.54
  120.0 2.0 collective-permute-start.5
  122.1 3.3 collective-permute-start.4
  125.3 12.8 %collective-permute-done.11.refs_11_ = bf16[1024,512]{1,0:T(8,128)(2,1)} collective-permute-done((bf16[1024,512]{1,0:T(8,128)(2,1)}, bf16[1024,512]{1,0:T(8,128)(2,1)}, u32[]{:S(2)}, u32[]{:S(2)}) %collective-permute-start.11) | collective-permute-done | bytes 1048608 | tf_op jit(solution)/shard_map/ppermute | solution.py:172
  138.2 1.1 slice.66
  139.2 1.9 collective-permute-start.13
  141.2 1.1 slice.67
  142.3 4.6 %collective-permute-start.14 = (bf16[512,512]{1,0:T(8,128)(2,1)S(1)}, bf16[512,512]{1,0:T(8,128)(2,1)S(1)}, u32[]{:S(2)}, u32[]{:S(2)}) collective-permute-start(bf16[512,512]{1,0:T(8,128)(2,1)S(1)} %slice.67), channel_id=1, source_target_pairs={{0,6},{2,0},{4,2},{6,4},{1,7},{3,1},{5,3},{7,5},{8,14},{10,8},{12,... | collective-permute-start | bytes 1572872 | tf_op jit(solution)/shard_map/ppermute | solution.py:172
  146.9 25.0 %collective-permute-done.13.refs_13_ = bf16[512,512]{1,0:T(8,128)(2,1)S(1)} collective-permute-done((bf16[512,512]{1,0:T(8,128)(2,1)S(1)}, bf16[512,512]{1,0:T(8,128)(2,1)S(1)}, u32[]{:S(2)}, u32[]{:S(2)}) %collective-permute-start.13) | collective-permute-done | bytes 524320 | tf_op jit(solution)/shard_map/ppermute | solution.py:172
  171.9 2.5 collective-permute-start.18
  174.4 1.9 collective-permute-start.19
  177.1 2.4 collective-permute-start.7
  179.5 1.9 collective-permute-start.10
  181.5 2.4 collective-permute-start.9
  184.7 1.9 collective-permute-start.6
  187.4 2.4 collective-permute-start.8
  189.9 1.9 collective-permute-start.16
  191.8 1.0 copy-done.15
  192.8 2.4 collective-permute-start.17
  195.6 2.2 collective-permute-done.17.refs_17_
  197.9 1.0 copy-done.2
  198.9 1.0 copy-done.4
  199.9 1.0 copy-done.6
  201.0 26.4 %experts.1 = bf16[640,4096]{1,0:T(8,128)(2,1)} custom-call(s32[8]{0:T(128)S(1)} %fusion.69.order_ref, bf16[640,4096]{1,0:T(8,128)(2,1)} %all-gather.2.cloned.1.call-done.all_ref, bf16[320,640]{1,0:T(8,128)(2,1)S(1)} %fusion.10.take_ref, bf16[640,320]{1,0:T(8,128)(2,1)S(1)} %fusion.9.put_ref, bf16[4096,256]{1,0:T(8,128)(2,1)} %bitcast.24.refs_0_, ...), custom_call_target="tpu_custom_call" | custom-call | tf_op jit(solution)/shard_map/experts/pallas_call | solution.py:151
  228.1 69.1 %reduce-scatter.2.cloned.1.call-done = bf16[40,4096]{1,0:T(8,128)(2,1)} async-done(((bf16[640,4096]{1,0:T(8,128)(2,1)}), bf16[40,4096]{1,0:T(8,128)(2,1)}) %reduce-scatter.2.cloned.1.call-update) | async-done | bytes 327696 | tf_op jit(solution)/shard_map/reduce_scatter | solution.py:291
  297.2 1.1 copy.46
  298.3 1.0 copy.39
  299.3 16.6 %all-to-all-start.2 = ((bf16[32,10,512]{2,1,0:T(8,128)(2,1)}), bf16[32,10,512]{2,1,0:T(8,128)(2,1)S(1)}, u32[]{:S(2)}, u32[]{:S(2)}) async-start(bf16[32,10,512]{2,1,0:T(8,128)(2,1)} %copy.39), calls=%async_computation.3 | async-start | bytes 1048576 | tf_op jit(solution)/shard_map/all_to_all | solution.py:293
  315.9 11.6 %all-to-all-done.2 = bf16[32,10,512]{2,1,0:T(8,128)(2,1)S(1)} async-done(((bf16[32,10,512]{2,1,0:T(8,128)(2,1)}), bf16[32,10,512]{2,1,0:T(8,128)(2,1)S(1)}, u32[]{:S(2)}, u32[]{:S(2)}) %all-to-all-start.2) | async-done | bytes 327712 | tf_op jit(solution)/shard_map/all_to_all | solution.py:293
  (130 shorter events, 14.6 us)
Async XLA Ops:
  6.5 28.0 %copy-start = (bf16[128,16,256]{2,1,0:T(8,128)(2,1)S(1)}, bf16[128,16,256]{2,1,0:T(8,128)(2,1)}, u32[]{:S(2)}) copy-start(bf16[128,16,256]{2,1,0:T(8,128)(2,1)} %param.15) | copy-start | bytes 3145732
  6.5 19.9 %copy-start.26 = (s32[64]{0:T(128)S(1)}, s32[64]{0:T(128)}, u32[]{:S(2)}) copy-start(s32[64]{0:T(128)} %param.23) | copy-start | bytes 772
  6.5 25.5 %copy-start.24 = (s32[256]{0:T(256)S(1)}, s32[256]{0:T(256)}, u32[]{:S(2)}) copy-start(s32[256]{0:T(256)} %param.21) | copy-start | bytes 3076
  6.5 25.5 %copy-start.25 = (s32[256]{0:T(256)S(1)}, s32[256]{0:T(256)}, u32[]{:S(2)}) copy-start(s32[256]{0:T(256)} %param.20) | copy-start | bytes 3076
  6.5 26.3 %copy-start.27 = (s32[1,128]{1,0:T(1,128)S(1)}, s32[1,128]{1,0:T(1,128)}, u32[]{:S(2)}) copy-start(s32[1,128]{1,0:T(1,128)} %param.22) | copy-start | bytes 1540
  6.5 27.8 %copy-start.18 = (s32[128,2]{0,1:T(2,128)S(1)}, s32[128,2]{0,1:T(2,128)}, u32[]{:S(2)}) copy-start(s32[128,2]{0,1:T(2,128)} %param.24) | copy-start | bytes 3076
  6.6 103.2 %collective-permute-start.2 = (bf16[4096,256]{1,0:T(8,128)(2,1)}, bf16[4096,256]{1,0:T(8,128)(2,1)S(1)}, u32[]{:S(2)}, u32[]{:S(2)}) collective-permute-start(bf16[4096,256]{1,0:T(8,128)(2,1)} %bitcast.24.refs_0_), channel_id=1, source_target_pairs={{0,2},{2,4},{4,6},{6,0},{1,3},{3,5},{5,7},{7,1},{8,10},{10,12},{12... | collective-permute-start | bytes 6291464 | tf_op jit(solution)/shard_map/ppermute | solution.py:172
  10.7 99.0 %collective-permute-start.3 = (bf16[4096,256]{1,0:T(8,128)(2,1)}, bf16[4096,256]{1,0:T(8,128)(2,1)}, u32[]{:S(2)}, u32[]{:S(2)}) collective-permute-start(bf16[4096,256]{1,0:T(8,128)(2,1)} %bitcast.24.refs_0_), channel_id=1, source_target_pairs={{0,6},{2,0},{4,2},{6,4},{1,7},{3,1},{5,3},{7,5},{8,14},{10,8},{12,... | collective-permute-start | bytes 6291464 | tf_op jit(solution)/shard_map/ppermute | solution.py:172
  16.6 45.2 %all-to-all-start = ((bf16[16,8,768]{2,0,1:T(8,128)(2,1)}), bf16[16,8,768]{2,0,1:T(8,128)(2,1)S(1)}, u32[]{:S(2)}, u32[]{:S(2)}) async-start(bf16[16,8,768]{2,0,1:T(8,128)(2,1)} %copy.33), calls=%async_computation | async-start | bytes 393216 | tf_op jit(solution)/shard_map/all_to_all | solution.py:218
  26.5 171.4 %all-gather.2.cloned.1.call-start = ((), (), s32[]{:S(2)}) async-start(), calls=%async_computation.4 | async-start | bytes 5570560 | tf_op jit(solution)/shard_map/all_gather | solution.py:275
  30.1 42.5 %collective-permute-start = (bf16[32,512]{1,0:T(8,128)(2,1)}, bf16[32,512]{1,0:T(8,128)(2,1)}, u32[]{:S(2)}, u32[]{:S(2)}) collective-permute-start(bf16[32,512]{1,0:T(8,128)(2,1)} %dynamic-slice_bitcast_fusion), channel_id=1, source_target_pairs={{0,8},{8,16},{16,24},{24,32},{32,40},{40,48},{48,56},{56,64},{64,7... | collective-permute-start | bytes 98312 | tf_op jit(solution)/shard_map/ppermute | solution.py:222
  32.3 29.6 %copy-start.28 = (pred[4,32]{1,0:T(4,128)(4,1)}, pred[4,32]{1,0:T(4,128)(4,1)S(1)}, u32[]{:S(2)}) copy-start(pred[4,32]{1,0:T(4,128)(4,1)S(1)} %iota_compare_fusion.16) | copy-start | bytes 388
  62.5 3.5 %copy-start.17 = (bf16[128,256]{1,0:T(8,128)(2,1)S(1)}, bf16[128,256]{1,0:T(8,128)(2,1)}, u32[]{:S(2)}) copy-start(bf16[128,256]{1,0:T(8,128)(2,1)} %slice.60) | copy-start | bytes 196612
  66.0 2.0 copy-start.23
  66.0 6.1 %copy-start.29 = (pred[4,32]{1,0:T(4,128)(4,1)S(1)}, pred[4,32]{1,0:T(4,128)(4,1)}, u32[]{:S(2)}) copy-start(pred[4,32]{1,0:T(4,128)(4,1)} %copy-done.28) | copy-start | bytes 388
  66.0 16.6 %copy-start.16 = (bf16[128,512]{1,0:T(8,128)(2,1)S(1)}, bf16[128,512]{1,0:T(8,128)(2,1)}, u32[]{:S(2)}) copy-start(bf16[128,512]{1,0:T(8,128)(2,1)} %param.16) | copy-start | bytes 393220
  66.0 16.6 %copy-start.20 = (f32[512]{0:T(512)S(1)}, f32[512]{0:T(512)}, u32[]{:S(2)}) copy-start(f32[512]{0:T(512)} %param.17) | copy-start | bytes 6148
  68.0 14.6 %collective-permute-start.1 = (bf16[32,512]{1,0:T(8,128)(2,1)S(1)}, bf16[32,512]{1,0:T(8,128)(2,1)S(1)}, u32[]{:S(2)}, u32[]{:S(2)}) collective-permute-start(bf16[32,512]{1,0:T(8,128)(2,1)S(1)} %fusion.45), channel_id=1, source_target_pairs={{0,8},{8,16},{16,24},{24,32},{32,40},{40,48},{48,56},{56,64},{64,7... | collective-permute-start | bytes 98312 | tf_op jit(solution)/shard_map/ppermute | solution.py:236
  109.8 12.2 %copy-start.7 = (bf16[4096,256]{1,0:T(8,128)(2,1)}, bf16[4096,256]{1,0:T(8,128)(2,1)S(1)}, u32[]{:S(2)}) copy-start(bf16[4096,256]{1,0:T(8,128)(2,1)S(1)} %collective-permute-done.2.refs_1_) | copy-start | bytes 6291460
  109.8 187.4 %reduce-scatter.2.cloned.1.call-start = ((), (), s32[]{:S(2)}) async-start(), calls=%async_computation.5 | async-start | bytes 5570560 | tf_op jit(solution)/shard_map/reduce_scatter | solution.py:291
  109.8 28.3 %collective-permute-start.11 = (bf16[1024,512]{1,0:T(8,128)(2,1)}, bf16[1024,512]{1,0:T(8,128)(2,1)}, u32[]{:S(2)}, u32[]{:S(2)}) collective-permute-start(bf16[1024,512]{1,0:T(8,128)(2,1)} %bitcast.101), channel_id=1, source_target_pairs={{0,2},{2,4},{4,6},{6,0},{1,3},{3,5},{5,7},{7,1},{8,10},{10,12},{12... | collective-permute-start | bytes 3145736 | tf_op jit(solution)/shard_map/ppermute | solution.py:172
  111.8 29.4 %collective-permute-start.12 = (bf16[1024,512]{1,0:T(8,128)(2,1)}, bf16[1024,512]{1,0:T(8,128)(2,1)}, u32[]{:S(2)}, u32[]{:S(2)}) collective-permute-start(bf16[1024,512]{1,0:T(8,128)(2,1)} %bitcast.102), channel_id=1, source_target_pairs={{0,6},{2,0},{4,2},{6,4},{1,7},{3,1},{5,3},{7,5},{8,14},{10,8},{12,... | collective-permute-start | bytes 3145736 | tf_op jit(solution)/shard_map/ppermute | solution.py:172
  116.4 65.0 %collective-permute-start.15 = (bf16[1024,512]{1,0:T(8,128)(2,1)}, bf16[1024,512]{1,0:T(8,128)(2,1)S(1)}, u32[]{:S(2)}, u32[]{:S(2)}) collective-permute-start(bf16[1024,512]{1,0:T(8,128)(2,1)} %bitcast.103), channel_id=1, source_target_pairs={{0,1},{1,0},{2,3},{3,2},{4,5},{5,4},{6,7},{7,6},{8,9},{9,8},{10,11... | collective-permute-start | bytes 3145736 | tf_op jit(solution)/shard_map/ppermute | solution.py:176
  120.0 57.1 %collective-permute-start.5 = (bf16[2048,256]{1,0:T(8,128)(2,1)S(1)}, bf16[2048,256]{1,0:T(8,128)(2,1)S(1)}, u32[]{:S(2)}, u32[]{:S(2)}) collective-permute-start(bf16[2048,256]{1,0:T(8,128)(2,1)S(1)} %slice.54), channel_id=1, source_target_pairs={{0,6},{2,0},{4,2},{6,4},{1,7},{3,1},{5,3},{7,5},{8,14},{10,8},{12,... | collective-permute-start | bytes 3145736 | tf_op jit(solution)/shard_map/ppermute | solution.py:172
  122.1 57.4 %collective-permute-start.4 = (bf16[2048,256]{1,0:T(8,128)(2,1)S(1)}, bf16[2048,256]{1,0:T(8,128)(2,1)S(1)}, u32[]{:S(2)}, u32[]{:S(2)}) collective-permute-start(bf16[2048,256]{1,0:T(8,128)(2,1)S(1)} %slice.53), channel_id=1, source_target_pairs={{0,2},{2,4},{4,6},{6,0},{1,3},{3,5},{5,7},{7,1},{8,10},{10,12},{12... | collective-permute-start | bytes 3145736 | tf_op jit(solution)/shard_map/ppermute | solution.py:172
  139.2 32.6 %collective-permute-start.13 = (bf16[512,512]{1,0:T(8,128)(2,1)S(1)}, bf16[512,512]{1,0:T(8,128)(2,1)S(1)}, u32[]{:S(2)}, u32[]{:S(2)}) collective-permute-start(bf16[512,512]{1,0:T(8,128)(2,1)S(1)} %slice.66), channel_id=1, source_target_pairs={{0,2},{2,4},{4,6},{6,0},{1,3},{3,5},{5,7},{7,1},{8,10},{10,12},{12... | collective-permute-start | bytes 1572872 | tf_op jit(solution)/shard_map/ppermute | solution.py:172
  142.3 32.1 %collective-permute-start.14 = (bf16[512,512]{1,0:T(8,128)(2,1)S(1)}, bf16[512,512]{1,0:T(8,128)(2,1)S(1)}, u32[]{:S(2)}, u32[]{:S(2)}) collective-permute-start(bf16[512,512]{1,0:T(8,128)(2,1)S(1)} %slice.67), channel_id=1, source_target_pairs={{0,6},{2,0},{4,2},{6,4},{1,7},{3,1},{5,3},{7,5},{8,14},{10,8},{12,... | collective-permute-start | bytes 1572872 | tf_op jit(solution)/shard_map/ppermute | solution.py:172
  171.9 12.0 %collective-permute-start.18 = (bf16[512,512]{1,0:T(8,128)(2,1)S(1)}, bf16[512,512]{1,0:T(8,128)(2,1)S(1)}, u32[]{:S(2)}, u32[]{:S(2)}) collective-permute-start(bf16[512,512]{1,0:T(8,128)(2,1)S(1)} %collective-permute-done.13.refs_13_), channel_id=1, source_target_pairs={{0,1},{1,0},{2,3},{3,2},{4,5},{5,4},{6,7},{7,6},{8,9},{9,8},{10,11... | collective-permute-start | bytes 1572872 | tf_op jit(solution)/shard_map/ppermute | solution.py:176
  174.4 12.3 %collective-permute-start.19 = (bf16[512,512]{1,0:T(8,128)(2,1)S(1)}, bf16[512,512]{1,0:T(8,128)(2,1)S(1)}, u32[]{:S(2)}, u32[]{:S(2)}) collective-permute-start(bf16[512,512]{1,0:T(8,128)(2,1)S(1)} %collective-permute-done.14.refs_14_), channel_id=1, source_target_pairs={{0,1},{1,0},{2,3},{3,2},{4,5},{5,4},{6,7},{7,6},{8,9},{9,8},{10,11... | collective-permute-start | bytes 1572872 | tf_op jit(solution)/shard_map/ppermute | solution.py:176
  177.1 14.7 %copy-start.13 = (bf16[2048,256]{1,0:T(8,128)(2,1)}, bf16[2048,256]{1,0:T(8,128)(2,1)S(1)}, u32[]{:S(2)}) copy-start(bf16[2048,256]{1,0:T(8,128)(2,1)S(1)} %collective-permute-done.5.refs_4_) | copy-start | bytes 3145732
  177.1 20.7 %collective-permute-start.7 = (bf16[4096,256]{1,0:T(8,128)(2,1)}, bf16[4096,256]{1,0:T(8,128)(2,1)}, u32[]{:S(2)}, u32[]{:S(2)}) collective-permute-start(bf16[4096,256]{1,0:T(8,128)(2,1)} %copy-done.7), channel_id=1, source_target_pairs={{0,1},{1,0},{2,3},{3,2},{4,5},{5,4},{6,7},{7,6},{8,9},{9,8},{10,11... | collective-permute-start | bytes 6291464 | tf_op jit(solution)/shard_map/ppermute | solution.py:176
  179.5 10.3 %collective-permute-start.10 = (bf16[2048,256]{1,0:T(8,128)(2,1)S(1)}, bf16[2048,256]{1,0:T(8,128)(2,1)S(1)}, u32[]{:S(2)}, u32[]{:S(2)}) collective-permute-start(bf16[2048,256]{1,0:T(8,128)(2,1)S(1)} %collective-permute-done.5.refs_4_), channel_id=1, source_target_pairs={{0,1},{1,0},{2,3},{3,2},{4,5},{5,4},{6,7},{7,6},{8,9},{9,8},{10,11... | collective-permute-start | bytes 3145736 | tf_op jit(solution)/shard_map/ppermute | solution.py:176
  181.4 10.4 %copy-start.12 = (bf16[1024,512]{1,0:T(8,128)(2,1)}, bf16[1024,512]{1,0:T(8,128)(2,1)S(1)}, u32[]{:S(2)}) copy-start(bf16[1024,512]{1,0:T(8,128)(2,1)S(1)} %collective-permute-done.15.refs_15_) | copy-start | bytes 3145732
  181.5 10.3 %collective-permute-start.9 = (bf16[2048,256]{1,0:T(8,128)(2,1)S(1)}, bf16[2048,256]{1,0:T(8,128)(2,1)S(1)}, u32[]{:S(2)}, u32[]{:S(2)}) collective-permute-start(bf16[2048,256]{1,0:T(8,128)(2,1)S(1)} %collective-permute-done.4.refs_3_), channel_id=1, source_target_pairs={{0,1},{1,0},{2,3},{3,2},{4,5},{5,4},{6,7},{7,6},{8,9},{9,8},{10,11... | collective-permute-start | bytes 3145736 | tf_op jit(solution)/shard_map/ppermute | solution.py:176
  184.7 13.1 %collective-permute-start.6 = (bf16[4096,256]{1,0:T(8,128)(2,1)}, bf16[4096,256]{1,0:T(8,128)(2,1)}, u32[]{:S(2)}, u32[]{:S(2)}) collective-permute-start(bf16[4096,256]{1,0:T(8,128)(2,1)} %bitcast.24.refs_0_), channel_id=1, source_target_pairs={{0,1},{1,0},{2,3},{3,2},{4,5},{5,4},{6,7},{7,6},{8,9},{9,8},{10,11... | collective-permute-start | bytes 6291464 | tf_op jit(solution)/shard_map/ppermute | solution.py:176
  187.4 10.4 %collective-permute-start.8 = (bf16[4096,256]{1,0:T(8,128)(2,1)}, bf16[4096,256]{1,0:T(8,128)(2,1)}, u32[]{:S(2)}, u32[]{:S(2)}) collective-permute-start(bf16[4096,256]{1,0:T(8,128)(2,1)} %collective-permute-done.3.refs_2_), channel_id=1, source_target_pairs={{0,1},{1,0},{2,3},{3,2},{4,5},{5,4},{6,7},{7,6},{8,9},{9,8},{10,11... | collective-permute-start | bytes 6291464 | tf_op jit(solution)/shard_map/ppermute | solution.py:176
  189.8 2.0 copy-start.14
  189.9 5.7 %collective-permute-start.16 = (bf16[1024,512]{1,0:T(8,128)(2,1)}, bf16[1024,512]{1,0:T(8,128)(2,1)}, u32[]{:S(2)}, u32[]{:S(2)}) collective-permute-start(bf16[1024,512]{1,0:T(8,128)(2,1)} %collective-permute-done.11.refs_11_), channel_id=1, source_target_pairs={{0,1},{1,0},{2,3},{3,2},{4,5},{5,4},{6,7},{7,6},{8,9},{9,8},{10,11... | collective-permute-start | bytes 3145736 | tf_op jit(solution)/shard_map/ppermute | solution.py:176
  191.8 1.0 copy-start.15
  192.8 5.0 %collective-permute-start.17 = (bf16[1024,512]{1,0:T(8,128)(2,1)}, bf16[1024,512]{1,0:T(8,128)(2,1)}, u32[]{:S(2)}, u32[]{:S(2)}) collective-permute-start(bf16[1024,512]{1,0:T(8,128)(2,1)} %collective-permute-done.12.refs_12_), channel_id=1, source_target_pairs={{0,1},{1,0},{2,3},{3,2},{4,5},{5,4},{6,7},{7,6},{8,9},{9,8},{10,11... | collective-permute-start | bytes 3145736 | tf_op jit(solution)/shard_map/ppermute | solution.py:176
  197.8 1.0 copy-start.2
  198.9 1.0 copy-start.4
  199.9 1.0 copy-start.6
  298.3 29.3 %copy-start.22 = (s32[128]{0:T(128)S(1)}, s32[128]{0:T(128)}, u32[]{:S(2)}) copy-start(s32[128]{0:T(128)} %get-tuple-element.20) | copy-start | bytes 1540
  299.3 28.6 %copy-start.9 = (bf16[128,512]{1,0:T(8,128)(2,1)S(1)}, bf16[128,512]{1,0:T(8,128)(2,1)}, u32[]{:S(2)}) copy-start(bf16[128,512]{1,0:T(8,128)(2,1)} %copy-done.8) | copy-start | bytes 393220
  299.3 28.6 %copy-start.11 = (bf16[128,512]{1,0:T(8,128)(2,1)S(1)}, bf16[128,512]{1,0:T(8,128)(2,1)}, u32[]{:S(2)}) copy-start(bf16[128,512]{1,0:T(8,128)(2,1)} %copy-done.10) | copy-start | bytes 393220
  299.3 28.7 %copy-start.21 = (s32[128]{0:T(128)S(1)}, s32[128]{0:T(128)}, u32[]{:S(2)}) copy-start(s32[128]{0:T(128)} %get-tuple-element.21) | copy-start | bytes 1540
  299.3 28.2 %all-to-all-start.2 = ((bf16[32,10,512]{2,1,0:T(8,128)(2,1)}), bf16[32,10,512]{2,1,0:T(8,128)(2,1)S(1)}, u32[]{:S(2)}, u32[]{:S(2)}) async-start(bf16[32,10,512]{2,1,0:T(8,128)(2,1)} %copy.39), calls=%async_computation.3 | async-start | bytes 1048576 | tf_op jit(solution)/shard_map/all_to_all | solution.py:293
  (6 other events, 4.5 us)
Sparse Core Ops, SparseCore 0:
  109.9 68.6 all-gather.1
  227.5 69.6 reduce-scatter.1

commit v3 on v2

--- a/solution.py
+++ b/solution.py
@@ -90,38 +90,45 @@
     )(received)
 
 
+CHUNKS = 4
+
+
 def expert_kernel(order_ref, all_ref, take_ref, put_ref, *refs):
-    in_refs, down_refs = refs[:10], refs[10:20]
-    out_ref, gathered, rows, in_buf, down_buf, active, whole, parts, sems = refs[20:]
-    copies = [[pltpu.make_async_copy(all_ref, gathered, sems.at[0])]]
-    count = 1
-    for pieces, buf in ((in_refs, in_buf), (down_refs, down_buf)):
-        for core in range(2):
-            for k in range(4):
-                chunk = buf.at[core * 4 + k]
-                found = []
-                if k < 3:
-                    found.append((pieces[core * 5 + k], chunk))
-                else:
-                    half = chunk.shape[0] // 2
-                    found.append((pieces[core * 5 + 3], chunk.at[pl.ds(0, half)]))
-                    found.append((pieces[core * 5 + 4], chunk.at[pl.ds(half, half)]))
-                group = []
-                for source, target in found:
-                    group.append(pltpu.make_async_copy(source, target, sems.at[count]))
-                    count += 1
-                copies.append(group)
-    for group in copies:
-        for copy in group:
-            copy.start()
-    copies[0][0].wait()
-    for n in range(8):
-        part = slice(n * 512, (n + 1) * 512)
-        rows[:, part] = jnp.dot(
-            take_ref[...], gathered[:, part], preferred_element_type=jnp.float32
+    in_refs, down_hbm = refs[:14], refs[14]
+    out_ref, gathered, rows, in_buf, down_buf, active, whole, sems = refs[15:]
+    width = D // CHUNKS
+    half = D // 2
+    count = iter(range(30))
+
+    def begin(source, target):
+        copy = pltpu.make_async_copy(source, target, sems.at[next(count)])
+        copy.start()
+        return copy
+
+    parts = [
+        begin(all_ref.at[:, pl.ds(n * width, width)], gathered.at[n]) for n in range(CHUNKS)
+    ]
+    loads = []
+    for core in range(NC):
+        for k in range(NY):
+            chunk, first = in_buf.at[core * NY + k], core * 7 + 2 * k
+            if k == 0:
+                loads.append([begin(in_refs[first], chunk)])
+            else:
+                loads.append(
+                    [
+                        begin(in_refs[first - 1], chunk.at[pl.ds(0, half)]),
+                        begin(in_refs[first], chunk.at[pl.ds(half, half)]),
+                    ]
+                )
+    downs = [begin(down_hbm.at[t], down_buf.at[t]) for t in range(N_TP)]
+    for n in range(CHUNKS):
+        parts[n].wait()
+        rows[:, n * width : (n + 1) * width] = jnp.dot(
+            take_ref[...], gathered[n], preferred_element_type=jnp.float32
         ).astype(jnp.bfloat16)
     for k in range(N_TP):
-        for copy in copies[1 + k]:
+        for copy in loads[k]:
             copy.wait()
         both = jnp.dot(rows[...], in_buf[k], preferred_element_type=jnp.float32)
         gate = both[:, :128]
@@ -129,43 +136,39 @@
     for t in range(N_TP):
         whole[:, t * 128 : (t + 1) * 128] = active[t]
     outs = []
-    for k in range(N_TP):
-        for copy in copies[1 + N_TP + k]:
-            copy.wait()
-        part = jnp.dot(whole[...], down_buf[k], preferred_element_type=jnp.float32)
-        parts[k] = jnp.dot(
+    for t in range(N_TP):
+        downs[t].wait()
+        part = jnp.dot(whole[...], down_buf[t], preferred_element_type=jnp.float32)
+        n, lane = t // 2, t % 2 * 512
+        gathered[n, :, lane : lane + 512] = jnp.dot(
             put_ref[...], part.astype(jnp.bfloat16), preferred_element_type=jnp.float32
         ).astype(jnp.bfloat16)
-        lanes = pl.ds(pl.multiple_of(order_ref[k] * 512, 512), 512)
-        copy = pltpu.make_async_copy(parts.at[k], out_ref.at[:, lanes], sems.at[count])
-        count += 1
-        copy.start()
-        outs.append(copy)
+        if t % 2:
+            outs.append(begin(gathered.at[n], out_ref.at[:, pl.ds(n * width, width)]))
     for copy in outs:
         copy.wait()
 
 
 def run_experts(order, all_rows, take, put, weights_in, weights_down):
-    anywhere = pl.BlockSpec(memory_space=pl.ANY)
+    far = pl.BlockSpec(memory_space=pltpu.HBM)
     local = pl.BlockSpec(memory_space=pltpu.VMEM)
     return pl.pallas_call(
         expert_kernel,
         out_shape=jax.ShapeDtypeStruct((ALL_ROWS, D), jnp.bfloat16),
-        in_specs=[pl.BlockSpec(memory_space=pltpu.SMEM), anywhere, local, local] + [anywhere] * 20,
-        out_specs=anywhere,
+        in_specs=[pl.BlockSpec(memory_space=pltpu.SMEM), far, local, local] + [far] * 15,
+        out_specs=far,
         scratch_shapes=[
-            pltpu.VMEM((ALL_ROWS, D), jnp.bfloat16),
+            pltpu.VMEM((CHUNKS, ALL_ROWS, D // CHUNKS), jnp.bfloat16),
             pltpu.VMEM((OWN_ROWS, D), jnp.bfloat16),
             pltpu.VMEM((N_TP, D, 256), jnp.bfloat16),
             pltpu.VMEM((N_TP, 1024, 512), jnp.bfloat16),
             pltpu.VMEM((N_TP, OWN_ROWS, 128), jnp.bfloat16),
             pltpu.VMEM((OWN_ROWS, 1024), jnp.bfloat16),
-            pltpu.VMEM((N_TP, ALL_ROWS, 512), jnp.bfloat16),
-            pltpu.SemaphoreType.DMA((29,)),
+            pltpu.SemaphoreType.DMA((30,)),
         ],
-        compiler_params=pltpu.CompilerParams(vmem_limit_bytes=50 << 20),
+        compiler_params=pltpu.CompilerParams(vmem_limit_bytes=46 << 20),
         name="experts",
-    )(order, all_rows, take, put, *weights_in, *weights_down)
+    )(order, all_rows, take, put, *weights_in, weights_down)
 
 
 def by_y(value, step):
@@ -176,9 +179,13 @@
     return lax.ppermute(value, "c", [(0, 1), (1, 0)])
 
 
-def gather_rest(own, below, above):
+def gather_pieces(own):
     half = own.shape[0] // 2
-    pieces = [own, below, above, by_y(below[:half], 1), by_y(above[half:], -1)]
+    top, bottom = own[:half], own[half:]
+    below_top, above_bottom = by_y(top, 1), by_y(bottom, -1)
+    below_bottom, above_top = by_y(bottom, 1), by_y(top, -1)
+    far_top, far_bottom = by_y(below_top, 1), by_y(above_bottom, -1)
+    pieces = [own, below_top, below_bottom, above_top, above_bottom, far_top, far_bottom]
     return pieces + [other_core(piece) for piece in pieces]
 
 
@@ -211,13 +218,13 @@
     leave_slot = leaving[my_group]
     handing = [(i, (i + 1) % N_REP) for i in range(N_REP)]
 
-    in_own, down_own = gate_up[0], down_proj[0]
+    in_own = gate_up[0]
+    weights_down = lax.all_gather(down_proj[0], TP)
     mixed = jnp.concatenate(
         [queries.reshape(-1, N_TP, 512), fresh_kv.reshape(-1, N_TP, 256)], axis=2
     )
     heads = lax.all_to_all(mixed, TP, split_axis=1, concat_axis=0, tiled=True)[:, 0]
     query_heads, kv_rows = heads[:, :512], heads[:, 512:]
-    in_below, in_above = by_y(in_own, 1), by_y(in_own, -1)
     resid_slots = residual.reshape(REQ, FRESH, -1)
     resid_came = lax.ppermute(
         lax.dynamic_index_in_dim(resid_slots, leave_slot, 0, keepdims=False), REP, handing
@@ -269,12 +276,9 @@
     packed = jnp.dot(placing, payload, preferred_element_type=jnp.float32).astype(jnp.bfloat16)
     received = lax.all_to_all(packed.reshape(NX * N_TP, PIECE, WIDE), SPREAD, 0, 0)
     normed = norm_rows(received.reshape(NX * N_TP, PIECE, WIDE))
-    normed, in_own, in_below, in_above, down_own = lax.optimization_barrier(
-        (normed, in_own, in_below, in_above, down_own)
-    )
+    normed, in_own, weights_down = lax.optimization_barrier((normed, in_own, weights_down))
     all_rows = lax.all_gather(normed, "z", tiled=True)
-    weights_in = gather_rest(in_own, in_below, in_above)
-    weights_down = gather_rest(down_own, by_y(down_own, 1), by_y(down_own, -1))
+    weights_in = gather_pieces(in_own)
     my_y, my_core = lax.axis_index("y"), lax.axis_index("c")
     piece = jnp.arange(N_TP, dtype=jnp.int32)
     step = piece % 4

time: 337 us -> 308 us (0.914)
  starting transfers between devices: 79.8 us -> 67.5 us
  local copies, waits for them, and re-layouts: 24.5 us -> 12.3 us
    all_to_all x1, waiting for transfers between devices: 25 us -> 0.01 us  [per_device(): lax.all_to_all(mixed, TP, split_axis=1, concat_axis=0, tiled=True)[:, 0]]
    all_gather x0 -> x1, waiting for transfers between devices: none -> 17.3 us  [per_device(): weights_down = lax.all_gather(down_proj[0], TP)]
    ppermute x8 -> x6, waiting for transfers between devices: 37.8 us -> 44.2 us  [by_y(): return lax.ppermute(value, 'y', [(i, (i + step) % NY) for i in range(NY)])]
    ppermute x8 -> x6, starting transfers between devices: 25.8 us -> 19.5 us  [by_y(): return lax.ppermute(value, 'y', [(i, (i + step) % NY) for i in range(NY)])]
    unnamed x64 -> x32, local copies, waits for them, and re-layouts: 11.3 us -> 6.42 us
    reduce_scatter x1, waiting for transfers between devices: 69.1 us -> 73.9 us  [per_device(): lax.psum_scatter(partial_rows, 'z', scatter_dimension=0, tiled=True)]
    ppermute x10 -> x7, starting transfers between devices: 22 us -> 17.3 us  [other_core(): return lax.ppermute(value, 'c', [(0, 1), (1, 0)])]
  transfers between devices with their start and end apart: 24 -> 20, of which waited for: 8 -> 8; matrix products, arithmetic and copies ran while one was open for 7% -> 4% of each run, Pallas kernels for 1% -> 1%
where the time goes in v3:
time: 308 us; the launch traced here: 307 us
  waiting for transfers between devices  158 us (51%)
  starting transfers between devices  67.5 us (22%)
  Pallas kernels  27.9 us (9%)
  blocking collectives  18.6 us (6%)
  between operations  15.6 us (5%)
  local copies, waits for them, and re-layouts  12.3 us (4%)
  matrix products  5.11 us (2%)
    reduce_scatter x1, waiting for transfers between devices, per_device(): lax.psum_scatter(partial_rows, 'z', scatter_dimension=0, tiled=True)  73.9 us
    ppermute x6, waiting for transfers between devices, by_y(): return lax.ppermute(value, 'y', [(i, (i + step) % NY) for i in range(NY)])  44.2 us
    pallas_call x1, Pallas kernels, run_experts(): pl.pallas_call(expert_kernel, out_shape=jax.ShapeDtypeStruct((ALL_ROWS, D...  25.9 us
    ppermute x6, starting transfers between devices, by_y(): return lax.ppermute(value, 'y', [(i, (i + step) % NY) for i in range(NY)])  19.5 us
    all_to_all x1, blocking collectives, per_device(): lax.all_to_all(packed.reshape(NX * N_TP, PIECE, WIDE), SPREAD, 0, 0)  18.6 us
    all_gather x1, waiting for transfers between devices, per_device(): weights_down = lax.all_gather(down_proj[0], TP)  17.3 us
    ppermute x7, starting transfers between devices, other_core(): return lax.ppermute(value, 'c', [(0, 1), (1, 0)])  17.3 us
    all_to_all x1, starting transfers between devices, per_device(): returned = lax.all_to_all(back.reshape(NX * N_TP, PIECE, 512), SPREAD, 0, 0)  16.5 us
  transfers between devices with their start and end apart: 20, of which 8 were waited for; matrix products, arithmetic and copies ran while one was open for 4% of the time, Pallas kernels for 1%

profile of v3, /device:TPU:1, one launch (start us, length us, event | category | flops | bytes accessed | tf_op | source)
XLA Modules:
  0.0 307.1 jit_solution(8893153454958891485)
XLA Ops:
  6.6 0.7 all-gather.3.cloned.1.call-update
  7.3 0.9 copy.43
  8.3 0.7 copy.33
  9.0 10.3 %all-to-all-start = ((bf16[16,8,768]{2,0,1:T(8,128)(2,1)}), bf16[16,8,768]{2,0,1:T(8,128)(2,1)S(1)}, u32[]{:S(2)}, u32[]{:S(2)}) async-start(bf16[16,8,768]{2,0,1:T(8,128)(2,1)} %copy.33), calls=%async_computation | async-start | bytes 393216 | tf_op jit(solution)/shard_map/all_to_all | solution.py:226
  19.3 0.6 dynamic_slice.16
  21.9 1.9 collective-permute-start
  24.0 0.5 broadcast.378
  24.5 0.6 reduce.3
  25.3 0.6 gather_fusion
  26.5 1.8 fusion.88
  28.3 1.7 fusion.11
  30.1 1.9 collective-permute-start.1
  32.0 0.7 iota_compare_fusion.17
  33.1 7.8 %collective-permute-done.1 = bf16[32,512]{1,0:T(8,128)(2,1)S(1)} collective-permute-done((bf16[32,512]{1,0:T(8,128)(2,1)S(1)}, bf16[32,512]{1,0:T(8,128)(2,1)S(1)}, u32[]{:S(2)}, u32[]{:S(2)}) %collective-permute-start.1) | collective-permute-done | bytes 32800 | tf_op jit(solution)/shard_map/ppermute | solution.py:243
  41.4 0.3 convolution_convert_fusion
  41.9 18.6 %all_to_all.25.recv_ref = bf16[32,10,640]{2,1,0:T(8,128)(2,1)} all-to-all(bf16[32,10,640]{2,1,0:T(8,128)(2,1)S(1)} %reshape.317), channel_id=1, replica_groups=mesh['x'=4,'z'=16,'y'=4,'c'=2] {'x','y','c'}, dimensions={0} | all-to-all | bytes 819200 | tf_op jit(solution)/shard_map/all_to_all | solution.py:277
  60.4 2.0 norm_rows.1
  62.4 17.3 %all-gather.3.cloned.1.call-done.refs_14_ = bf16[8,1024,512]{2,1,0:T(8,128)(2,1)} async-done(((bf16[1,1024,512]{2,1,0:T(8,128)(2,1)}), bf16[8,1024,512]{2,1,0:T(8,128)(2,1)}) %all-gather.3.cloned.1.call-update) | async-done | bytes 8388624 | tf_op jit(solution)/shard_map/all_gather | solution.py:222
  79.8 2.2 collective-permute-start.8
  82.0 1.7 fusion.87
  83.7 2.3 collective-permute-start.2
  86.0 4.2 %collective-permute-start.5 = (bf16[2048,256]{1,0:T(8,128)(2,1)S(1)}, bf16[2048,256]{1,0:T(8,128)(2,1)}, u32[]{:S(2)}, u32[]{:S(2)}) collective-permute-start(bf16[2048,256]{1,0:T(8,128)(2,1)S(1)} %get-tuple-element.14), channel_id=1, source_target_pairs={{0,6},{2,0},{4,2},{6,4},{1,7},{3,1},{5,3},{7,5},{8,14},{10,8},{12,... | collective-permute-start | bytes 3145736 | tf_op jit(solution)/shard_map/ppermute | solution.py:175
  90.2 1.9 collective-permute-start.3
  92.1 4.6 %collective-permute-start.4 = (bf16[2048,256]{1,0:T(8,128)(2,1)S(1)}, bf16[2048,256]{1,0:T(8,128)(2,1)}, u32[]{:S(2)}, u32[]{:S(2)}) collective-permute-start(bf16[2048,256]{1,0:T(8,128)(2,1)S(1)} %get-tuple-element.15), channel_id=1, source_target_pairs={{0,6},{2,0},{4,2},{6,4},{1,7},{3,1},{5,3},{7,5},{8,14},{10,8},{12,... | collective-permute-start | bytes 3145736 | tf_op jit(solution)/shard_map/ppermute | solution.py:175
  96.7 14.7 %collective-permute-done.2.refs_1_ = bf16[2048,256]{1,0:T(8,128)(2,1)S(1)} collective-permute-done((bf16[2048,256]{1,0:T(8,128)(2,1)S(1)}, bf16[2048,256]{1,0:T(8,128)(2,1)S(1)}, u32[]{:S(2)}, u32[]{:S(2)}) %collective-permute-start.2) | collective-permute-done | bytes 1048608 | tf_op jit(solution)/shard_map/ppermute | solution.py:175
  111.4 1.9 collective-permute-start.6
  113.3 4.6 %collective-permute-start.7 = (bf16[2048,256]{1,0:T(8,128)(2,1)}, bf16[2048,256]{1,0:T(8,128)(2,1)}, u32[]{:S(2)}, u32[]{:S(2)}) collective-permute-start(bf16[2048,256]{1,0:T(8,128)(2,1)} %collective-permute-done.5.refs_4_), channel_id=1, source_target_pairs={{0,6},{2,0},{4,2},{6,4},{1,7},{3,1},{5,3},{7,5},{8,14},{10,8},{12,... | collective-permute-start | bytes 3145736 | tf_op jit(solution)/shard_map/ppermute | solution.py:175
  117.9 16.0 %collective-permute-done.3.refs_2_ = bf16[2048,256]{1,0:T(8,128)(2,1)S(1)} collective-permute-done((bf16[2048,256]{1,0:T(8,128)(2,1)S(1)}, bf16[2048,256]{1,0:T(8,128)(2,1)S(1)}, u32[]{:S(2)}, u32[]{:S(2)}) %collective-permute-start.3) | collective-permute-done | bytes 1048608 | tf_op jit(solution)/shard_map/ppermute | solution.py:175
  133.9 3.5 %collective-permute-start.10 = (bf16[2048,256]{1,0:T(8,128)(2,1)S(1)}, bf16[2048,256]{1,0:T(8,128)(2,1)S(1)}, u32[]{:S(2)}, u32[]{:S(2)}) collective-permute-start(bf16[2048,256]{1,0:T(8,128)(2,1)S(1)} %collective-permute-done.3.refs_2_), channel_id=1, source_target_pairs={{0,1},{1,0},{2,3},{3,2},{4,5},{5,4},{6,7},{7,6},{8,9},{9,8},{10,11... | collective-permute-start | bytes 3145736 | tf_op jit(solution)/shard_map/ppermute | solution.py:179
  137.4 1.0 copy-done.1
  138.4 1.9 collective-permute-start.12
  140.3 2.4 collective-permute-start.9
  142.8 13.6 %collective-permute-done.6.refs_5_ = bf16[2048,256]{1,0:T(8,128)(2,1)} collective-permute-done((bf16[2048,256]{1,0:T(8,128)(2,1)S(1)}, bf16[2048,256]{1,0:T(8,128)(2,1)}, u32[]{:S(2)}, u32[]{:S(2)}) %collective-permute-start.6) | collective-permute-done | bytes 1048608 | tf_op jit(solution)/shard_map/ppermute | solution.py:175
  156.3 3.0 collective-permute-start.11
  159.3 1.9 collective-permute-start.13
  161.3 1.0 copy-done.4
  162.3 2.4 collective-permute-start.14
  165.0 2.2 collective-permute-done.14.refs_13_
  167.3 1.2 copy-done.2
  168.5 25.9 %experts.1 = bf16[640,4096]{1,0:T(8,128)(2,1)} custom-call(s32[8]{0:T(128)S(1)} %fusion.69.order_ref, bf16[640,4096]{1,0:T(8,128)(2,1)} %all-gather.5.cloned.1.call-done.all_ref, bf16[320,640]{1,0:T(8,128)(2,1)S(1)} %fusion.10.take_ref, bf16[640,320]{1,0:T(8,128)(2,1)S(1)} %fusion.9.put_ref, bf16[4096,256]{1,0:T(8,128)(2,1)} %bitcast.24.refs_0_, ...), custom_call_target="tpu_custom_call" | custom-call | tf_op jit(solution)/shard_map/experts/pallas_call | solution.py:155
  194.4 0.6 copy-done.8
  195.1 73.9 %reduce-scatter.2.cloned.1.call-done = bf16[40,4096]{1,0:T(8,128)(2,1)} async-done(((bf16[640,4096]{1,0:T(8,128)(2,1)}), bf16[40,4096]{1,0:T(8,128)(2,1)}) %reduce-scatter.2.cloned.1.call-update) | async-done | bytes 327696 | tf_op jit(solution)/shard_map/reduce_scatter | solution.py:295
  269.1 1.1 copy.46
  270.2 1.0 copy.39
  271.2 16.5 %all-to-all-start.2 = ((bf16[32,10,512]{2,1,0:T(8,128)(2,1)}), bf16[32,10,512]{2,1,0:T(8,128)(2,1)S(1)}, u32[]{:S(2)}, u32[]{:S(2)}) async-start(bf16[32,10,512]{2,1,0:T(8,128)(2,1)} %copy.39), calls=%async_computation.3 | async-start | bytes 1048576 | tf_op jit(solution)/shard_map/all_to_all | solution.py:297
  287.7 11.6 %all-to-all-done.2 = bf16[32,10,512]{2,1,0:T(8,128)(2,1)S(1)} async-done(((bf16[32,10,512]{2,1,0:T(8,128)(2,1)}), bf16[32,10,512]{2,1,0:T(8,128)(2,1)S(1)}, u32[]{:S(2)}, u32[]{:S(2)}) %all-to-all-start.2) | async-done | bytes 327712 | tf_op jit(solution)/shard_map/all_to_all | solution.py:297
  299.4 0.3 convolution_multiply_fusion.2
  299.7 0.9 fusion.8
  (88 shorter events, 2.7 us)
Async XLA Ops:
  6.5 18.7 %copy-start = (bf16[128,16,256]{2,1,0:T(8,128)(2,1)S(1)}, bf16[128,16,256]{2,1,0:T(8,128)(2,1)}, u32[]{:S(2)}) copy-start(bf16[128,16,256]{2,1,0:T(8,128)(2,1)} %param.15) | copy-start | bytes 3145732
  6.5 1.7 copy-start.6
  6.5 12.8 %copy-start.12 = (s32[64]{0:T(128)S(1)}, s32[64]{0:T(128)}, u32[]{:S(2)}) copy-start(s32[64]{0:T(128)} %param.23) | copy-start | bytes 772
  6.5 15.3 %copy-start.5 = (bf16[128,512]{1,0:T(8,128)(2,1)S(1)}, bf16[128,512]{1,0:T(8,128)(2,1)}, u32[]{:S(2)}) copy-start(bf16[128,512]{1,0:T(8,128)(2,1)} %param.16) | copy-start | bytes 393220
  6.5 17.3 %copy-start.10 = (s32[256]{0:T(256)S(1)}, s32[256]{0:T(256)}, u32[]{:S(2)}) copy-start(s32[256]{0:T(256)} %param.21) | copy-start | bytes 3076
  6.5 17.4 %copy-start.11 = (s32[256]{0:T(256)S(1)}, s32[256]{0:T(256)}, u32[]{:S(2)}) copy-start(s32[256]{0:T(256)} %param.20) | copy-start | bytes 3076
  6.6 17.9 %copy-start.13 = (s32[1,128]{1,0:T(1,128)S(1)}, s32[1,128]{1,0:T(1,128)}, u32[]{:S(2)}) copy-start(s32[1,128]{1,0:T(1,128)} %param.22) | copy-start | bytes 1540
  6.6 73.2 %all-gather.3.cloned.1.call-start = ((), (), s32[]{:S(2)}) async-start(), calls=%async_computation.4 | async-start | bytes 9437184 | tf_op jit(solution)/shard_map/all_gather | solution.py:222
  9.0 17.0 %copy-start.7 = (s32[128,2]{0,1:T(2,128)S(1)}, s32[128,2]{0,1:T(2,128)}, u32[]{:S(2)}) copy-start(s32[128,2]{0,1:T(2,128)} %param.24) | copy-start | bytes 3076
  9.0 17.4 %all-to-all-start = ((bf16[16,8,768]{2,0,1:T(8,128)(2,1)}), bf16[16,8,768]{2,0,1:T(8,128)(2,1)S(1)}, u32[]{:S(2)}, u32[]{:S(2)}) async-start(bf16[16,8,768]{2,0,1:T(8,128)(2,1)} %copy.33), calls=%async_computation | async-start | bytes 393216 | tf_op jit(solution)/shard_map/all_to_all | solution.py:226
  19.3 147.9 %all-gather.5.cloned.1.call-start = ((), (), s32[]{:S(2)}) async-start(), calls=%async_computation.5 | async-start | bytes 5570560 | tf_op jit(solution)/shard_map/all_gather | solution.py:280
  21.9 11.2 %collective-permute-start = (bf16[32,512]{1,0:T(8,128)(2,1)S(1)}, bf16[32,512]{1,0:T(8,128)(2,1)S(1)}, u32[]{:S(2)}, u32[]{:S(2)}) collective-permute-start(bf16[32,512]{1,0:T(8,128)(2,1)S(1)} %dynamic-slice_bitcast_fusion), channel_id=1, source_target_pairs={{0,8},{8,16},{16,24},{24,32},{32,40},{40,48},{48,56},{56,64},{64,7... | collective-permute-start | bytes 98312 | tf_op jit(solution)/shard_map/ppermute | solution.py:229
  28.3 12.6 %copy-start.9 = (f32[512]{0:T(512)S(1)}, f32[512]{0:T(512)}, u32[]{:S(2)}) copy-start(f32[512]{0:T(512)} %param.17) | copy-start | bytes 6148
  30.1 10.8 %collective-permute-start.1 = (bf16[32,512]{1,0:T(8,128)(2,1)S(1)}, bf16[32,512]{1,0:T(8,128)(2,1)S(1)}, u32[]{:S(2)}, u32[]{:S(2)}) collective-permute-start(bf16[32,512]{1,0:T(8,128)(2,1)S(1)} %fusion.45), channel_id=1, source_target_pairs={{0,8},{8,16},{16,24},{24,32},{32,40},{40,48},{48,56},{56,64},{64,7... | collective-permute-start | bytes 98312 | tf_op jit(solution)/shard_map/ppermute | solution.py:243
  79.8 189.3 %reduce-scatter.2.cloned.1.call-start = ((), (), s32[]{:S(2)}) async-start(), calls=%async_computation.6 | async-start | bytes 5570560 | tf_op jit(solution)/shard_map/reduce_scatter | solution.py:295
  79.8 60.5 %collective-permute-start.8 = (bf16[4096,256]{1,0:T(8,128)(2,1)}, bf16[4096,256]{1,0:T(8,128)(2,1)S(1)}, u32[]{:S(2)}, u32[]{:S(2)}) collective-permute-start(bf16[4096,256]{1,0:T(8,128)(2,1)} %bitcast.24.refs_0_), channel_id=1, source_target_pairs={{0,1},{1,0},{2,3},{3,2},{4,5},{5,4},{6,7},{7,6},{8,9},{9,8},{10,11... | collective-permute-start | bytes 6291464 | tf_op jit(solution)/shard_map/ppermute | solution.py:179
  83.7 27.7 %collective-permute-start.2 = (bf16[2048,256]{1,0:T(8,128)(2,1)S(1)}, bf16[2048,256]{1,0:T(8,128)(2,1)S(1)}, u32[]{:S(2)}, u32[]{:S(2)}) collective-permute-start(bf16[2048,256]{1,0:T(8,128)(2,1)S(1)} %get-tuple-element.15), channel_id=1, source_target_pairs={{0,2},{2,4},{4,6},{6,0},{1,3},{3,5},{5,7},{7,1},{8,10},{10,12},{12... | collective-permute-start | bytes 3145736 | tf_op jit(solution)/shard_map/ppermute | solution.py:175
  86.0 27.3 %collective-permute-start.5 = (bf16[2048,256]{1,0:T(8,128)(2,1)S(1)}, bf16[2048,256]{1,0:T(8,128)(2,1)}, u32[]{:S(2)}, u32[]{:S(2)}) collective-permute-start(bf16[2048,256]{1,0:T(8,128)(2,1)S(1)} %get-tuple-element.14), channel_id=1, source_target_pairs={{0,6},{2,0},{4,2},{6,4},{1,7},{3,1},{5,3},{7,5},{8,14},{10,8},{12,... | collective-permute-start | bytes 3145736 | tf_op jit(solution)/shard_map/ppermute | solution.py:175
  90.2 43.7 %collective-permute-start.3 = (bf16[2048,256]{1,0:T(8,128)(2,1)S(1)}, bf16[2048,256]{1,0:T(8,128)(2,1)S(1)}, u32[]{:S(2)}, u32[]{:S(2)}) collective-permute-start(bf16[2048,256]{1,0:T(8,128)(2,1)S(1)} %get-tuple-element.14), channel_id=1, source_target_pairs={{0,2},{2,4},{4,6},{6,0},{1,3},{3,5},{5,7},{7,1},{8,10},{10,12},{12... | collective-permute-start | bytes 3145736 | tf_op jit(solution)/shard_map/ppermute | solution.py:175
  92.1 46.3 %collective-permute-start.4 = (bf16[2048,256]{1,0:T(8,128)(2,1)S(1)}, bf16[2048,256]{1,0:T(8,128)(2,1)}, u32[]{:S(2)}, u32[]{:S(2)}) collective-permute-start(bf16[2048,256]{1,0:T(8,128)(2,1)S(1)} %get-tuple-element.15), channel_id=1, source_target_pairs={{0,6},{2,0},{4,2},{6,4},{1,7},{3,1},{5,3},{7,5},{8,14},{10,8},{12,... | collective-permute-start | bytes 3145736 | tf_op jit(solution)/shard_map/ppermute | solution.py:175
  111.4 44.9 %collective-permute-start.6 = (bf16[2048,256]{1,0:T(8,128)(2,1)S(1)}, bf16[2048,256]{1,0:T(8,128)(2,1)}, u32[]{:S(2)}, u32[]{:S(2)}) collective-permute-start(bf16[2048,256]{1,0:T(8,128)(2,1)S(1)} %collective-permute-done.2.refs_1_), channel_id=1, source_target_pairs={{0,2},{2,4},{4,6},{6,0},{1,3},{3,5},{5,7},{7,1},{8,10},{10,12},{12... | collective-permute-start | bytes 3145736 | tf_op jit(solution)/shard_map/ppermute | solution.py:175
  113.3 46.0 %collective-permute-start.7 = (bf16[2048,256]{1,0:T(8,128)(2,1)}, bf16[2048,256]{1,0:T(8,128)(2,1)}, u32[]{:S(2)}, u32[]{:S(2)}) collective-permute-start(bf16[2048,256]{1,0:T(8,128)(2,1)} %collective-permute-done.5.refs_4_), channel_id=1, source_target_pairs={{0,6},{2,0},{4,2},{6,4},{1,7},{3,1},{5,3},{7,5},{8,14},{10,8},{12,... | collective-permute-start | bytes 3145736 | tf_op jit(solution)/shard_map/ppermute | solution.py:175
  133.9 27.4 %collective-permute-start.10 = (bf16[2048,256]{1,0:T(8,128)(2,1)S(1)}, bf16[2048,256]{1,0:T(8,128)(2,1)S(1)}, u32[]{:S(2)}, u32[]{:S(2)}) collective-permute-start(bf16[2048,256]{1,0:T(8,128)(2,1)S(1)} %collective-permute-done.3.refs_2_), channel_id=1, source_target_pairs={{0,1},{1,0},{2,3},{3,2},{4,5},{5,4},{6,7},{7,6},{8,9},{9,8},{10,11... | collective-permute-start | bytes 3145736 | tf_op jit(solution)/shard_map/ppermute | solution.py:179
  137.4 1.0 copy-start.1
  138.4 26.6 %collective-permute-start.12 = (bf16[2048,256]{1,0:T(8,128)(2,1)}, bf16[2048,256]{1,0:T(8,128)(2,1)}, u32[]{:S(2)}, u32[]{:S(2)}) collective-permute-start(bf16[2048,256]{1,0:T(8,128)(2,1)} %collective-permute-done.5.refs_4_), channel_id=1, source_target_pairs={{0,1},{1,0},{2,3},{3,2},{4,5},{5,4},{6,7},{7,6},{8,9},{9,8},{10,11... | collective-permute-start | bytes 3145736 | tf_op jit(solution)/shard_map/ppermute | solution.py:179
  140.3 20.9 %copy-start.3 = (bf16[4096,256]{1,0:T(8,128)(2,1)}, bf16[4096,256]{1,0:T(8,128)(2,1)S(1)}, u32[]{:S(2)}) copy-start(bf16[4096,256]{1,0:T(8,128)(2,1)S(1)} %collective-permute-done.8.refs_7_) | copy-start | bytes 6291460
  140.3 24.7 %collective-permute-start.9 = (bf16[2048,256]{1,0:T(8,128)(2,1)S(1)}, bf16[2048,256]{1,0:T(8,128)(2,1)}, u32[]{:S(2)}, u32[]{:S(2)}) collective-permute-start(bf16[2048,256]{1,0:T(8,128)(2,1)S(1)} %collective-permute-done.2.refs_1_), channel_id=1, source_target_pairs={{0,1},{1,0},{2,3},{3,2},{4,5},{5,4},{6,7},{7,6},{8,9},{9,8},{10,11... | collective-permute-start | bytes 3145736 | tf_op jit(solution)/shard_map/ppermute | solution.py:179
  156.3 8.7 %collective-permute-start.11 = (bf16[2048,256]{1,0:T(8,128)(2,1)}, bf16[2048,256]{1,0:T(8,128)(2,1)}, u32[]{:S(2)}, u32[]{:S(2)}) collective-permute-start(bf16[2048,256]{1,0:T(8,128)(2,1)} %collective-permute-done.4.refs_3_), channel_id=1, source_target_pairs={{0,1},{1,0},{2,3},{3,2},{4,5},{5,4},{6,7},{7,6},{8,9},{9,8},{10,11... | collective-permute-start | bytes 3145736 | tf_op jit(solution)/shard_map/ppermute | solution.py:179
  159.3 5.7 %collective-permute-start.13 = (bf16[2048,256]{1,0:T(8,128)(2,1)}, bf16[2048,256]{1,0:T(8,128)(2,1)}, u32[]{:S(2)}, u32[]{:S(2)}) collective-permute-start(bf16[2048,256]{1,0:T(8,128)(2,1)} %collective-permute-done.6.refs_5_), channel_id=1, source_target_pairs={{0,1},{1,0},{2,3},{3,2},{4,5},{5,4},{6,7},{7,6},{8,9},{9,8},{10,11... | collective-permute-start | bytes 3145736 | tf_op jit(solution)/shard_map/ppermute | solution.py:179
  161.3 1.0 copy-start.4
  162.3 5.0 %collective-permute-start.14 = (bf16[2048,256]{1,0:T(8,128)(2,1)}, bf16[2048,256]{1,0:T(8,128)(2,1)}, u32[]{:S(2)}, u32[]{:S(2)}) collective-permute-start(bf16[2048,256]{1,0:T(8,128)(2,1)} %collective-permute-done.7.refs_6_), channel_id=1, source_target_pairs={{0,1},{1,0},{2,3},{3,2},{4,5},{5,4},{6,7},{7,6},{8,9},{9,8},{10,11... | collective-permute-start | bytes 3145736 | tf_op jit(solution)/shard_map/ppermute | solution.py:179
  167.3 1.2 copy-start.2
  194.4 0.7 copy-start.8
  271.2 28.1 %all-to-all-start.2 = ((bf16[32,10,512]{2,1,0:T(8,128)(2,1)}), bf16[32,10,512]{2,1,0:T(8,128)(2,1)S(1)}, u32[]{:S(2)}, u32[]{:S(2)}) async-start(bf16[32,10,512]{2,1,0:T(8,128)(2,1)} %copy.39), calls=%async_computation.3 | async-start | bytes 1048576 | tf_op jit(solution)/shard_map/all_to_all | solution.py:297
Sparse Core Ops, SparseCore 0:
  9.6 70.1 all-gather.2
  81.8 74.1 all-gather.4
  194.6 74.4 reduce-scatter.1

commit v4 on v3

--- a/solution.py
+++ b/solution.py
@@ -91,84 +91,130 @@
 
 
 CHUNKS = 4
-
-
-def expert_kernel(order_ref, all_ref, take_ref, put_ref, *refs):
-    in_refs, down_hbm = refs[:14], refs[14]
-    out_ref, gathered, rows, in_buf, down_buf, active, whole, sems = refs[15:]
-    width = D // CHUNKS
-    half = D // 2
-    count = iter(range(30))
+HALF = D // 2
+DEEP = 512
+
+
+def activate(rows, weights):
+    both = jnp.dot(rows, weights, preferred_element_type=jnp.float32)
+    gate = both[:, :128]
+    return (gate / (1.0 + jnp.exp(-gate)) * both[:, 128:]).astype(jnp.bfloat16)
+
+
+def starter(sems):
+    numbers = iter(range(sems.shape[0]))
 
     def begin(source, target):
-        copy = pltpu.make_async_copy(source, target, sems.at[next(count)])
+        copy = pltpu.make_async_copy(source, target, sems.at[next(numbers)])
         copy.start()
         return copy
 
+    return begin
+
+
+def near_kernel(all_ref, take_ref, *refs):
+    in_refs = refs[:6]
+    rows_ref, active_ref, gathered, in_buf, sems = refs[6:]
+    begin = starter(sems)
+    width = D // CHUNKS
     parts = [
         begin(all_ref.at[:, pl.ds(n * width, width)], gathered.at[n]) for n in range(CHUNKS)
     ]
-    loads = []
+    loads = [begin(in_refs[k], in_buf.at[k]) for k in range(6)]
+    for n in range(CHUNKS):
+        parts[n].wait()
+        rows_ref[:, n * width : (n + 1) * width] = jnp.dot(
+            take_ref[...], gathered[n], preferred_element_type=jnp.float32
+        ).astype(jnp.bfloat16)
+    for k in range(6):
+        loads[k].wait()
+        active_ref[k] = activate(rows_ref[...], in_buf[k])
+
+
+def far_kernel(order_ref, rows_ref, active_ref, put_ref, low_ref, *refs):
+    in_refs, down_refs = refs[:4], refs[4:14]
+    out_ref, in_buf, down_buf, active, whole, parts, sems = refs[14:]
+    begin = starter(sems)
+    loads = [
+        [
+            begin(in_refs[2 * core], in_buf.at[core, pl.ds(0, HALF)]),
+            begin(in_refs[2 * core + 1], in_buf.at[core, pl.ds(HALF, HALF)]),
+        ]
+        for core in range(NC)
+    ]
+    downs = []
     for core in range(NC):
         for k in range(NY):
-            chunk, first = in_buf.at[core * NY + k], core * 7 + 2 * k
-            if k == 0:
-                loads.append([begin(in_refs[first], chunk)])
+            slot = core * NY + k
+            group = [begin(low_ref.at[order_ref[slot]], down_buf.at[slot, pl.ds(0, DEEP)])]
+            if k < 3:
+                group.append(begin(down_refs[core * 5 + k], down_buf.at[slot, pl.ds(DEEP, DEEP)]))
             else:
-                loads.append(
-                    [
-                        begin(in_refs[first - 1], chunk.at[pl.ds(0, half)]),
-                        begin(in_refs[first], chunk.at[pl.ds(half, half)]),
-                    ]
-                )
-    downs = [begin(down_hbm.at[t], down_buf.at[t]) for t in range(N_TP)]
-    for n in range(CHUNKS):
-        parts[n].wait()
-        rows[:, n * width : (n + 1) * width] = jnp.dot(
-            take_ref[...], gathered[n], preferred_element_type=jnp.float32
-        ).astype(jnp.bfloat16)
-    for k in range(N_TP):
-        for copy in loads[k]:
+                for i in range(2):
+                    place = pl.ds(DEEP + i * DEEP // 2, DEEP // 2)
+                    group.append(begin(down_refs[core * 5 + 3 + i], down_buf.at[slot, place]))
+            downs.append(group)
+    for core in range(NC):
+        for k in range(3):
+            active[order_ref[core * NY + k]] = active_ref[core * 3 + k]
+        for copy in loads[core]:
             copy.wait()
-        both = jnp.dot(rows[...], in_buf[k], preferred_element_type=jnp.float32)
-        gate = both[:, :128]
-        active[order_ref[k]] = (gate / (1.0 + jnp.exp(-gate)) * both[:, 128:]).astype(jnp.bfloat16)
+        active[order_ref[core * NY + 3]] = activate(rows_ref[...], in_buf[core])
     for t in range(N_TP):
         whole[:, t * 128 : (t + 1) * 128] = active[t]
     outs = []
-    for t in range(N_TP):
-        downs[t].wait()
-        part = jnp.dot(whole[...], down_buf[t], preferred_element_type=jnp.float32)
-        n, lane = t // 2, t % 2 * 512
-        gathered[n, :, lane : lane + 512] = jnp.dot(
+    for slot in range(N_TP):
+        for copy in downs[slot]:
+            copy.wait()
+        part = jnp.dot(whole[...], down_buf[slot], preferred_element_type=jnp.float32)
+        parts[slot] = jnp.dot(
             put_ref[...], part.astype(jnp.bfloat16), preferred_element_type=jnp.float32
         ).astype(jnp.bfloat16)
-        if t % 2:
-            outs.append(begin(gathered.at[n], out_ref.at[:, pl.ds(n * width, width)]))
+        lanes = pl.ds(pl.multiple_of(order_ref[slot] * 512, 512), 512)
+        outs.append(begin(parts.at[slot], out_ref.at[:, lanes]))
     for copy in outs:
         copy.wait()
 
 
-def run_experts(order, all_rows, take, put, weights_in, weights_down):
+def run_experts(order, all_rows, take, put, near_in, far_in, low_down, high_down):
     far = pl.BlockSpec(memory_space=pltpu.HBM)
     local = pl.BlockSpec(memory_space=pltpu.VMEM)
+    rows, active = pl.pallas_call(
+        near_kernel,
+        out_shape=(
+            jax.ShapeDtypeStruct((OWN_ROWS, D), jnp.bfloat16),
+            jax.ShapeDtypeStruct((6, OWN_ROWS, 128), jnp.bfloat16),
+        ),
+        in_specs=[far, local] + [far] * 6,
+        out_specs=(local, local),
+        scratch_shapes=[
+            pltpu.VMEM((CHUNKS, ALL_ROWS, D // CHUNKS), jnp.bfloat16),
+            pltpu.VMEM((6, D, 256), jnp.bfloat16),
+            pltpu.SemaphoreType.DMA((CHUNKS + 6,)),
+        ],
+        compiler_params=pltpu.CompilerParams(vmem_limit_bytes=NEAR_VMEM),
+        name="near_experts",
+    )(all_rows, take, *near_in)
     return pl.pallas_call(
-        expert_kernel,
+        far_kernel,
         out_shape=jax.ShapeDtypeStruct((ALL_ROWS, D), jnp.bfloat16),
-        in_specs=[pl.BlockSpec(memory_space=pltpu.SMEM), far, local, local] + [far] * 15,
+        in_specs=[pl.BlockSpec(memory_space=pltpu.SMEM)] + [local] * 3 + [far] * 15,
         out_specs=far,
         scratch_shapes=[
-            pltpu.VMEM((CHUNKS, ALL_ROWS, D // CHUNKS), jnp.bfloat16),
-            pltpu.VMEM((OWN_ROWS, D), jnp.bfloat16),
-            pltpu.VMEM((N_TP, D, 256), jnp.bfloat16),
+            pltpu.VMEM((NC, D, 256), jnp.bfloat16),
             pltpu.VMEM((N_TP, 1024, 512), jnp.bfloat16),
             pltpu.VMEM((N_TP, OWN_ROWS, 128), jnp.bfloat16),
             pltpu.VMEM((OWN_ROWS, 1024), jnp.bfloat16),
+            pltpu.VMEM((N_TP, ALL_ROWS, 512), jnp.bfloat16),
             pltpu.SemaphoreType.DMA((30,)),
         ],
-        compiler_params=pltpu.CompilerParams(vmem_limit_bytes=46 << 20),
-        name="experts",
-    )(order, all_rows, take, put, *weights_in, weights_down)
+        compiler_params=pltpu.CompilerParams(vmem_limit_bytes=FAR_VMEM),
+        name="far_experts",
+    )(order, rows, active, put, low_down, *far_in, *high_down)
+
+
+NEAR_VMEM = 50 << 20
+FAR_VMEM = 50 << 20
 
 
 def by_y(value, step):
@@ -179,14 +225,13 @@
     return lax.ppermute(value, "c", [(0, 1), (1, 0)])
 
 
-def gather_pieces(own):
-    half = own.shape[0] // 2
-    top, bottom = own[:half], own[half:]
-    below_top, above_bottom = by_y(top, 1), by_y(bottom, -1)
-    below_bottom, above_top = by_y(bottom, 1), by_y(top, -1)
-    far_top, far_bottom = by_y(below_top, 1), by_y(above_bottom, -1)
-    pieces = [own, below_top, below_bottom, above_top, above_bottom, far_top, far_bottom]
+def both_cores(pieces):
     return pieces + [other_core(piece) for piece in pieces]
+
+
+def far_halves(below, above):
+    half = below.shape[0] // 2
+    return both_cores([by_y(below[:half], 1), by_y(above[half:], -1)])
 
 
 def three_parts(values):
@@ -219,7 +264,8 @@
     handing = [(i, (i + 1) % N_REP) for i in range(N_REP)]
 
     in_own = gate_up[0]
-    weights_down = lax.all_gather(down_proj[0], TP)
+    low_down = lax.all_gather(down_proj[0, :DEEP], TP)
+    down_own = down_proj[0, DEEP:]
     mixed = jnp.concatenate(
         [queries.reshape(-1, N_TP, 512), fresh_kv.reshape(-1, N_TP, 256)], axis=2
     )
@@ -276,9 +322,17 @@
     packed = jnp.dot(placing, payload, preferred_element_type=jnp.float32).astype(jnp.bfloat16)
     received = lax.all_to_all(packed.reshape(NX * N_TP, PIECE, WIDE), SPREAD, 0, 0)
     normed = norm_rows(received.reshape(NX * N_TP, PIECE, WIDE))
-    normed, in_own, weights_down = lax.optimization_barrier((normed, in_own, weights_down))
+    normed, in_own, low_down = lax.optimization_barrier((normed, in_own, low_down))
     all_rows = lax.all_gather(normed, "z", tiled=True)
-    weights_in = gather_pieces(in_own)
+    in_below, in_above, down_own = lax.optimization_barrier(
+        (by_y(in_own, 1), by_y(in_own, -1), down_own)
+    )
+    far_in = far_halves(in_below, in_above)
+    near_in = both_cores([in_own, in_below, in_above])
+    down_below, down_above = by_y(down_own, 1), by_y(down_own, -1)
+    near_down = both_cores([down_own, down_below, down_above])
+    far_down = far_halves(down_below, down_above)
+    high_down = near_down[:3] + far_down[:2] + near_down[3:] + far_down[2:]
     my_y, my_core = lax.axis_index("y"), lax.axis_index("c")
     piece = jnp.arange(N_TP, dtype=jnp.int32)
     step = piece % 4
@@ -291,7 +345,9 @@
     own_index = jnp.arange(OWN_ROWS, dtype=jnp.int32)
     take = (own_index[:, None] == compact[None, :]).astype(jnp.bfloat16)
     put = (compact[:, None] == own_index[None, :]).astype(jnp.bfloat16)
-    partial_rows = run_experts(order, all_rows, take, put, weights_in, weights_down)
+    partial_rows = run_experts(
+        order, all_rows, take, put, near_in, far_in, low_down, high_down
+    )
     summed = lax.psum_scatter(partial_rows, "z", scatter_dimension=0, tiled=True)
     back = summed.reshape(NX, PIECE, N_TP, 512).transpose(0, 2, 1, 3)
     returned = lax.all_to_all(back.reshape(NX * N_TP, PIECE, 512), SPREAD, 0, 0)

time: 308 us -> 332 us (1.078)
  starting transfers between devices: 67.5 us -> 82.8 us
  waiting for transfers between devices: 158 us -> 162 us
    ppermute x6 -> x8, waiting for transfers between devices: 44.2 us -> 68.4 us  [by_y(): return lax.ppermute(value, 'y', [(i, (i + step) % NY) for i in range(NY)])]
    all_gather x1, waiting for transfers between devices: 17.3 us -> 0.01 us  [per_device(): low_down = lax.all_gather(down_proj[0, :DEEP], TP)]
    ppermute x7 -> x10, starting transfers between devices: 17.3 us -> 27.8 us  [other_core(): return lax.ppermute(value, 'c', [(0, 1), (1, 0)])]
    ppermute x6 -> x8, starting transfers between devices: 19.5 us -> 24.1 us  [by_y(): return lax.ppermute(value, 'y', [(i, (i + step) % NY) for i in range(NY)])]
    pallas_call x1 -> x2, Pallas kernels: 25.9 us -> 28.6 us  [the longest x1 15.4 us: run_experts(): pl.pallas_call(far_kernel, out_shape=jax.ShapeDtypeStruct((ALL_ROWS, D),...]
  transfers between devices with their start and end apart: 20 -> 25, of which waited for: 8 -> 11; matrix products, arithmetic and copies ran while one was open for 4% -> 4% of each run, Pallas kernels for 1% -> 5%
where the time goes in v4:
time: 332 us; the launch traced here: 331 us
  waiting for transfers between devices  162 us (49%)
  starting transfers between devices  82.8 us (25%)
  Pallas kernels  30.6 us (9%)
  blocking collectives  18.6 us (6%)
  between operations  15.8 us (5%)
  local copies, waits for them, and re-layouts  14.3 us (4%)
  matrix products  5.06 us (2%)
    reduce_scatter x1, waiting for transfers between devices, per_device(): lax.psum_scatter(partial_rows, 'z', scatter_dimension=0, tiled=True)  71.1 us
    ppermute x8, waiting for transfers between devices, by_y(): return lax.ppermute(value, 'y', [(i, (i + step) % NY) for i in range(NY)])  68.4 us
    ppermute x10, starting transfers between devices, other_core(): return lax.ppermute(value, 'c', [(0, 1), (1, 0)])  27.8 us
    ppermute x8, starting transfers between devices, by_y(): return lax.ppermute(value, 'y', [(i, (i + step) % NY) for i in range(NY)])  24.1 us
    all_to_all x1, blocking collectives, per_device(): lax.all_to_all(packed.reshape(NX * N_TP, PIECE, WIDE), SPREAD, 0, 0)  18.6 us
    all_to_all x1, starting transfers between devices, per_device(): returned = lax.all_to_all(back.reshape(NX * N_TP, PIECE, 512), SPREAD, 0, 0)  16.7 us
    pallas_call x1, Pallas kernels, run_experts(): pl.pallas_call(far_kernel, out_shape=jax.ShapeDtypeStruct((ALL_ROWS, D),...  15.4 us
    pallas_call x1, Pallas kernels, run_experts(): pl.pallas_call(near_kernel, out_shape=(jax.ShapeDtypeStruct((OWN_ROWS, D)...  13.3 us
  transfers between devices with their start and end apart: 25, of which 11 were waited for; matrix products, arithmetic and copies ran while one was open for 4% of the time, Pallas kernels for 5%

profile of v4, /device:TPU:1, one launch (start us, length us, event | category | flops | bytes accessed | tf_op | source)
XLA Modules:
  0.0 331.1 jit_solution(1253954961164504418)
XLA Ops:
  6.5 2.2 slice_bitcast_fusion
  8.9 0.7 copy.33
  9.6 10.3 %all-to-all-start = ((bf16[16,8,768]{2,0,1:T(8,128)(2,1)}), bf16[16,8,768]{2,0,1:T(8,128)(2,1)S(1)}, u32[]{:S(2)}, u32[]{:S(2)}) async-start(bf16[16,8,768]{2,0,1:T(8,128)(2,1)} %copy.33), calls=%async_computation | async-start | bytes 393216 | tf_op jit(solution)/shard_map/all_to_all | solution.py:272
  22.5 1.9 collective-permute-start
  25.1 0.7 reduce.3
  27.2 1.8 fusion.87
  28.9 1.7 fusion.11
  30.8 1.9 collective-permute-start.1
  33.7 7.9 %collective-permute-done.1 = bf16[32,512]{1,0:T(8,128)(2,1)S(1)} collective-permute-done((bf16[32,512]{1,0:T(8,128)(2,1)S(1)}, bf16[32,512]{1,0:T(8,128)(2,1)S(1)}, u32[]{:S(2)}, u32[]{:S(2)}) %collective-permute-start.1) | collective-permute-done | bytes 32800 | tf_op jit(solution)/shard_map/ppermute | solution.py:289
  43.2 18.6 %all_to_all.25.recv_ref = bf16[32,10,640]{2,1,0:T(8,128)(2,1)} all-to-all(bf16[32,10,640]{2,1,0:T(8,128)(2,1)S(1)} %reshape.317), channel_id=1, replica_groups=mesh['x'=4,'z'=16,'y'=4,'c'=2] {'x','y','c'}, dimensions={0} | all-to-all | bytes 819200 | tf_op jit(solution)/shard_map/all_to_all | solution.py:323
  61.7 2.0 norm_rows.1
  63.8 1.9 collective-permute-start.2
  65.8 4.6 %collective-permute-start.3 = (bf16[4096,256]{1,0:T(8,128)(2,1)}, bf16[4096,256]{1,0:T(8,128)(2,1)}, u32[]{:S(2)}, u32[]{:S(2)}) collective-permute-start(bf16[4096,256]{1,0:T(8,128)(2,1)} %bitcast.99), channel_id=1, source_target_pairs={{0,6},{2,0},{4,2},{6,4},{1,7},{3,1},{5,3},{7,5},{8,14},{10,8},{12,... | collective-permute-start | bytes 6291464 | tf_op jit(solution)/shard_map/ppermute | solution.py:221
  70.4 2.3 collective-permute-start.4
  72.6 42.0 %collective-permute-done.2.refs_1_ = bf16[4096,256]{1,0:T(8,128)(2,1)} collective-permute-done((bf16[4096,256]{1,0:T(8,128)(2,1)}, bf16[4096,256]{1,0:T(8,128)(2,1)}, u32[]{:S(2)}, u32[]{:S(2)}) %collective-permute-start.2) | collective-permute-done | bytes 2097184 | tf_op jit(solution)/shard_map/ppermute | solution.py:221
  114.6 1.0 collective-permute-done.3.refs_2_
  115.6 2.8 collective-permute-start.5
  118.4 1.9 collective-permute-start.11
  120.3 2.2 collective-permute-start.6
  122.5 5.0 %collective-permute-start.12 = (bf16[512,512]{1,0:T(8,128)(2,1)S(1)}, bf16[512,512]{1,0:T(8,128)(2,1)S(1)}, u32[]{:S(2)}, u32[]{:S(2)}) collective-permute-start(bf16[512,512]{1,0:T(8,128)(2,1)S(1)} %get-tuple-element.20.refs_4_), channel_id=1, source_target_pairs={{0,6},{2,0},{4,2},{6,4},{1,7},{3,1},{5,3},{7,5},{8,14},{10,8},{12,... | collective-permute-start | bytes 1572872 | tf_op jit(solution)/shard_map/ppermute | solution.py:221
  127.6 1.3 slice.62
  128.9 1.3 slice.61
  130.2 3.6 %collective-permute-start.8 = (bf16[2048,256]{1,0:T(8,128)(2,1)S(1)}, bf16[2048,256]{1,0:T(8,128)(2,1)}, u32[]{:S(2)}, u32[]{:S(2)}) collective-permute-start(bf16[2048,256]{1,0:T(8,128)(2,1)S(1)} %slice.62), channel_id=1, source_target_pairs={{0,6},{2,0},{4,2},{6,4},{1,7},{3,1},{5,3},{7,5},{8,14},{10,8},{12,... | collective-permute-start | bytes 3145736 | tf_op jit(solution)/shard_map/ppermute | solution.py:221
  133.9 2.2 collective-permute-done.11.refs_5_
  136.1 1.9 collective-permute-start.7
  138.4 4.2 %collective-permute-start.15 = (bf16[512,512]{1,0:T(8,128)(2,1)S(1)}, bf16[512,512]{1,0:T(8,128)(2,1)S(1)}, u32[]{:S(2)}, u32[]{:S(2)}) collective-permute-start(bf16[512,512]{1,0:T(8,128)(2,1)S(1)} %get-tuple-element.20.refs_4_), channel_id=1, source_target_pairs={{0,1},{1,0},{2,3},{3,2},{4,5},{5,4},{6,7},{7,6},{8,9},{9,8},{10,11... | collective-permute-start | bytes 1572872 | tf_op jit(solution)/shard_map/ppermute | solution.py:225
  142.6 1.5 collective-permute-done.15.refs_9_
  144.1 3.1 collective-permute-start.13
  147.2 21.8 %collective-permute-done.13.refs_7_ = bf16[256,512]{1,0:T(8,128)(2,1)S(1)} collective-permute-done((bf16[256,512]{1,0:T(8,128)(2,1)S(1)}, bf16[256,512]{1,0:T(8,128)(2,1)S(1)}, u32[]{:S(2)}, u32[]{:S(2)}) %collective-permute-start.13) | collective-permute-done | bytes 262176 | tf_op jit(solution)/shard_map/ppermute | solution.py:221
  169.1 1.9 collective-permute-start.14
  171.0 3.6 %collective-permute-start.10 = (bf16[2048,256]{1,0:T(8,128)(2,1)}, bf16[2048,256]{1,0:T(8,128)(2,1)}, u32[]{:S(2)}, u32[]{:S(2)}) collective-permute-start(bf16[2048,256]{1,0:T(8,128)(2,1)} %collective-permute-done.8.refs_1_), channel_id=1, source_target_pairs={{0,1},{1,0},{2,3},{3,2},{4,5},{5,4},{6,7},{7,6},{8,9},{9,8},{10,11... | collective-permute-start | bytes 3145736 | tf_op jit(solution)/shard_map/ppermute | solution.py:225
  174.6 1.9 collective-permute-start.9
  176.5 1.0 collective-permute-done.14.refs_8_
  177.5 4.2 %collective-permute-start.18 = (bf16[256,512]{1,0:T(8,128)(2,1)S(1)}, bf16[256,512]{1,0:T(8,128)(2,1)S(1)}, u32[]{:S(2)}, u32[]{:S(2)}) collective-permute-start(bf16[256,512]{1,0:T(8,128)(2,1)S(1)} %collective-permute-done.13.refs_7_), channel_id=1, source_target_pairs={{0,1},{1,0},{2,3},{3,2},{4,5},{5,4},{6,7},{7,6},{8,9},{9,8},{10,11... | collective-permute-start | bytes 786440 | tf_op jit(solution)/shard_map/ppermute | solution.py:225
  181.7 1.1 collective-permute-done.18.refs_12_
  182.8 0.7 copy-done.4
  183.5 2.3 collective-permute-start.16
  185.8 2.0 collective-permute-start.17
  188.0 2.5 collective-permute-start.19
  190.7 1.6 copy-done.1
  192.3 13.3 %near_experts.1 = (bf16[320,4096]{1,0:T(8,128)(2,1)}, bf16[6,320,128]{2,1,0:T(8,128)(2,1)S(1)}) custom-call(bf16[640,4096]{1,0:T(8,128)(2,1)} %all-gather.5.cloned.1.call-done.all_ref, bf16[320,640]{1,0:T(8,128)(2,1)S(1)} %fusion.10.take_ref, bf16[4096,256]{1,0:T(8,128)(2,1)S(1)} %bitcast.101, bf16[4096,256]{1,0:T(8,128)(2,1)} %collective-permute-done.2.refs_1_, ...), custom_call_target="tpu_custom_call" | custom-call | tf_op jit(solution)/shard_map/near_experts/pallas_call | solution.py:182
  205.6 15.4 %far_experts.1 = bf16[640,4096]{1,0:T(8,128)(2,1)} custom-call(s32[8]{0:T(128)S(1)} %fusion.69.order_ref, bf16[320,4096]{1,0:T(8,128)(2,1)} %get-tuple-element.17.rows_ref, bf16[6,320,128]{2,1,0:T(8,128)(2,1)S(1)} %get-tuple-element.18.active_ref, bf16[640,320]{1,0:T(8,128)(2,1)S(1)} %fusion.9.put_ref, ...), custom_call_target="tpu_custom_call" | custom-call | tf_op jit(solution)/shard_map/far_experts/pallas_call | solution.py:198
  221.7 71.1 %reduce-scatter.2.cloned.1.call-done = bf16[40,4096]{1,0:T(8,128)(2,1)} async-done(((bf16[640,4096]{1,0:T(8,128)(2,1)}), bf16[40,4096]{1,0:T(8,128)(2,1)}) %reduce-scatter.2.cloned.1.call-update) | async-done | bytes 327696 | tf_op jit(solution)/shard_map/reduce_scatter | solution.py:351
  292.8 1.1 copy.46
  293.9 1.0 copy.39
  294.9 16.7 %all-to-all-start.2 = ((bf16[32,10,512]{2,1,0:T(8,128)(2,1)}), bf16[32,10,512]{2,1,0:T(8,128)(2,1)S(1)}, u32[]{:S(2)}, u32[]{:S(2)}) async-start(bf16[32,10,512]{2,1,0:T(8,128)(2,1)} %copy.39), calls=%async_computation.3 | async-start | bytes 1048576 | tf_op jit(solution)/shard_map/all_to_all | solution.py:353
  311.6 11.6 %all-to-all-done.2 = bf16[32,10,512]{2,1,0:T(8,128)(2,1)S(1)} async-done(((bf16[32,10,512]{2,1,0:T(8,128)(2,1)}), bf16[32,10,512]{2,1,0:T(8,128)(2,1)S(1)}, u32[]{:S(2)}, u32[]{:S(2)}) %all-to-all-start.2) | async-done | bytes 327712 | tf_op jit(solution)/shard_map/all_to_all | solution.py:353
  323.6 0.9 fusion.8
  (119 shorter events, 7.3 us)
Async XLA Ops:
  6.5 19.4 %copy-start = (bf16[128,16,256]{2,1,0:T(8,128)(2,1)S(1)}, bf16[128,16,256]{2,1,0:T(8,128)(2,1)}, u32[]{:S(2)}) copy-start(bf16[128,16,256]{2,1,0:T(8,128)(2,1)} %param.15) | copy-start | bytes 3145732
  6.5 2.2 copy-start.13
  6.5 2.3 copy-start.14
  6.5 57.2 %all-gather.3.cloned.1.call-start = ((), (), s32[]{:S(2)}) async-start(), calls=%async_computation.4 | async-start | bytes 4718592 | tf_op jit(solution)/shard_map/all_gather | solution.py:267
  8.7 11.2 %copy-start.20 = (s32[64]{0:T(128)S(1)}, s32[64]{0:T(128)}, u32[]{:S(2)}) copy-start(s32[64]{0:T(128)} %param.23) | copy-start | bytes 772
  8.7 13.7 %copy-start.12 = (bf16[128,512]{1,0:T(8,128)(2,1)S(1)}, bf16[128,512]{1,0:T(8,128)(2,1)}, u32[]{:S(2)}) copy-start(bf16[128,512]{1,0:T(8,128)(2,1)} %param.16) | copy-start | bytes 393220
  8.7 15.7 %copy-start.18 = (s32[256]{0:T(256)S(1)}, s32[256]{0:T(256)}, u32[]{:S(2)}) copy-start(s32[256]{0:T(256)} %param.21) | copy-start | bytes 3076
  8.7 15.8 %copy-start.19 = (s32[256]{0:T(256)S(1)}, s32[256]{0:T(256)}, u32[]{:S(2)}) copy-start(s32[256]{0:T(256)} %param.20) | copy-start | bytes 3076
  8.7 16.4 %copy-start.21 = (s32[1,128]{1,0:T(1,128)S(1)}, s32[1,128]{1,0:T(1,128)}, u32[]{:S(2)}) copy-start(s32[1,128]{1,0:T(1,128)} %param.22) | copy-start | bytes 1540
  9.6 17.1 %copy-start.15 = (s32[128,2]{0,1:T(2,128)S(1)}, s32[128,2]{0,1:T(2,128)}, u32[]{:S(2)}) copy-start(s32[128,2]{0,1:T(2,128)} %param.24) | copy-start | bytes 3076
  9.6 17.5 %all-to-all-start = ((bf16[16,8,768]{2,0,1:T(8,128)(2,1)}), bf16[16,8,768]{2,0,1:T(8,128)(2,1)S(1)}, u32[]{:S(2)}, u32[]{:S(2)}) async-start(bf16[16,8,768]{2,0,1:T(8,128)(2,1)} %copy.33), calls=%async_computation | async-start | bytes 393216 | tf_op jit(solution)/shard_map/all_to_all | solution.py:272
  19.9 170.8 %all-gather.5.cloned.1.call-start = ((), (), s32[]{:S(2)}) async-start(), calls=%async_computation.5 | async-start | bytes 5570560 | tf_op jit(solution)/shard_map/all_gather | solution.py:326
  22.5 11.3 %collective-permute-start = (bf16[32,512]{1,0:T(8,128)(2,1)S(1)}, bf16[32,512]{1,0:T(8,128)(2,1)S(1)}, u32[]{:S(2)}, u32[]{:S(2)}) collective-permute-start(bf16[32,512]{1,0:T(8,128)(2,1)S(1)} %dynamic-slice_bitcast_fusion), channel_id=1, source_target_pairs={{0,8},{8,16},{16,24},{24,32},{32,40},{40,48},{48,56},{56,64},{64,7... | collective-permute-start | bytes 98312 | tf_op jit(solution)/shard_map/ppermute | solution.py:275
  28.9 12.7 %copy-start.17 = (f32[512]{0:T(512)S(1)}, f32[512]{0:T(512)}, u32[]{:S(2)}) copy-start(f32[512]{0:T(512)} %param.17) | copy-start | bytes 6148
  30.8 10.8 %collective-permute-start.1 = (bf16[32,512]{1,0:T(8,128)(2,1)S(1)}, bf16[32,512]{1,0:T(8,128)(2,1)S(1)}, u32[]{:S(2)}, u32[]{:S(2)}) collective-permute-start(bf16[32,512]{1,0:T(8,128)(2,1)S(1)} %fusion.45), channel_id=1, source_target_pairs={{0,8},{8,16},{16,24},{24,32},{32,40},{40,48},{48,56},{56,64},{64,7... | collective-permute-start | bytes 98312 | tf_op jit(solution)/shard_map/ppermute | solution.py:289
  41.8 0.7 copy-start.7
  41.8 0.8 copy-start.9
  63.8 229.1 %reduce-scatter.2.cloned.1.call-start = ((), (), s32[]{:S(2)}) async-start(), calls=%async_computation.6 | async-start | bytes 5570560 | tf_op jit(solution)/shard_map/reduce_scatter | solution.py:351
  63.8 50.8 %collective-permute-start.2 = (bf16[4096,256]{1,0:T(8,128)(2,1)}, bf16[4096,256]{1,0:T(8,128)(2,1)}, u32[]{:S(2)}, u32[]{:S(2)}) collective-permute-start(bf16[4096,256]{1,0:T(8,128)(2,1)} %bitcast.98), channel_id=1, source_target_pairs={{0,2},{2,4},{4,6},{6,0},{1,3},{3,5},{5,7},{7,1},{8,10},{10,12},{12... | collective-permute-start | bytes 6291464 | tf_op jit(solution)/shard_map/ppermute | solution.py:221
  65.8 49.9 %collective-permute-start.3 = (bf16[4096,256]{1,0:T(8,128)(2,1)}, bf16[4096,256]{1,0:T(8,128)(2,1)}, u32[]{:S(2)}, u32[]{:S(2)}) collective-permute-start(bf16[4096,256]{1,0:T(8,128)(2,1)} %bitcast.99), channel_id=1, source_target_pairs={{0,6},{2,0},{4,2},{6,4},{1,7},{3,1},{5,3},{7,5},{8,14},{10,8},{12,... | collective-permute-start | bytes 6291464 | tf_op jit(solution)/shard_map/ppermute | solution.py:221
  70.4 59.8 %collective-permute-start.4 = (bf16[4096,256]{1,0:T(8,128)(2,1)}, bf16[4096,256]{1,0:T(8,128)(2,1)S(1)}, u32[]{:S(2)}, u32[]{:S(2)}) collective-permute-start(bf16[4096,256]{1,0:T(8,128)(2,1)} %bitcast.100), channel_id=1, source_target_pairs={{0,1},{1,0},{2,3},{3,2},{4,5},{5,4},{6,7},{7,6},{8,9},{9,8},{10,11... | collective-permute-start | bytes 6291464 | tf_op jit(solution)/shard_map/ppermute | solution.py:225
  115.6 70.2 %collective-permute-start.5 = (bf16[4096,256]{1,0:T(8,128)(2,1)}, bf16[4096,256]{1,0:T(8,128)(2,1)}, u32[]{:S(2)}, u32[]{:S(2)}) collective-permute-start(bf16[4096,256]{1,0:T(8,128)(2,1)} %collective-permute-done.2.refs_1_), channel_id=1, source_target_pairs={{0,1},{1,0},{2,3},{3,2},{4,5},{5,4},{6,7},{7,6},{8,9},{9,8},{10,11... | collective-permute-start | bytes 6291464 | tf_op jit(solution)/shard_map/ppermute | solution.py:225
  118.4 17.7 %collective-permute-start.11 = (bf16[512,512]{1,0:T(8,128)(2,1)S(1)}, bf16[512,512]{1,0:T(8,128)(2,1)S(1)}, u32[]{:S(2)}, u32[]{:S(2)}) collective-permute-start(bf16[512,512]{1,0:T(8,128)(2,1)S(1)} %get-tuple-element.20.refs_4_), channel_id=1, source_target_pairs={{0,2},{2,4},{4,6},{6,0},{1,3},{3,5},{5,7},{7,1},{8,10},{10,12},{12... | collective-permute-start | bytes 1572872 | tf_op jit(solution)/shard_map/ppermute | solution.py:221
  120.3 67.7 %collective-permute-start.6 = (bf16[4096,256]{1,0:T(8,128)(2,1)}, bf16[4096,256]{1,0:T(8,128)(2,1)}, u32[]{:S(2)}, u32[]{:S(2)}) collective-permute-start(bf16[4096,256]{1,0:T(8,128)(2,1)} %collective-permute-done.3.refs_2_), channel_id=1, source_target_pairs={{0,1},{1,0},{2,3},{3,2},{4,5},{5,4},{6,7},{7,6},{8,9},{9,8},{10,11... | collective-permute-start | bytes 6291464 | tf_op jit(solution)/shard_map/ppermute | solution.py:225
  122.5 15.8 %collective-permute-start.12 = (bf16[512,512]{1,0:T(8,128)(2,1)S(1)}, bf16[512,512]{1,0:T(8,128)(2,1)S(1)}, u32[]{:S(2)}, u32[]{:S(2)}) collective-permute-start(bf16[512,512]{1,0:T(8,128)(2,1)S(1)} %get-tuple-element.20.refs_4_), channel_id=1, source_target_pairs={{0,6},{2,0},{4,2},{6,4},{1,7},{3,1},{5,3},{7,5},{8,14},{10,8},{12,... | collective-permute-start | bytes 1572872 | tf_op jit(solution)/shard_map/ppermute | solution.py:221
  130.2 46.3 %copy-start.6 = (bf16[4096,256]{1,0:T(8,128)(2,1)}, bf16[4096,256]{1,0:T(8,128)(2,1)S(1)}, u32[]{:S(2)}) copy-start(bf16[4096,256]{1,0:T(8,128)(2,1)S(1)} %collective-permute-done.4.refs_3_) | copy-start | bytes 6291460
  130.2 40.8 %collective-permute-start.8 = (bf16[2048,256]{1,0:T(8,128)(2,1)S(1)}, bf16[2048,256]{1,0:T(8,128)(2,1)}, u32[]{:S(2)}, u32[]{:S(2)}) collective-permute-start(bf16[2048,256]{1,0:T(8,128)(2,1)S(1)} %slice.62), channel_id=1, source_target_pairs={{0,6},{2,0},{4,2},{6,4},{1,7},{3,1},{5,3},{7,5},{8,14},{10,8},{12,... | collective-permute-start | bytes 3145736 | tf_op jit(solution)/shard_map/ppermute | solution.py:221
  136.1 38.4 %collective-permute-start.7 = (bf16[2048,256]{1,0:T(8,128)(2,1)S(1)}, bf16[2048,256]{1,0:T(8,128)(2,1)}, u32[]{:S(2)}, u32[]{:S(2)}) collective-permute-start(bf16[2048,256]{1,0:T(8,128)(2,1)S(1)} %slice.61), channel_id=1, source_target_pairs={{0,2},{2,4},{4,6},{6,0},{1,3},{3,5},{5,7},{7,1},{8,10},{10,12},{12... | collective-permute-start | bytes 3145736 | tf_op jit(solution)/shard_map/ppermute | solution.py:221
  138.4 5.7 %collective-permute-start.15 = (bf16[512,512]{1,0:T(8,128)(2,1)S(1)}, bf16[512,512]{1,0:T(8,128)(2,1)S(1)}, u32[]{:S(2)}, u32[]{:S(2)}) collective-permute-start(bf16[512,512]{1,0:T(8,128)(2,1)S(1)} %get-tuple-element.20.refs_4_), channel_id=1, source_target_pairs={{0,1},{1,0},{2,3},{3,2},{4,5},{5,4},{6,7},{7,6},{8,9},{9,8},{10,11... | collective-permute-start | bytes 1572872 | tf_op jit(solution)/shard_map/ppermute | solution.py:225
  144.1 33.4 %copy-start.11 = (bf16[512,512]{1,0:T(8,128)(2,1)}, bf16[512,512]{1,0:T(8,128)(2,1)S(1)}, u32[]{:S(2)}) copy-start(bf16[512,512]{1,0:T(8,128)(2,1)S(1)} %collective-permute-done.15.refs_9_) | copy-start | bytes 1572868
  144.1 25.0 %collective-permute-start.13 = (bf16[256,512]{1,0:T(8,128)(2,1)S(1)}, bf16[256,512]{1,0:T(8,128)(2,1)S(1)}, u32[]{:S(2)}, u32[]{:S(2)}) collective-permute-start(bf16[256,512]{1,0:T(8,128)(2,1)S(1)} %slice.74), channel_id=1, source_target_pairs={{0,2},{2,4},{4,6},{6,0},{1,3},{3,5},{5,7},{7,1},{8,10},{10,12},{12... | collective-permute-start | bytes 786440 | tf_op jit(solution)/shard_map/ppermute | solution.py:221
  169.1 21.4 %copy-start.2 = (bf16[256,512]{1,0:T(8,128)(2,1)}, bf16[256,512]{1,0:T(8,128)(2,1)S(1)}, u32[]{:S(2)}) copy-start(bf16[256,512]{1,0:T(8,128)(2,1)S(1)} %collective-permute-done.13.refs_7_) | copy-start | bytes 786436
  169.1 8.5 %collective-permute-start.14 = (bf16[256,512]{1,0:T(8,128)(2,1)S(1)}, bf16[256,512]{1,0:T(8,128)(2,1)}, u32[]{:S(2)}, u32[]{:S(2)}) collective-permute-start(bf16[256,512]{1,0:T(8,128)(2,1)S(1)} %slice.75), channel_id=1, source_target_pairs={{0,6},{2,0},{4,2},{6,4},{1,7},{3,1},{5,3},{7,5},{8,14},{10,8},{12,... | collective-permute-start | bytes 786440 | tf_op jit(solution)/shard_map/ppermute | solution.py:221
  171.0 34.6 %collective-permute-start.10 = (bf16[2048,256]{1,0:T(8,128)(2,1)}, bf16[2048,256]{1,0:T(8,128)(2,1)}, u32[]{:S(2)}, u32[]{:S(2)}) collective-permute-start(bf16[2048,256]{1,0:T(8,128)(2,1)} %collective-permute-done.8.refs_1_), channel_id=1, source_target_pairs={{0,1},{1,0},{2,3},{3,2},{4,5},{5,4},{6,7},{7,6},{8,9},{9,8},{10,11... | collective-permute-start | bytes 3145736 | tf_op jit(solution)/shard_map/ppermute | solution.py:225
  174.6 31.1 %collective-permute-start.9 = (bf16[2048,256]{1,0:T(8,128)(2,1)}, bf16[2048,256]{1,0:T(8,128)(2,1)}, u32[]{:S(2)}, u32[]{:S(2)}) collective-permute-start(bf16[2048,256]{1,0:T(8,128)(2,1)} %collective-permute-done.7.refs_0_), channel_id=1, source_target_pairs={{0,1},{1,0},{2,3},{3,2},{4,5},{5,4},{6,7},{7,6},{8,9},{9,8},{10,11... | collective-permute-start | bytes 3145736 | tf_op jit(solution)/shard_map/ppermute | solution.py:225
  177.5 5.3 %collective-permute-start.18 = (bf16[256,512]{1,0:T(8,128)(2,1)S(1)}, bf16[256,512]{1,0:T(8,128)(2,1)S(1)}, u32[]{:S(2)}, u32[]{:S(2)}) collective-permute-start(bf16[256,512]{1,0:T(8,128)(2,1)S(1)} %collective-permute-done.13.refs_7_), channel_id=1, source_target_pairs={{0,1},{1,0},{2,3},{3,2},{4,5},{5,4},{6,7},{7,6},{8,9},{9,8},{10,11... | collective-permute-start | bytes 786440 | tf_op jit(solution)/shard_map/ppermute | solution.py:225
  182.8 0.7 copy-start.4
  183.5 22.0 %collective-permute-start.16 = (bf16[512,512]{1,0:T(8,128)(2,1)S(1)}, bf16[512,512]{1,0:T(8,128)(2,1)}, u32[]{:S(2)}, u32[]{:S(2)}) collective-permute-start(bf16[512,512]{1,0:T(8,128)(2,1)S(1)} %collective-permute-done.11.refs_5_), channel_id=1, source_target_pairs={{0,1},{1,0},{2,3},{3,2},{4,5},{5,4},{6,7},{7,6},{8,9},{9,8},{10,11... | collective-permute-start | bytes 1572872 | tf_op jit(solution)/shard_map/ppermute | solution.py:225
  185.8 19.8 %collective-permute-start.17 = (bf16[512,512]{1,0:T(8,128)(2,1)S(1)}, bf16[512,512]{1,0:T(8,128)(2,1)}, u32[]{:S(2)}, u32[]{:S(2)}) collective-permute-start(bf16[512,512]{1,0:T(8,128)(2,1)S(1)} %collective-permute-done.12.refs_6_), channel_id=1, source_target_pairs={{0,1},{1,0},{2,3},{3,2},{4,5},{5,4},{6,7},{7,6},{8,9},{9,8},{10,11... | collective-permute-start | bytes 1572872 | tf_op jit(solution)/shard_map/ppermute | solution.py:225
  188.0 17.6 %collective-permute-start.19 = (bf16[256,512]{1,0:T(8,128)(2,1)}, bf16[256,512]{1,0:T(8,128)(2,1)}, u32[]{:S(2)}, u32[]{:S(2)}) collective-permute-start(bf16[256,512]{1,0:T(8,128)(2,1)} %collective-permute-done.14.refs_8_), channel_id=1, source_target_pairs={{0,1},{1,0},{2,3},{3,2},{4,5},{5,4},{6,7},{7,6},{8,9},{9,8},{10,11... | collective-permute-start | bytes 786440 | tf_op jit(solution)/shard_map/ppermute | solution.py:225
  190.7 1.6 copy-start.1
  192.3 13.3 %copy-start.3 = (bf16[256,512]{1,0:T(8,128)(2,1)S(1)}, bf16[256,512]{1,0:T(8,128)(2,1)}, u32[]{:S(2)}) copy-start(bf16[256,512]{1,0:T(8,128)(2,1)} %copy-done.2) | copy-start | bytes 786436
  192.3 13.3 %copy-start.5 = (bf16[256,512]{1,0:T(8,128)(2,1)S(1)}, bf16[256,512]{1,0:T(8,128)(2,1)}, u32[]{:S(2)}) copy-start(bf16[256,512]{1,0:T(8,128)(2,1)} %copy-done.4) | copy-start | bytes 786436
  221.0 0.7 copy-start.16
  294.9 28.7 %copy-start.8 = (bf16[128,512]{1,0:T(8,128)(2,1)S(1)}, bf16[128,512]{1,0:T(8,128)(2,1)}, u32[]{:S(2)}) copy-start(bf16[128,512]{1,0:T(8,128)(2,1)} %copy-done.7) | copy-start | bytes 393220
  294.9 28.7 %copy-start.10 = (bf16[128,512]{1,0:T(8,128)(2,1)S(1)}, bf16[128,512]{1,0:T(8,128)(2,1)}, u32[]{:S(2)}) copy-start(bf16[128,512]{1,0:T(8,128)(2,1)} %copy-done.9) | copy-start | bytes 393220
  294.9 28.3 %all-to-all-start.2 = ((bf16[32,10,512]{2,1,0:T(8,128)(2,1)}), bf16[32,10,512]{2,1,0:T(8,128)(2,1)S(1)}, u32[]{:S(2)}, u32[]{:S(2)}) async-start(bf16[32,10,512]{2,1,0:T(8,128)(2,1)} %copy.39), calls=%async_computation.3 | async-start | bytes 1048576 | tf_op jit(solution)/shard_map/all_to_all | solution.py:353
Sparse Core Ops, SparseCore 0:
  9.5 46.8 all-gather.2
  63.9 74.3 all-gather.4
  221.2 71.6 reduce-scatter.1

commit v5 on v3

--- a/solution.py
+++ b/solution.py
@@ -91,60 +91,63 @@
 
 
 CHUNKS = 4
+HALF = D // 2
 
 
 def expert_kernel(order_ref, all_ref, take_ref, put_ref, *refs):
-    in_refs, down_hbm = refs[:14], refs[14]
-    out_ref, gathered, rows, in_buf, down_buf, active, whole, sems = refs[15:]
+    in_refs, down_refs = refs[:10], refs[10:12]
+    out_ref, gathered, rows, in_buf, down_buf, active, whole, sems = refs[12:]
     width = D // CHUNKS
-    half = D // 2
-    count = iter(range(30))
+    numbers = iter(range(sems.shape[0]))
 
     def begin(source, target):
-        copy = pltpu.make_async_copy(source, target, sems.at[next(count)])
+        copy = pltpu.make_async_copy(source, target, sems.at[next(numbers)])
         copy.start()
         return copy
 
     parts = [
         begin(all_ref.at[:, pl.ds(n * width, width)], gathered.at[n]) for n in range(CHUNKS)
     ]
-    loads = []
+    loads = [None] * N_TP
     for core in range(NC):
-        for k in range(NY):
-            chunk, first = in_buf.at[core * NY + k], core * 7 + 2 * k
-            if k == 0:
-                loads.append([begin(in_refs[first], chunk)])
-            else:
-                loads.append(
-                    [
-                        begin(in_refs[first - 1], chunk.at[pl.ds(0, half)]),
-                        begin(in_refs[first], chunk.at[pl.ds(half, half)]),
-                    ]
-                )
-    downs = [begin(down_hbm.at[t], down_buf.at[t]) for t in range(N_TP)]
+        for k in range(3):
+            slot = core * NY + k
+            loads[slot] = [begin(in_refs[core * 5 + k], in_buf.at[slot])]
+    for core in range(NC):
+        chunk = in_buf.at[core * NY + 3]
+        loads[core * NY + 3] = [
+            begin(in_refs[core * 5 + 3 + i], chunk.at[pl.ds(i * HALF, HALF)]) for i in range(2)
+        ]
+    downs = [
+        begin(down_refs[core].at[k], down_buf.at[core * NY + k])
+        for core in range(NC)
+        for k in range(NY)
+    ]
     for n in range(CHUNKS):
         parts[n].wait()
         rows[:, n * width : (n + 1) * width] = jnp.dot(
             take_ref[...], gathered[n], preferred_element_type=jnp.float32
         ).astype(jnp.bfloat16)
-    for k in range(N_TP):
-        for copy in loads[k]:
+    for slot in (0, 1, 2, 4, 5, 6, 3, 7):
+        for copy in loads[slot]:
             copy.wait()
-        both = jnp.dot(rows[...], in_buf[k], preferred_element_type=jnp.float32)
+        both = jnp.dot(rows[...], in_buf[slot], preferred_element_type=jnp.float32)
         gate = both[:, :128]
-        active[order_ref[k]] = (gate / (1.0 + jnp.exp(-gate)) * both[:, 128:]).astype(jnp.bfloat16)
+        active[order_ref[slot]] = (gate / (1.0 + jnp.exp(-gate)) * both[:, 128:]).astype(
+            jnp.bfloat16
+        )
     for t in range(N_TP):
         whole[:, t * 128 : (t + 1) * 128] = active[t]
     outs = []
-    for t in range(N_TP):
-        downs[t].wait()
-        part = jnp.dot(whole[...], down_buf[t], preferred_element_type=jnp.float32)
-        n, lane = t // 2, t % 2 * 512
-        gathered[n, :, lane : lane + 512] = jnp.dot(
+    for slot in range(N_TP):
+        downs[slot].wait()
+        part = jnp.dot(whole[...], down_buf[slot], preferred_element_type=jnp.float32)
+        place = gathered.at[slot // 2, :, pl.ds(slot % 2 * 512, 512)]
+        place[...] = jnp.dot(
             put_ref[...], part.astype(jnp.bfloat16), preferred_element_type=jnp.float32
         ).astype(jnp.bfloat16)
-        if t % 2:
-            outs.append(begin(gathered.at[n], out_ref.at[:, pl.ds(n * width, width)]))
+        lanes = pl.ds(pl.multiple_of(order_ref[N_TP + slot] * 512, 512), 512)
+        outs.append(begin(place, out_ref.at[:, lanes]))
     for copy in outs:
         copy.wait()
 
@@ -155,7 +158,7 @@
     return pl.pallas_call(
         expert_kernel,
         out_shape=jax.ShapeDtypeStruct((ALL_ROWS, D), jnp.bfloat16),
-        in_specs=[pl.BlockSpec(memory_space=pltpu.SMEM), far, local, local] + [far] * 15,
+        in_specs=[pl.BlockSpec(memory_space=pltpu.SMEM), far, local, local] + [far] * 12,
         out_specs=far,
         scratch_shapes=[
             pltpu.VMEM((CHUNKS, ALL_ROWS, D // CHUNKS), jnp.bfloat16),
@@ -164,11 +167,11 @@
             pltpu.VMEM((N_TP, 1024, 512), jnp.bfloat16),
             pltpu.VMEM((N_TP, OWN_ROWS, 128), jnp.bfloat16),
             pltpu.VMEM((OWN_ROWS, 1024), jnp.bfloat16),
-            pltpu.SemaphoreType.DMA((30,)),
+            pltpu.SemaphoreType.DMA((CHUNKS + 10 + 2 * N_TP,)),
         ],
-        compiler_params=pltpu.CompilerParams(vmem_limit_bytes=46 << 20),
+        compiler_params=pltpu.CompilerParams(vmem_limit_bytes=50 << 20),
         name="experts",
-    )(order, all_rows, take, put, *weights_in, weights_down)
+    )(order, all_rows, take, put, *weights_in, *weights_down)
 
 
 def by_y(value, step):
@@ -179,13 +182,7 @@
     return lax.ppermute(value, "c", [(0, 1), (1, 0)])
 
 
-def gather_pieces(own):
-    half = own.shape[0] // 2
-    top, bottom = own[:half], own[half:]
-    below_top, above_bottom = by_y(top, 1), by_y(bottom, -1)
-    below_bottom, above_top = by_y(bottom, 1), by_y(top, -1)
-    far_top, far_bottom = by_y(below_top, 1), by_y(above_bottom, -1)
-    pieces = [own, below_top, below_bottom, above_top, above_bottom, far_top, far_bottom]
+def both_cores(pieces):
     return pieces + [other_core(piece) for piece in pieces]
 
 
@@ -219,7 +216,7 @@
     handing = [(i, (i + 1) % N_REP) for i in range(N_REP)]
 
     in_own = gate_up[0]
-    weights_down = lax.all_gather(down_proj[0], TP)
+    down_mine = lax.all_gather(down_proj[0], "y")
     mixed = jnp.concatenate(
         [queries.reshape(-1, N_TP, 512), fresh_kv.reshape(-1, N_TP, 256)], axis=2
     )
@@ -275,15 +272,22 @@
     )
     packed = jnp.dot(placing, payload, preferred_element_type=jnp.float32).astype(jnp.bfloat16)
     received = lax.all_to_all(packed.reshape(NX * N_TP, PIECE, WIDE), SPREAD, 0, 0)
+    received, in_own = lax.optimization_barrier((received, in_own))
+    in_below, in_above = by_y(in_own, 1), by_y(in_own, -1)
     normed = norm_rows(received.reshape(NX * N_TP, PIECE, WIDE))
-    normed, in_own, weights_down = lax.optimization_barrier((normed, in_own, weights_down))
     all_rows = lax.all_gather(normed, "z", tiled=True)
-    weights_in = gather_pieces(in_own)
+    in_below, in_above, in_own, down_mine = lax.optimization_barrier(
+        (in_below, in_above, in_own, down_mine)
+    )
+    weights_down = both_cores([down_mine])
+    far_in = [by_y(in_below[:HALF], 1), by_y(in_above[HALF:], -1)]
+    weights_in = both_cores([in_own, in_below, in_above] + far_in)
     my_y, my_core = lax.axis_index("y"), lax.axis_index("c")
-    piece = jnp.arange(N_TP, dtype=jnp.int32)
-    step = piece % 4
+    piece = jnp.arange(2 * N_TP, dtype=jnp.int32)
+    step = piece % NY
     step = jnp.where(step == 1, NY - 1, jnp.where(step == 2, 1, jnp.where(step == 3, 2, 0)))
-    order = (my_y + step) % NY * NC + (my_core + piece // 4) % NC
+    place_y = jnp.where(piece < N_TP, (my_y + step) % NY, piece % NY)
+    order = place_y * NC + (my_core + piece // NY) % NC
 
     index = jnp.arange(ALL_ROWS, dtype=jnp.int32)
     own = (index // SHARE) % 2 == my_z // 8

time: 308 us -> 307 us (level)
  waiting for transfers between devices: 158 us -> 169 us
  starting transfers between devices: 67.5 us -> 57 us
    ppermute x6 -> x4, waiting for transfers between devices: 44.2 us -> 71.5 us  [by_y(): return lax.ppermute(value, 'y', [(i, (i + step) % NY) for i in range(NY)])]
    all_gather x1, waiting for transfers between devices: 17.3 us -> 0.01 us  [per_device(): down_mine = lax.all_gather(down_proj[0], 'y')]
    ppermute x6 -> x4, starting transfers between devices: 19.5 us -> 11.8 us  [by_y(): return lax.ppermute(value, 'y', [(i, (i + step) % NY) for i in range(NY)])]
    ppermute x7 -> x6, starting transfers between devices: 17.3 us -> 14.3 us  [other_core(): return lax.ppermute(value, 'c', [(0, 1), (1, 0)])]
    unnamed x32 -> x26, local copies, waits for them, and re-layouts: 6.42 us -> 4.24 us
  transfers between devices with their start and end apart: 20 -> 17, of which waited for: 8 -> 8; matrix products, arithmetic and copies ran while one was open for 4% -> 4% of each run, Pallas kernels for 1% -> 1%
where the time goes in v5:
time: 307 us; the launch traced here: 306 us
  waiting for transfers between devices  169 us (55%)
  starting transfers between devices  57 us (19%)
  Pallas kernels  27.8 us (9%)
  blocking collectives  18.5 us (6%)
  between operations  15.5 us (5%)
  local copies, waits for them, and re-layouts  11 us (4%)
  matrix products  5.08 us (2%)
    reduce_scatter x1, waiting for transfers between devices, per_device(): lax.psum_scatter(partial_rows, 'z', scatter_dimension=0, tiled=True)  74.6 us
    ppermute x4, waiting for transfers between devices, by_y(): return lax.ppermute(value, 'y', [(i, (i + step) % NY) for i in range(NY)])  71.5 us
    pallas_call x1, Pallas kernels, run_experts(): pl.pallas_call(expert_kernel, out_shape=jax.ShapeDtypeStruct((ALL_ROWS, D...  25.7 us
    all_to_all x1, blocking collectives, per_device(): lax.all_to_all(packed.reshape(NX * N_TP, PIECE, WIDE), SPREAD, 0, 0)  18.5 us
    all_to_all x1, starting transfers between devices, per_device(): returned = lax.all_to_all(back.reshape(NX * N_TP, PIECE, 512), SPREAD, 0, 0)  16.7 us
    ppermute x6, starting transfers between devices, other_core(): return lax.ppermute(value, 'c', [(0, 1), (1, 0)])  14.3 us
    ppermute x4, starting transfers between devices, by_y(): return lax.ppermute(value, 'y', [(i, (i + step) % NY) for i in range(NY)])  11.8 us
    all_to_all x1, waiting for transfers between devices, per_device(): returned = lax.all_to_all(back.reshape(NX * N_TP, PIECE, 512), SPREAD, 0, 0)  11.6 us
  transfers between devices with their start and end apart: 17, of which 8 were waited for; matrix products, arithmetic and copies ran while one was open for 4% of the time, Pallas kernels for 1%

profile of v5, /device:TPU:1, one launch (start us, length us, event | category | flops | bytes accessed | tf_op | source)
XLA Modules:
  0.0 306.3 jit_solution(16789657813904287496)
XLA Ops:
  6.6 0.7 all-gather.5.cloned.1.call-update
  7.3 0.9 copy.43
  8.3 0.7 copy.33
  9.0 10.3 %all-to-all-start = ((bf16[16,8,768]{2,0,1:T(8,128)(2,1)}), bf16[16,8,768]{2,0,1:T(8,128)(2,1)S(1)}, u32[]{:S(2)}, u32[]{:S(2)}) async-start(bf16[16,8,768]{2,0,1:T(8,128)(2,1)} %copy.33), calls=%async_computation | async-start | bytes 393216 | tf_op jit(solution)/shard_map/all_to_all | solution.py:223
  19.3 0.6 dynamic_slice.16
  21.9 1.9 collective-permute-start
  24.0 0.5 broadcast.384
  24.5 0.6 reduce.3
  25.4 0.6 gather_fusion
  26.1 0.1 fusion.44
  26.6 1.8 fusion.86
  28.4 1.7 fusion.11
  30.2 1.9 collective-permute-start.1
  32.1 0.7 iota_compare_fusion.17
  33.2 7.8 %collective-permute-done.1 = bf16[32,512]{1,0:T(8,128)(2,1)S(1)} collective-permute-done((bf16[32,512]{1,0:T(8,128)(2,1)S(1)}, bf16[32,512]{1,0:T(8,128)(2,1)S(1)}, u32[]{:S(2)}, u32[]{:S(2)}) %collective-permute-start.1) | collective-permute-done | bytes 32800 | tf_op jit(solution)/shard_map/ppermute | solution.py:240
  41.0 0.2 multiply_convert_fusion
  41.4 0.1 copy.37
  41.5 0.3 convolution_convert_fusion
  41.8 0.1 reshape.317
  41.9 18.5 %all_to_all.25.recv_ref = bf16[32,10,640]{2,1,0:T(8,128)(2,1)} all-to-all(bf16[32,10,640]{2,1,0:T(8,128)(2,1)S(1)} %reshape.317), channel_id=1, replica_groups=mesh['x'=4,'z'=16,'y'=4,'c'=2] {'x','y','c'}, dimensions={0} | all-to-all | bytes 819200 | tf_op jit(solution)/shard_map/all_to_all | solution.py:274
  60.5 2.0 norm_rows.1
  62.6 1.9 collective-permute-start.2
  64.5 4.6 %collective-permute-start.3 = (bf16[4096,256]{1,0:T(8,128)(2,1)}, bf16[4096,256]{1,0:T(8,128)(2,1)}, u32[]{:S(2)}, u32[]{:S(2)}) collective-permute-start(bf16[4096,256]{1,0:T(8,128)(2,1)} %bitcast.24.refs_0_), channel_id=1, source_target_pairs={{0,6},{2,0},{4,2},{6,4},{1,7},{3,1},{5,3},{7,5},{8,14},{10,8},{12,... | collective-permute-start | bytes 6291464 | tf_op jit(solution)/shard_map/ppermute | solution.py:178
  69.1 53.6 %collective-permute-done.2.refs_1_ = bf16[4096,256]{1,0:T(8,128)(2,1)} collective-permute-done((bf16[4096,256]{1,0:T(8,128)(2,1)}, bf16[4096,256]{1,0:T(8,128)(2,1)}, u32[]{:S(2)}, u32[]{:S(2)}) %collective-permute-start.2) | collective-permute-done | bytes 2097184 | tf_op jit(solution)/shard_map/ppermute | solution.py:178
  122.7 2.4 collective-permute-start.11
  125.1 1.3 slice.48
  126.4 2.5 collective-permute-start.5
  128.9 1.3 slice.47
  130.2 2.8 collective-permute-start.4
  133.0 2.5 collective-permute-start.7
  135.5 17.7 %collective-permute-done.5.refs_4_ = bf16[2048,256]{1,0:T(8,128)(2,1)S(1)} collective-permute-done((bf16[2048,256]{1,0:T(8,128)(2,1)S(1)}, bf16[2048,256]{1,0:T(8,128)(2,1)S(1)}, u32[]{:S(2)}, u32[]{:S(2)}) %collective-permute-start.5) | collective-permute-done | bytes 1048608 | tf_op jit(solution)/shard_map/ppermute | solution.py:178
  153.2 2.6 collective-permute-start.10
  155.8 1.9 collective-permute-start.6
  157.7 0.2 collective-permute-done.4.refs_3_
  157.9 3.0 collective-permute-start.8
  160.9 1.0 copy-done.1
  161.9 1.9 collective-permute-start.9
  164.0 0.2 fusion.9.put_ref
  164.1 2.7 collective-permute-done.9.refs_8_
  166.9 25.7 %experts.1 = bf16[640,4096]{1,0:T(8,128)(2,1)} custom-call(s32[16]{0:T(128)S(1)} %fusion.69.order_ref, bf16[640,4096]{1,0:T(8,128)(2,1)} %all-gather.3.cloned.1.call-done.all_ref, bf16[320,640]{1,0:T(8,128)(2,1)S(1)} %fusion.10.take_ref, bf16[640,320]{1,0:T(8,128)(2,1)S(1)} %fusion.9.put_ref, bf16[4096,256]{1,0:T(8,128)(2,1)} %bitcast.24.refs_0_, ...), custom_call_target="tpu_custom_call" | custom-call | tf_op jit(solution)/shard_map/experts/pallas_call | solution.py:158
  192.7 0.6 copy-done.5
  193.4 74.6 %reduce-scatter.2.cloned.1.call-done = bf16[40,4096]{1,0:T(8,128)(2,1)} async-done(((bf16[640,4096]{1,0:T(8,128)(2,1)}), bf16[40,4096]{1,0:T(8,128)(2,1)}) %reduce-scatter.2.cloned.1.call-update) | async-done | bytes 327696 | tf_op jit(solution)/shard_map/reduce_scatter | solution.py:299
  268.0 1.1 copy.46
  269.1 1.0 copy.39
  270.1 16.7 %all-to-all-start.2 = ((bf16[32,10,512]{2,1,0:T(8,128)(2,1)}), bf16[32,10,512]{2,1,0:T(8,128)(2,1)S(1)}, u32[]{:S(2)}, u32[]{:S(2)}) async-start(bf16[32,10,512]{2,1,0:T(8,128)(2,1)} %copy.39), calls=%async_computation.3 | async-start | bytes 1048576 | tf_op jit(solution)/shard_map/all_to_all | solution.py:301
  286.8 11.6 %all-to-all-done.2 = bf16[32,10,512]{2,1,0:T(8,128)(2,1)S(1)} async-done(((bf16[32,10,512]{2,1,0:T(8,128)(2,1)}), bf16[32,10,512]{2,1,0:T(8,128)(2,1)S(1)}, u32[]{:S(2)}, u32[]{:S(2)}) %all-to-all-start.2) | async-done | bytes 327712 | tf_op jit(solution)/shard_map/all_to_all | solution.py:301
  298.5 0.3 convolution_multiply_fusion.2
  298.8 0.9 fusion.8
  (77 shorter events, 2.1 us)
Async XLA Ops:
  6.5 18.8 %copy-start = (bf16[128,16,256]{2,1,0:T(8,128)(2,1)S(1)}, bf16[128,16,256]{2,1,0:T(8,128)(2,1)}, u32[]{:S(2)}) copy-start(bf16[128,16,256]{2,1,0:T(8,128)(2,1)} %param.15) | copy-start | bytes 3145732
  6.5 1.7 copy-start.3
  6.5 12.8 %copy-start.9 = (s32[64]{0:T(128)S(1)}, s32[64]{0:T(128)}, u32[]{:S(2)}) copy-start(s32[64]{0:T(128)} %param.23) | copy-start | bytes 772
  6.5 15.3 %copy-start.2 = (bf16[128,512]{1,0:T(8,128)(2,1)S(1)}, bf16[128,512]{1,0:T(8,128)(2,1)}, u32[]{:S(2)}) copy-start(bf16[128,512]{1,0:T(8,128)(2,1)} %param.16) | copy-start | bytes 393220
  6.5 17.3 %copy-start.7 = (s32[256]{0:T(256)S(1)}, s32[256]{0:T(256)}, u32[]{:S(2)}) copy-start(s32[256]{0:T(256)} %param.21) | copy-start | bytes 3076
  6.5 17.4 %copy-start.8 = (s32[256]{0:T(256)S(1)}, s32[256]{0:T(256)}, u32[]{:S(2)}) copy-start(s32[256]{0:T(256)} %param.20) | copy-start | bytes 3076
  6.6 18.0 %copy-start.10 = (s32[1,128]{1,0:T(1,128)S(1)}, s32[1,128]{1,0:T(1,128)}, u32[]{:S(2)}) copy-start(s32[1,128]{1,0:T(1,128)} %param.22) | copy-start | bytes 1540
  6.6 116.1 %all-gather.5.cloned.1.call-start = ((), (), s32[]{:S(2)}) async-start(), calls=%async_computation.5 | async-start | bytes 5242880 | tf_op jit(solution)/shard_map/all_gather | solution.py:219
  9.0 17.1 %copy-start.4 = (s32[128,2]{0,1:T(2,128)S(1)}, s32[128,2]{0,1:T(2,128)}, u32[]{:S(2)}) copy-start(s32[128,2]{0,1:T(2,128)} %param.24) | copy-start | bytes 3076
  9.0 17.5 %all-to-all-start = ((bf16[16,8,768]{2,0,1:T(8,128)(2,1)}), bf16[16,8,768]{2,0,1:T(8,128)(2,1)S(1)}, u32[]{:S(2)}, u32[]{:S(2)}) async-start(bf16[16,8,768]{2,0,1:T(8,128)(2,1)} %copy.33), calls=%async_computation | async-start | bytes 393216 | tf_op jit(solution)/shard_map/all_to_all | solution.py:223
  19.3 147.6 %all-gather.3.cloned.1.call-start = ((), (), s32[]{:S(2)}) async-start(), calls=%async_computation.4 | async-start | bytes 5570560 | tf_op jit(solution)/shard_map/all_gather | solution.py:278
  21.9 11.3 %collective-permute-start = (bf16[32,512]{1,0:T(8,128)(2,1)S(1)}, bf16[32,512]{1,0:T(8,128)(2,1)S(1)}, u32[]{:S(2)}, u32[]{:S(2)}) collective-permute-start(bf16[32,512]{1,0:T(8,128)(2,1)S(1)} %dynamic-slice_bitcast_fusion), channel_id=1, source_target_pairs={{0,8},{8,16},{16,24},{24,32},{32,40},{40,48},{48,56},{56,64},{64,7... | collective-permute-start | bytes 98312 | tf_op jit(solution)/shard_map/ppermute | solution.py:226
  28.4 12.6 %copy-start.6 = (f32[512]{0:T(512)S(1)}, f32[512]{0:T(512)}, u32[]{:S(2)}) copy-start(f32[512]{0:T(512)} %param.17) | copy-start | bytes 6148
  30.2 10.8 %collective-permute-start.1 = (bf16[32,512]{1,0:T(8,128)(2,1)S(1)}, bf16[32,512]{1,0:T(8,128)(2,1)S(1)}, u32[]{:S(2)}, u32[]{:S(2)}) collective-permute-start(bf16[32,512]{1,0:T(8,128)(2,1)S(1)} %fusion.45), channel_id=1, source_target_pairs={{0,8},{8,16},{16,24},{24,32},{32,40},{40,48},{48,56},{56,64},{64,7... | collective-permute-start | bytes 98312 | tf_op jit(solution)/shard_map/ppermute | solution.py:240
  62.5 205.5 %reduce-scatter.2.cloned.1.call-start = ((), (), s32[]{:S(2)}) async-start(), calls=%async_computation.6 | async-start | bytes 5570560 | tf_op jit(solution)/shard_map/reduce_scatter | solution.py:299
  62.6 60.1 %collective-permute-start.2 = (bf16[4096,256]{1,0:T(8,128)(2,1)}, bf16[4096,256]{1,0:T(8,128)(2,1)}, u32[]{:S(2)}, u32[]{:S(2)}) collective-permute-start(bf16[4096,256]{1,0:T(8,128)(2,1)} %bitcast.24.refs_0_), channel_id=1, source_target_pairs={{0,2},{2,4},{4,6},{6,0},{1,3},{3,5},{5,7},{7,1},{8,10},{10,12},{12... | collective-permute-start | bytes 6291464 | tf_op jit(solution)/shard_map/ppermute | solution.py:178
  64.5 58.1 %collective-permute-start.3 = (bf16[4096,256]{1,0:T(8,128)(2,1)}, bf16[4096,256]{1,0:T(8,128)(2,1)}, u32[]{:S(2)}, u32[]{:S(2)}) collective-permute-start(bf16[4096,256]{1,0:T(8,128)(2,1)} %bitcast.24.refs_0_), channel_id=1, source_target_pairs={{0,6},{2,0},{4,2},{6,4},{1,7},{3,1},{5,3},{7,5},{8,14},{10,8},{12,... | collective-permute-start | bytes 6291464 | tf_op jit(solution)/shard_map/ppermute | solution.py:178
  122.7 44.3 %collective-permute-start.11 = (bf16[4,1024,512]{2,1,0:T(8,128)(2,1)}, bf16[4,1024,512]{2,1,0:T(8,128)(2,1)}, u32[]{:S(2)}, u32[]{:S(2)}) collective-permute-start(bf16[4,1024,512]{2,1,0:T(8,128)(2,1)} %all-gather.5.cloned.1.call-done.refs_10_), channel_id=1, source_target_pairs={{0,1},{1,0},{2,3},{3,2},{4,5},{5,4},{6,7},{7,6},{8,9},{9,8},{10,11... | collective-permute-start | bytes 12582920 | tf_op jit(solution)/shard_map/ppermute | solution.py:182
  126.4 26.8 %collective-permute-start.5 = (bf16[2048,256]{1,0:T(8,128)(2,1)S(1)}, bf16[2048,256]{1,0:T(8,128)(2,1)S(1)}, u32[]{:S(2)}, u32[]{:S(2)}) collective-permute-start(bf16[2048,256]{1,0:T(8,128)(2,1)S(1)} %slice.48), channel_id=1, source_target_pairs={{0,6},{2,0},{4,2},{6,4},{1,7},{3,1},{5,3},{7,5},{8,14},{10,8},{12,... | collective-permute-start | bytes 3145736 | tf_op jit(solution)/shard_map/ppermute | solution.py:178
  130.2 27.7 %collective-permute-start.4 = (bf16[2048,256]{1,0:T(8,128)(2,1)S(1)}, bf16[2048,256]{1,0:T(8,128)(2,1)}, u32[]{:S(2)}, u32[]{:S(2)}) collective-permute-start(bf16[2048,256]{1,0:T(8,128)(2,1)S(1)} %slice.47), channel_id=1, source_target_pairs={{0,2},{2,4},{4,6},{6,0},{1,3},{3,5},{5,7},{7,1},{8,10},{10,12},{12... | collective-permute-start | bytes 3145736 | tf_op jit(solution)/shard_map/ppermute | solution.py:178
  133.0 33.8 %collective-permute-start.7 = (bf16[4096,256]{1,0:T(8,128)(2,1)}, bf16[4096,256]{1,0:T(8,128)(2,1)}, u32[]{:S(2)}, u32[]{:S(2)}) collective-permute-start(bf16[4096,256]{1,0:T(8,128)(2,1)} %collective-permute-done.2.refs_1_), channel_id=1, source_target_pairs={{0,1},{1,0},{2,3},{3,2},{4,5},{5,4},{6,7},{7,6},{8,9},{9,8},{10,11... | collective-permute-start | bytes 6291464 | tf_op jit(solution)/shard_map/ppermute | solution.py:182
  153.2 7.7 %collective-permute-start.10 = (bf16[2048,256]{1,0:T(8,128)(2,1)S(1)}, bf16[2048,256]{1,0:T(8,128)(2,1)S(1)}, u32[]{:S(2)}, u32[]{:S(2)}) collective-permute-start(bf16[2048,256]{1,0:T(8,128)(2,1)S(1)} %collective-permute-done.5.refs_4_), channel_id=1, source_target_pairs={{0,1},{1,0},{2,3},{3,2},{4,5},{5,4},{6,7},{7,6},{8,9},{9,8},{10,11... | collective-permute-start | bytes 3145736 | tf_op jit(solution)/shard_map/ppermute | solution.py:182
  155.8 11.0 %collective-permute-start.6 = (bf16[4096,256]{1,0:T(8,128)(2,1)}, bf16[4096,256]{1,0:T(8,128)(2,1)}, u32[]{:S(2)}, u32[]{:S(2)}) collective-permute-start(bf16[4096,256]{1,0:T(8,128)(2,1)} %bitcast.24.refs_0_), channel_id=1, source_target_pairs={{0,1},{1,0},{2,3},{3,2},{4,5},{5,4},{6,7},{7,6},{8,9},{9,8},{10,11... | collective-permute-start | bytes 6291464 | tf_op jit(solution)/shard_map/ppermute | solution.py:182
  157.9 8.9 %collective-permute-start.8 = (bf16[4096,256]{1,0:T(8,128)(2,1)}, bf16[4096,256]{1,0:T(8,128)(2,1)}, u32[]{:S(2)}, u32[]{:S(2)}) collective-permute-start(bf16[4096,256]{1,0:T(8,128)(2,1)} %collective-permute-done.3.refs_2_), channel_id=1, source_target_pairs={{0,1},{1,0},{2,3},{3,2},{4,5},{5,4},{6,7},{7,6},{8,9},{9,8},{10,11... | collective-permute-start | bytes 6291464 | tf_op jit(solution)/shard_map/ppermute | solution.py:182
  160.9 1.0 copy-start.1
  161.9 4.9 %collective-permute-start.9 = (bf16[2048,256]{1,0:T(8,128)(2,1)}, bf16[2048,256]{1,0:T(8,128)(2,1)}, u32[]{:S(2)}, u32[]{:S(2)}) collective-permute-start(bf16[2048,256]{1,0:T(8,128)(2,1)} %collective-permute-done.4.refs_3_), channel_id=1, source_target_pairs={{0,1},{1,0},{2,3},{3,2},{4,5},{5,4},{6,7},{7,6},{8,9},{9,8},{10,11... | collective-permute-start | bytes 3145736 | tf_op jit(solution)/shard_map/ppermute | solution.py:182
  192.7 0.7 copy-start.5
  270.1 28.3 %all-to-all-start.2 = ((bf16[32,10,512]{2,1,0:T(8,128)(2,1)}), bf16[32,10,512]{2,1,0:T(8,128)(2,1)S(1)}, u32[]{:S(2)}, u32[]{:S(2)}) async-start(bf16[32,10,512]{2,1,0:T(8,128)(2,1)} %copy.39), calls=%async_computation.3 | async-start | bytes 1048576 | tf_op jit(solution)/shard_map/all_to_all | solution.py:301
Sparse Core Ops, SparseCore 0:
  9.5 77.0 all-gather.4
  88.6 78.2 all-gather.2
  192.8 75.1 reduce-scatter.1

commit v6 on v5

--- a/solution.py
+++ b/solution.py
@@ -92,11 +92,12 @@
 
 CHUNKS = 4
 HALF = D // 2
+DEEP = 512
 
 
 def expert_kernel(order_ref, all_ref, take_ref, put_ref, *refs):
-    in_refs, down_refs = refs[:10], refs[10:12]
-    out_ref, gathered, rows, in_buf, down_buf, active, whole, sems = refs[12:]
+    in_refs, low_ref, high_refs = refs[:10], refs[10], refs[11:21]
+    out_ref, gathered, rows, in_buf, down_buf, active, whole, sems = refs[21:]
     width = D // CHUNKS
     numbers = iter(range(sems.shape[0]))
 
@@ -118,11 +119,18 @@
         loads[core * NY + 3] = [
             begin(in_refs[core * 5 + 3 + i], chunk.at[pl.ds(i * HALF, HALF)]) for i in range(2)
         ]
-    downs = [
-        begin(down_refs[core].at[k], down_buf.at[core * NY + k])
-        for core in range(NC)
-        for k in range(NY)
-    ]
+    downs = []
+    for core in range(NC):
+        for k in range(NY):
+            slot = core * NY + k
+            group = [begin(low_ref.at[order_ref[slot]], down_buf.at[slot, pl.ds(0, DEEP)])]
+            if k < 3:
+                group.append(begin(high_refs[core * 5 + k], down_buf.at[slot, pl.ds(DEEP, DEEP)]))
+            else:
+                for i in range(2):
+                    place = pl.ds(DEEP + i * DEEP // 2, DEEP // 2)
+                    group.append(begin(high_refs[core * 5 + 3 + i], down_buf.at[slot, place]))
+            downs.append(group)
     for n in range(CHUNKS):
         parts[n].wait()
         rows[:, n * width : (n + 1) * width] = jnp.dot(
@@ -140,25 +148,26 @@
         whole[:, t * 128 : (t + 1) * 128] = active[t]
     outs = []
     for slot in range(N_TP):
-        downs[slot].wait()
+        for copy in downs[slot]:
+            copy.wait()
         part = jnp.dot(whole[...], down_buf[slot], preferred_element_type=jnp.float32)
         place = gathered.at[slot // 2, :, pl.ds(slot % 2 * 512, 512)]
         place[...] = jnp.dot(
             put_ref[...], part.astype(jnp.bfloat16), preferred_element_type=jnp.float32
         ).astype(jnp.bfloat16)
-        lanes = pl.ds(pl.multiple_of(order_ref[N_TP + slot] * 512, 512), 512)
+        lanes = pl.ds(pl.multiple_of(order_ref[slot] * 512, 512), 512)
         outs.append(begin(place, out_ref.at[:, lanes]))
     for copy in outs:
         copy.wait()
 
 
-def run_experts(order, all_rows, take, put, weights_in, weights_down):
+def run_experts(order, all_rows, take, put, weights_in, low_down, high_down):
     far = pl.BlockSpec(memory_space=pltpu.HBM)
     local = pl.BlockSpec(memory_space=pltpu.VMEM)
     return pl.pallas_call(
         expert_kernel,
         out_shape=jax.ShapeDtypeStruct((ALL_ROWS, D), jnp.bfloat16),
-        in_specs=[pl.BlockSpec(memory_space=pltpu.SMEM), far, local, local] + [far] * 12,
+        in_specs=[pl.BlockSpec(memory_space=pltpu.SMEM), far, local, local] + [far] * 21,
         out_specs=far,
         scratch_shapes=[
             pltpu.VMEM((CHUNKS, ALL_ROWS, D // CHUNKS), jnp.bfloat16),
@@ -167,11 +176,11 @@
             pltpu.VMEM((N_TP, 1024, 512), jnp.bfloat16),
             pltpu.VMEM((N_TP, OWN_ROWS, 128), jnp.bfloat16),
             pltpu.VMEM((OWN_ROWS, 1024), jnp.bfloat16),
-            pltpu.SemaphoreType.DMA((CHUNKS + 10 + 2 * N_TP,)),
+            pltpu.SemaphoreType.DMA((CHUNKS + 10 + 18 + N_TP,)),
         ],
         compiler_params=pltpu.CompilerParams(vmem_limit_bytes=50 << 20),
         name="experts",
-    )(order, all_rows, take, put, *weights_in, *weights_down)
+    )(order, all_rows, take, put, *weights_in, low_down, *high_down)
 
 
 def by_y(value, step):
@@ -180,10 +189,6 @@
 
 def other_core(value):
     return lax.ppermute(value, "c", [(0, 1), (1, 0)])
-
-
-def both_cores(pieces):
-    return pieces + [other_core(piece) for piece in pieces]
 
 
 def three_parts(values):
@@ -216,11 +221,14 @@
     handing = [(i, (i + 1) % N_REP) for i in range(N_REP)]
 
     in_own = gate_up[0]
-    down_mine = lax.all_gather(down_proj[0], "y")
+    low_down = lax.all_gather(down_proj[0, :DEEP], TP)
+    down_own = down_proj[0, DEEP:]
     mixed = jnp.concatenate(
         [queries.reshape(-1, N_TP, 512), fresh_kv.reshape(-1, N_TP, 256)], axis=2
     )
     heads = lax.all_to_all(mixed, TP, split_axis=1, concat_axis=0, tiled=True)[:, 0]
+    heads, down_own = lax.optimization_barrier((heads, down_own))
+    down_below, down_above = by_y(down_own, 1), by_y(down_own, -1)
     query_heads, kv_rows = heads[:, :512], heads[:, 512:]
     resid_slots = residual.reshape(REQ, FRESH, -1)
     resid_came = lax.ppermute(
@@ -272,22 +280,29 @@
     )
     packed = jnp.dot(placing, payload, preferred_element_type=jnp.float32).astype(jnp.bfloat16)
     received = lax.all_to_all(packed.reshape(NX * N_TP, PIECE, WIDE), SPREAD, 0, 0)
-    received, in_own = lax.optimization_barrier((received, in_own))
+    received, in_own, down_own, down_below, down_above = lax.optimization_barrier(
+        (received, in_own, down_own, down_below, down_above)
+    )
     in_below, in_above = by_y(in_own, 1), by_y(in_own, -1)
     normed = norm_rows(received.reshape(NX * N_TP, PIECE, WIDE))
     all_rows = lax.all_gather(normed, "z", tiled=True)
-    in_below, in_above, in_own, down_mine = lax.optimization_barrier(
-        (in_below, in_above, in_own, down_mine)
-    )
-    weights_down = both_cores([down_mine])
+    far_down = [by_y(down_below[: DEEP // 2], 1), by_y(down_above[DEEP // 2 :], -1)]
+    other_own = other_core(in_own)
+    other_down = [other_core(piece) for piece in (down_own, down_below, down_above)]
+    in_below, in_above, far_down, low_down = lax.optimization_barrier(
+        (in_below, in_above, far_down, low_down)
+    )
     far_in = [by_y(in_below[:HALF], 1), by_y(in_above[HALF:], -1)]
-    weights_in = both_cores([in_own, in_below, in_above] + far_in)
+    other_in = [other_own, other_core(in_below), other_core(in_above)]
+    weights_in = [in_own, in_below, in_above] + far_in + other_in
+    weights_in += [other_core(piece) for piece in far_in]
+    high_down = [down_own, down_below, down_above] + far_down + other_down
+    high_down += [other_core(piece) for piece in far_down]
     my_y, my_core = lax.axis_index("y"), lax.axis_index("c")
-    piece = jnp.arange(2 * N_TP, dtype=jnp.int32)
+    piece = jnp.arange(N_TP, dtype=jnp.int32)
     step = piece % NY
     step = jnp.where(step == 1, NY - 1, jnp.where(step == 2, 1, jnp.where(step == 3, 2, 0)))
-    place_y = jnp.where(piece < N_TP, (my_y + step) % NY, piece % NY)
-    order = place_y * NC + (my_core + piece // NY) % NC
+    order = (my_y + step) % NY * NC + (my_core + piece // NY) % NC
 
     index = jnp.arange(ALL_ROWS, dtype=jnp.int32)
     own = (index // SHARE) % 2 == my_z // 8
@@ -295,7 +310,9 @@
     own_index = jnp.arange(OWN_ROWS, dtype=jnp.int32)
     take = (own_index[:, None] == compact[None, :]).astype(jnp.bfloat16)
     put = (compact[:, None] == own_index[None, :]).astype(jnp.bfloat16)
-    partial_rows = run_experts(order, all_rows, take, put, weights_in, weights_down)
+    partial_rows = run_experts(
+        order, all_rows, take, put, weights_in, low_down, high_down
+    )
     summed = lax.psum_scatter(partial_rows, "z", scatter_dimension=0, tiled=True)
     back = summed.reshape(NX, PIECE, N_TP, 512).transpose(0, 2, 1, 3)
     returned = lax.all_to_all(back.reshape(NX * N_TP, PIECE, 512), SPREAD, 0, 0)

time: 307 us -> 324 us (1.055)
  starting transfers between devices: 57 us -> 82.1 us
  waiting for transfers between devices: 169 us -> 145 us
  blocking collectives: 18.5 us -> 26.7 us
  local copies, waits for them, and re-layouts: 11 us -> 18.1 us
    ppermute x4 -> x8, waiting for transfers between devices: 71.5 us -> 54.2 us  [by_y(): return lax.ppermute(value, 'y', [(i, (i + step) % NY) for i in range(NY)])]
    ppermute x4 -> x8, starting transfers between devices: 11.8 us -> 25.9 us  [by_y(): return lax.ppermute(value, 'y', [(i, (i + step) % NY) for i in range(NY)])]
    ppermute x6 -> x10, starting transfers between devices: 14.3 us -> 25.2 us  [other_core(): return lax.ppermute(value, 'c', [(0, 1), (1, 0)])]
    all_to_all x1, blocking collectives: 18.5 us -> 26.7 us  [per_device(): lax.all_to_all(packed.reshape(NX * N_TP, PIECE, WIDE), SPREAD, 0, 0)]
    ppermute x1, waiting for transfers between devices: 7.81 us -> 1.32 us  [per_device(): lax.ppermute(lax.dynamic_index_in_dim(attention, leave_slot, 0, keepdims=...]
    unnamed x26 -> x46, local copies, waits for them, and re-layouts: 4.24 us -> 8.12 us
  transfers between devices with their start and end apart: 17 -> 25, of which waited for: 8 -> 8; matrix products, arithmetic and copies ran while one was open for 4% -> 4% of each run, Pallas kernels for 1% -> 1%
where the time goes in v6:
time: 324 us; the launch traced here: 323 us
  waiting for transfers between devices  145 us (45%)
  starting transfers between devices  82.1 us (25%)
  Pallas kernels  27.8 us (9%)
  blocking collectives  26.7 us (8%)
  local copies, waits for them, and re-layouts  18.1 us (6%)
  between operations  15.7 us (5%)
  matrix products  5.81 us (2%)
    reduce_scatter x1, waiting for transfers between devices, per_device(): lax.psum_scatter(partial_rows, 'z', scatter_dimension=0, tiled=True)  74.4 us
    ppermute x8, waiting for transfers between devices, by_y(): return lax.ppermute(value, 'y', [(i, (i + step) % NY) for i in range(NY)])  54.2 us
    all_to_all x1, blocking collectives, per_device(): lax.all_to_all(packed.reshape(NX * N_TP, PIECE, WIDE), SPREAD, 0, 0)  26.7 us
    ppermute x8, starting transfers between devices, by_y(): return lax.ppermute(value, 'y', [(i, (i + step) % NY) for i in range(NY)])  25.9 us
    pallas_call x1, Pallas kernels, run_experts(): pl.pallas_call(expert_kernel, out_shape=jax.ShapeDtypeStruct((ALL_ROWS, D...  25.8 us
    ppermute x10, starting transfers between devices, other_core(): return lax.ppermute(value, 'c', [(0, 1), (1, 0)])  25.2 us
    all_to_all x1, starting transfers between devices, per_device(): returned = lax.all_to_all(back.reshape(NX * N_TP, PIECE, 512), SPREAD, 0, 0)  16.8 us
    all_to_all x1, waiting for transfers between devices, per_device(): returned = lax.all_to_all(back.reshape(NX * N_TP, PIECE, 512), SPREAD, 0, 0)  11.6 us
  transfers between devices with their start and end apart: 25, of which 8 were waited for; matrix products, arithmetic and copies ran while one was open for 4% of the time, Pallas kernels for 1%

profile of v6, /device:TPU:1, one launch (start us, length us, event | category | flops | bytes accessed | tf_op | source)
XLA Modules:
  0.0 323.2 jit_solution(17317891390992021620)
XLA Ops:
  6.5 2.1 fusion.87
  8.9 0.7 copy.33
  9.6 10.3 %all-to-all-start = ((bf16[16,8,768]{2,0,1:T(8,128)(2,1)}), bf16[16,8,768]{2,0,1:T(8,128)(2,1)S(1)}, u32[]{:S(2)}, u32[]{:S(2)}) async-start(bf16[16,8,768]{2,0,1:T(8,128)(2,1)} %copy.33), calls=%async_computation | async-start | bytes 393216 | tf_op jit(solution)/shard_map/all_to_all | solution.py:229
  22.5 1.9 collective-permute-start
  27.1 1.7 fusion.88
  28.8 1.7 fusion.11
  30.7 1.9 collective-permute-start.1
  33.6 3.3 %collective-permute-start.2 = (bf16[512,512]{1,0:T(8,128)(2,1)S(1)}, bf16[512,512]{1,0:T(8,128)(2,1)S(1)}, u32[]{:S(2)}, u32[]{:S(2)}) collective-permute-start(bf16[512,512]{1,0:T(8,128)(2,1)S(1)} %get-tuple-element.26.refs_11_), channel_id=1, source_target_pairs={{0,2},{2,4},{4,6},{6,0},{1,3},{3,5},{5,7},{7,1},{8,10},{10,12},{12... | collective-permute-start | bytes 1572872 | tf_op jit(solution)/shard_map/ppermute | solution.py:187
  36.9 3.2 collective-permute-start.3
  40.1 1.3 collective-permute-done.1
  42.6 1.0 convolution_convert_fusion
  43.7 1.1 reshape.317
  44.8 26.7 %all_to_all.25.recv_ref = bf16[32,10,640]{2,1,0:T(8,128)(2,1)} all-to-all(bf16[32,10,640]{2,1,0:T(8,128)(2,1)S(1)} %reshape.317), channel_id=1, replica_groups=mesh['x'=4,'z'=16,'y'=4,'c'=2] {'x','y','c'}, dimensions={0} | all-to-all | bytes 819200 | tf_op jit(solution)/shard_map/all_to_all | solution.py:282
  71.5 2.0 norm_rows.1
  73.6 2.6 collective-permute-start.4
  76.2 3.9 %collective-permute-start.5 = (bf16[4096,256]{1,0:T(8,128)(2,1)}, bf16[4096,256]{1,0:T(8,128)(2,1)}, u32[]{:S(2)}, u32[]{:S(2)}) collective-permute-start(bf16[4096,256]{1,0:T(8,128)(2,1)} %bitcast.99), channel_id=1, source_target_pairs={{0,6},{2,0},{4,2},{6,4},{1,7},{3,1},{5,3},{7,5},{8,14},{10,8},{12,... | collective-permute-start | bytes 6291464 | tf_op jit(solution)/shard_map/ppermute | solution.py:187
  80.1 1.9 collective-permute-start.6
  82.1 4.6 %collective-permute-start.7 = (bf16[256,512]{1,0:T(8,128)(2,1)S(1)}, bf16[256,512]{1,0:T(8,128)(2,1)}, u32[]{:S(2)}, u32[]{:S(2)}) collective-permute-start(bf16[256,512]{1,0:T(8,128)(2,1)S(1)} %slice.61), channel_id=1, source_target_pairs={{0,6},{2,0},{4,2},{6,4},{1,7},{3,1},{5,3},{7,5},{8,14},{10,8},{12,... | collective-permute-start | bytes 786440 | tf_op jit(solution)/shard_map/ppermute | solution.py:187
  86.7 3.5 %collective-permute-start.10 = (bf16[4096,256]{1,0:T(8,128)(2,1)}, bf16[4096,256]{1,0:T(8,128)(2,1)}, u32[]{:S(2)}, u32[]{:S(2)}) collective-permute-start(bf16[4096,256]{1,0:T(8,128)(2,1)} %bitcast.100), channel_id=1, source_target_pairs={{0,1},{1,0},{2,3},{3,2},{4,5},{5,4},{6,7},{7,6},{8,9},{9,8},{10,11... | collective-permute-start | bytes 6291464 | tf_op jit(solution)/shard_map/ppermute | solution.py:191
  90.2 39.1 %collective-permute-done.6.refs_14_ = bf16[256,512]{1,0:T(8,128)(2,1)} collective-permute-done((bf16[256,512]{1,0:T(8,128)(2,1)S(1)}, bf16[256,512]{1,0:T(8,128)(2,1)}, u32[]{:S(2)}, u32[]{:S(2)}) %collective-permute-start.6) | collective-permute-done | bytes 262176 | tf_op jit(solution)/shard_map/ppermute | solution.py:187
  129.3 3.2 %collective-permute-start.15 = (bf16[512,512]{1,0:T(8,128)(2,1)S(1)}, bf16[512,512]{1,0:T(8,128)(2,1)S(1)}, u32[]{:S(2)}, u32[]{:S(2)}) collective-permute-start(bf16[512,512]{1,0:T(8,128)(2,1)S(1)} %get-tuple-element.26.refs_11_), channel_id=1, source_target_pairs={{0,1},{1,0},{2,3},{3,2},{4,5},{5,4},{6,7},{7,6},{8,9},{9,8},{10,11... | collective-permute-start | bytes 1572872 | tf_op jit(solution)/shard_map/ppermute | solution.py:191
  132.6 1.9 collective-permute-start.16
  134.5 2.4 collective-permute-start.17
  137.0 1.3 slice.63
  138.3 1.9 collective-permute-start.8
  140.2 1.3 slice.64
  141.6 0.8 copy-done.1
  142.3 4.5 %collective-permute-start.9 = (bf16[2048,256]{1,0:T(8,128)(2,1)S(1)}, bf16[2048,256]{1,0:T(8,128)(2,1)}, u32[]{:S(2)}, u32[]{:S(2)}) collective-permute-start(bf16[2048,256]{1,0:T(8,128)(2,1)S(1)} %slice.64), channel_id=1, source_target_pairs={{0,6},{2,0},{4,2},{6,4},{1,7},{3,1},{5,3},{7,5},{8,14},{10,8},{12,... | collective-permute-start | bytes 3145736 | tf_op jit(solution)/shard_map/ppermute | solution.py:187
  146.9 2.5 collective-permute-start.11
  149.4 1.9 collective-permute-start.12
  151.3 14.9 %collective-permute-done.8.refs_3_ = bf16[2048,256]{1,0:T(8,128)(2,1)} collective-permute-done((bf16[2048,256]{1,0:T(8,128)(2,1)S(1)}, bf16[2048,256]{1,0:T(8,128)(2,1)}, u32[]{:S(2)}, u32[]{:S(2)}) %collective-permute-start.8) | collective-permute-done | bytes 1048608 | tf_op jit(solution)/shard_map/ppermute | solution.py:187
  166.3 2.7 collective-permute-start.13
  169.1 3.0 collective-permute-start.14
  172.2 1.9 collective-permute-start.18
  174.2 1.6 collective-permute-done.18.refs_19_
  175.8 0.7 copy-done.3
  176.5 2.0 collective-permute-start.19
  178.7 1.4 collective-permute-done.19.refs_20_
  180.9 1.0 copy-done.2
  182.0 0.9 copy-done.4
  182.9 0.9 copy-done.6
  183.8 25.8 %experts.1 = bf16[640,4096]{1,0:T(8,128)(2,1)} custom-call(s32[8]{0:T(128)S(1)} %fusion.69.order_ref, bf16[640,4096]{1,0:T(8,128)(2,1)} %all-gather.3.cloned.1.call-done.all_ref, bf16[320,640]{1,0:T(8,128)(2,1)S(1)} %fusion.10.take_ref, bf16[640,320]{1,0:T(8,128)(2,1)S(1)} %fusion.9.put_ref, bf16[4096,256]{1,0:T(8,128)(2,1)} %bitcast.101, ...), custom_call_target="tpu_custom_call" | custom-call | tf_op jit(solution)/shard_map/experts/pallas_call | solution.py:167
  210.4 74.4 %reduce-scatter.2.cloned.1.call-done = bf16[40,4096]{1,0:T(8,128)(2,1)} async-done(((bf16[640,4096]{1,0:T(8,128)(2,1)}), bf16[40,4096]{1,0:T(8,128)(2,1)}) %reduce-scatter.2.cloned.1.call-update) | async-done | bytes 327696 | tf_op jit(solution)/shard_map/reduce_scatter | solution.py:316
  284.8 1.1 copy.46
  285.9 1.0 copy.39
  286.9 16.8 %all-to-all-start.2 = ((bf16[32,10,512]{2,1,0:T(8,128)(2,1)}), bf16[32,10,512]{2,1,0:T(8,128)(2,1)S(1)}, u32[]{:S(2)}, u32[]{:S(2)}) async-start(bf16[32,10,512]{2,1,0:T(8,128)(2,1)} %copy.39), calls=%async_computation.3 | async-start | bytes 1048576 | tf_op jit(solution)/shard_map/all_to_all | solution.py:318
  303.7 11.6 %all-to-all-done.2 = bf16[32,10,512]{2,1,0:T(8,128)(2,1)S(1)} async-done(((bf16[32,10,512]{2,1,0:T(8,128)(2,1)}), bf16[32,10,512]{2,1,0:T(8,128)(2,1)S(1)}, u32[]{:S(2)}, u32[]{:S(2)}) %all-to-all-start.2) | async-done | bytes 327712 | tf_op jit(solution)/shard_map/all_to_all | solution.py:318
  315.7 0.9 fusion.8
  (116 shorter events, 8.0 us)
Async XLA Ops:
  6.5 19.3 %copy-start = (bf16[128,16,256]{2,1,0:T(8,128)(2,1)S(1)}, bf16[128,16,256]{2,1,0:T(8,128)(2,1)}, u32[]{:S(2)}) copy-start(bf16[128,16,256]{2,1,0:T(8,128)(2,1)} %param.15) | copy-start | bytes 3145732
  6.5 2.2 copy-start.12
  6.5 2.3 copy-start.13
  6.5 130.4 %all-gather.5.cloned.1.call-start = ((), (), s32[]{:S(2)}) async-start(), calls=%async_computation.5 | async-start | bytes 4718592 | tf_op jit(solution)/shard_map/all_gather | solution.py:224
  8.7 11.2 %copy-start.19 = (s32[64]{0:T(128)S(1)}, s32[64]{0:T(128)}, u32[]{:S(2)}) copy-start(s32[64]{0:T(128)} %param.23) | copy-start | bytes 772
  8.7 13.7 %copy-start.11 = (bf16[128,512]{1,0:T(8,128)(2,1)S(1)}, bf16[128,512]{1,0:T(8,128)(2,1)}, u32[]{:S(2)}) copy-start(bf16[128,512]{1,0:T(8,128)(2,1)} %param.16) | copy-start | bytes 393220
  8.7 15.7 %copy-start.17 = (s32[256]{0:T(256)S(1)}, s32[256]{0:T(256)}, u32[]{:S(2)}) copy-start(s32[256]{0:T(256)} %param.21) | copy-start | bytes 3076
  8.7 15.8 %copy-start.18 = (s32[256]{0:T(256)S(1)}, s32[256]{0:T(256)}, u32[]{:S(2)}) copy-start(s32[256]{0:T(256)} %param.20) | copy-start | bytes 3076
  8.7 16.4 %copy-start.20 = (s32[1,128]{1,0:T(1,128)S(1)}, s32[1,128]{1,0:T(1,128)}, u32[]{:S(2)}) copy-start(s32[1,128]{1,0:T(1,128)} %param.22) | copy-start | bytes 1540
  9.6 17.0 %copy-start.14 = (s32[128,2]{0,1:T(2,128)S(1)}, s32[128,2]{0,1:T(2,128)}, u32[]{:S(2)}) copy-start(s32[128,2]{0,1:T(2,128)} %param.24) | copy-start | bytes 3076
  9.6 17.4 %all-to-all-start = ((bf16[16,8,768]{2,0,1:T(8,128)(2,1)}), bf16[16,8,768]{2,0,1:T(8,128)(2,1)S(1)}, u32[]{:S(2)}, u32[]{:S(2)}) async-start(bf16[16,8,768]{2,0,1:T(8,128)(2,1)} %copy.33), calls=%async_computation | async-start | bytes 393216 | tf_op jit(solution)/shard_map/all_to_all | solution.py:229
  19.9 161.0 %all-gather.3.cloned.1.call-start = ((), (), s32[]{:S(2)}) async-start(), calls=%async_computation.4 | async-start | bytes 5570560 | tf_op jit(solution)/shard_map/all_gather | solution.py:288
  22.5 17.7 %collective-permute-start = (bf16[32,512]{1,0:T(8,128)(2,1)S(1)}, bf16[32,512]{1,0:T(8,128)(2,1)S(1)}, u32[]{:S(2)}, u32[]{:S(2)}) collective-permute-start(bf16[32,512]{1,0:T(8,128)(2,1)S(1)} %dynamic-slice_bitcast_fusion), channel_id=1, source_target_pairs={{0,8},{8,16},{16,24},{24,32},{32,40},{40,48},{48,56},{56,64},{64,7... | collective-permute-start | bytes 98312 | tf_op jit(solution)/shard_map/ppermute | solution.py:234
  28.8 12.6 %copy-start.16 = (f32[512]{0:T(512)S(1)}, f32[512]{0:T(512)}, u32[]{:S(2)}) copy-start(f32[512]{0:T(512)} %param.17) | copy-start | bytes 6148
  30.7 10.8 %collective-permute-start.1 = (bf16[32,512]{1,0:T(8,128)(2,1)S(1)}, bf16[32,512]{1,0:T(8,128)(2,1)S(1)}, u32[]{:S(2)}, u32[]{:S(2)}) collective-permute-start(bf16[32,512]{1,0:T(8,128)(2,1)S(1)} %fusion.45), channel_id=1, source_target_pairs={{0,8},{8,16},{16,24},{24,32},{32,40},{40,48},{48,56},{56,64},{64,7... | collective-permute-start | bytes 98312 | tf_op jit(solution)/shard_map/ppermute | solution.py:248
  33.6 37.9 %collective-permute-start.2 = (bf16[512,512]{1,0:T(8,128)(2,1)S(1)}, bf16[512,512]{1,0:T(8,128)(2,1)S(1)}, u32[]{:S(2)}, u32[]{:S(2)}) collective-permute-start(bf16[512,512]{1,0:T(8,128)(2,1)S(1)} %get-tuple-element.26.refs_11_), channel_id=1, source_target_pairs={{0,2},{2,4},{4,6},{6,0},{1,3},{3,5},{5,7},{7,1},{8,10},{10,12},{12... | collective-permute-start | bytes 1572872 | tf_op jit(solution)/shard_map/ppermute | solution.py:187
  36.9 34.6 %collective-permute-start.3 = (bf16[512,512]{1,0:T(8,128)(2,1)S(1)}, bf16[512,512]{1,0:T(8,128)(2,1)S(1)}, u32[]{:S(2)}, u32[]{:S(2)}) collective-permute-start(bf16[512,512]{1,0:T(8,128)(2,1)S(1)} %get-tuple-element.26.refs_11_), channel_id=1, source_target_pairs={{0,6},{2,0},{4,2},{6,4},{1,7},{3,1},{5,3},{7,5},{8,14},{10,8},{12,... | collective-permute-start | bytes 1572872 | tf_op jit(solution)/shard_map/ppermute | solution.py:187
  41.6 0.7 copy-start.7
  41.6 0.8 copy-start.9
  73.5 211.3 %reduce-scatter.2.cloned.1.call-start = ((), (), s32[]{:S(2)}) async-start(), calls=%async_computation.6 | async-start | bytes 5570560 | tf_op jit(solution)/shard_map/reduce_scatter | solution.py:316
  73.6 60.9 %collective-permute-start.4 = (bf16[4096,256]{1,0:T(8,128)(2,1)}, bf16[4096,256]{1,0:T(8,128)(2,1)}, u32[]{:S(2)}, u32[]{:S(2)}) collective-permute-start(bf16[4096,256]{1,0:T(8,128)(2,1)} %bitcast.98), channel_id=1, source_target_pairs={{0,2},{2,4},{4,6},{6,0},{1,3},{3,5},{5,7},{7,1},{8,10},{10,12},{12... | collective-permute-start | bytes 6291464 | tf_op jit(solution)/shard_map/ppermute | solution.py:187
  76.2 60.8 %collective-permute-start.5 = (bf16[4096,256]{1,0:T(8,128)(2,1)}, bf16[4096,256]{1,0:T(8,128)(2,1)}, u32[]{:S(2)}, u32[]{:S(2)}) collective-permute-start(bf16[4096,256]{1,0:T(8,128)(2,1)} %bitcast.99), channel_id=1, source_target_pairs={{0,6},{2,0},{4,2},{6,4},{1,7},{3,1},{5,3},{7,5},{8,14},{10,8},{12,... | collective-permute-start | bytes 6291464 | tf_op jit(solution)/shard_map/ppermute | solution.py:187
  80.1 49.2 %collective-permute-start.6 = (bf16[256,512]{1,0:T(8,128)(2,1)S(1)}, bf16[256,512]{1,0:T(8,128)(2,1)}, u32[]{:S(2)}, u32[]{:S(2)}) collective-permute-start(bf16[256,512]{1,0:T(8,128)(2,1)S(1)} %slice.60), channel_id=1, source_target_pairs={{0,2},{2,4},{4,6},{6,0},{1,3},{3,5},{5,7},{7,1},{8,10},{10,12},{12... | collective-permute-start | bytes 786440 | tf_op jit(solution)/shard_map/ppermute | solution.py:187
  82.1 50.5 %collective-permute-start.7 = (bf16[256,512]{1,0:T(8,128)(2,1)S(1)}, bf16[256,512]{1,0:T(8,128)(2,1)}, u32[]{:S(2)}, u32[]{:S(2)}) collective-permute-start(bf16[256,512]{1,0:T(8,128)(2,1)S(1)} %slice.61), channel_id=1, source_target_pairs={{0,6},{2,0},{4,2},{6,4},{1,7},{3,1},{5,3},{7,5},{8,14},{10,8},{12,... | collective-permute-start | bytes 786440 | tf_op jit(solution)/shard_map/ppermute | solution.py:187
  86.7 85.5 %collective-permute-start.10 = (bf16[4096,256]{1,0:T(8,128)(2,1)}, bf16[4096,256]{1,0:T(8,128)(2,1)}, u32[]{:S(2)}, u32[]{:S(2)}) collective-permute-start(bf16[4096,256]{1,0:T(8,128)(2,1)} %bitcast.100), channel_id=1, source_target_pairs={{0,1},{1,0},{2,3},{3,2},{4,5},{5,4},{6,7},{7,6},{8,9},{9,8},{10,11... | collective-permute-start | bytes 6291464 | tf_op jit(solution)/shard_map/ppermute | solution.py:191
  129.3 12.2 %collective-permute-start.15 = (bf16[512,512]{1,0:T(8,128)(2,1)S(1)}, bf16[512,512]{1,0:T(8,128)(2,1)S(1)}, u32[]{:S(2)}, u32[]{:S(2)}) collective-permute-start(bf16[512,512]{1,0:T(8,128)(2,1)S(1)} %get-tuple-element.26.refs_11_), channel_id=1, source_target_pairs={{0,1},{1,0},{2,3},{3,2},{4,5},{5,4},{6,7},{7,6},{8,9},{9,8},{10,11... | collective-permute-start | bytes 1572872 | tf_op jit(solution)/shard_map/ppermute | solution.py:191
  132.6 14.3 %collective-permute-start.16 = (bf16[512,512]{1,0:T(8,128)(2,1)S(1)}, bf16[512,512]{1,0:T(8,128)(2,1)}, u32[]{:S(2)}, u32[]{:S(2)}) collective-permute-start(bf16[512,512]{1,0:T(8,128)(2,1)S(1)} %collective-permute-done.2.refs_12_), channel_id=1, source_target_pairs={{0,1},{1,0},{2,3},{3,2},{4,5},{5,4},{6,7},{7,6},{8,9},{9,8},{10,11... | collective-permute-start | bytes 1572872 | tf_op jit(solution)/shard_map/ppermute | solution.py:191
  134.5 14.9 %collective-permute-start.17 = (bf16[512,512]{1,0:T(8,128)(2,1)S(1)}, bf16[512,512]{1,0:T(8,128)(2,1)}, u32[]{:S(2)}, u32[]{:S(2)}) collective-permute-start(bf16[512,512]{1,0:T(8,128)(2,1)S(1)} %collective-permute-done.3.refs_13_), channel_id=1, source_target_pairs={{0,1},{1,0},{2,3},{3,2},{4,5},{5,4},{6,7},{7,6},{8,9},{9,8},{10,11... | collective-permute-start | bytes 1572872 | tf_op jit(solution)/shard_map/ppermute | solution.py:191
  138.3 28.0 %collective-permute-start.8 = (bf16[2048,256]{1,0:T(8,128)(2,1)S(1)}, bf16[2048,256]{1,0:T(8,128)(2,1)}, u32[]{:S(2)}, u32[]{:S(2)}) collective-permute-start(bf16[2048,256]{1,0:T(8,128)(2,1)S(1)} %slice.63), channel_id=1, source_target_pairs={{0,2},{2,4},{4,6},{6,0},{1,3},{3,5},{5,7},{7,1},{8,10},{10,12},{12... | collective-permute-start | bytes 3145736 | tf_op jit(solution)/shard_map/ppermute | solution.py:187
  141.5 0.8 copy-start.1
  142.3 26.8 %collective-permute-start.9 = (bf16[2048,256]{1,0:T(8,128)(2,1)S(1)}, bf16[2048,256]{1,0:T(8,128)(2,1)}, u32[]{:S(2)}, u32[]{:S(2)}) collective-permute-start(bf16[2048,256]{1,0:T(8,128)(2,1)S(1)} %slice.64), channel_id=1, source_target_pairs={{0,6},{2,0},{4,2},{6,4},{1,7},{3,1},{5,3},{7,5},{8,14},{10,8},{12,... | collective-permute-start | bytes 3145736 | tf_op jit(solution)/shard_map/ppermute | solution.py:187
  146.9 34.0 %collective-permute-start.11 = (bf16[4096,256]{1,0:T(8,128)(2,1)}, bf16[4096,256]{1,0:T(8,128)(2,1)}, u32[]{:S(2)}, u32[]{:S(2)}) collective-permute-start(bf16[4096,256]{1,0:T(8,128)(2,1)} %collective-permute-done.4.refs_1_), channel_id=1, source_target_pairs={{0,1},{1,0},{2,3},{3,2},{4,5},{5,4},{6,7},{7,6},{8,9},{9,8},{10,11... | collective-permute-start | bytes 6291464 | tf_op jit(solution)/shard_map/ppermute | solution.py:191
  149.4 31.5 %collective-permute-start.12 = (bf16[4096,256]{1,0:T(8,128)(2,1)}, bf16[4096,256]{1,0:T(8,128)(2,1)}, u32[]{:S(2)}, u32[]{:S(2)}) collective-permute-start(bf16[4096,256]{1,0:T(8,128)(2,1)} %collective-permute-done.5.refs_2_), channel_id=1, source_target_pairs={{0,1},{1,0},{2,3},{3,2},{4,5},{5,4},{6,7},{7,6},{8,9},{9,8},{10,11... | collective-permute-start | bytes 6291464 | tf_op jit(solution)/shard_map/ppermute | solution.py:191
  166.3 14.6 %collective-permute-start.13 = (bf16[2048,256]{1,0:T(8,128)(2,1)}, bf16[2048,256]{1,0:T(8,128)(2,1)}, u32[]{:S(2)}, u32[]{:S(2)}) collective-permute-start(bf16[2048,256]{1,0:T(8,128)(2,1)} %collective-permute-done.8.refs_3_), channel_id=1, source_target_pairs={{0,1},{1,0},{2,3},{3,2},{4,5},{5,4},{6,7},{7,6},{8,9},{9,8},{10,11... | collective-permute-start | bytes 3145736 | tf_op jit(solution)/shard_map/ppermute | solution.py:191
  169.1 11.7 %collective-permute-start.14 = (bf16[2048,256]{1,0:T(8,128)(2,1)}, bf16[2048,256]{1,0:T(8,128)(2,1)}, u32[]{:S(2)}, u32[]{:S(2)}) collective-permute-start(bf16[2048,256]{1,0:T(8,128)(2,1)} %collective-permute-done.9.refs_4_), channel_id=1, source_target_pairs={{0,1},{1,0},{2,3},{3,2},{4,5},{5,4},{6,7},{7,6},{8,9},{9,8},{10,11... | collective-permute-start | bytes 3145736 | tf_op jit(solution)/shard_map/ppermute | solution.py:191
  172.2 3.6 %collective-permute-start.18 = (bf16[256,512]{1,0:T(8,128)(2,1)}, bf16[256,512]{1,0:T(8,128)(2,1)S(1)}, u32[]{:S(2)}, u32[]{:S(2)}) collective-permute-start(bf16[256,512]{1,0:T(8,128)(2,1)} %collective-permute-done.6.refs_14_), channel_id=1, source_target_pairs={{0,1},{1,0},{2,3},{3,2},{4,5},{5,4},{6,7},{7,6},{8,9},{9,8},{10,11... | collective-permute-start | bytes 786440 | tf_op jit(solution)/shard_map/ppermute | solution.py:191
  175.8 0.7 copy-start.3
  176.5 3.6 %collective-permute-start.19 = (bf16[256,512]{1,0:T(8,128)(2,1)}, bf16[256,512]{1,0:T(8,128)(2,1)S(1)}, u32[]{:S(2)}, u32[]{:S(2)}) collective-permute-start(bf16[256,512]{1,0:T(8,128)(2,1)} %collective-permute-done.7.refs_15_), channel_id=1, source_target_pairs={{0,1},{1,0},{2,3},{3,2},{4,5},{5,4},{6,7},{7,6},{8,9},{9,8},{10,11... | collective-permute-start | bytes 786440 | tf_op jit(solution)/shard_map/ppermute | solution.py:191
  180.1 0.7 copy-start.5
  180.9 1.0 copy-start.2
  181.9 0.9 copy-start.4
  182.9 0.9 copy-start.6
  209.7 0.7 copy-start.15
  286.9 28.8 %copy-start.8 = (bf16[128,512]{1,0:T(8,128)(2,1)S(1)}, bf16[128,512]{1,0:T(8,128)(2,1)}, u32[]{:S(2)}) copy-start(bf16[128,512]{1,0:T(8,128)(2,1)} %copy-done.7) | copy-start | bytes 393220
  286.9 28.8 %copy-start.10 = (bf16[128,512]{1,0:T(8,128)(2,1)S(1)}, bf16[128,512]{1,0:T(8,128)(2,1)}, u32[]{:S(2)}) copy-start(bf16[128,512]{1,0:T(8,128)(2,1)} %copy-done.9) | copy-start | bytes 393220
  286.9 28.4 %all-to-all-start.2 = ((bf16[32,10,512]{2,1,0:T(8,128)(2,1)}), bf16[32,10,512]{2,1,0:T(8,128)(2,1)S(1)}, u32[]{:S(2)}, u32[]{:S(2)}) async-start(bf16[32,10,512]{2,1,0:T(8,128)(2,1)} %copy.39), calls=%async_computation.3 | async-start | bytes 1048576 | tf_op jit(solution)/shard_map/all_to_all | solution.py:318
Sparse Core Ops, SparseCore 0:
  9.5 63.7 all-gather.4
  75.4 72.9 all-gather.2
  209.8 74.9 reduce-scatter.1

commit v7 on v3

--- a/solution.py
+++ b/solution.py
@@ -108,26 +108,30 @@
     parts = [
         begin(all_ref.at[:, pl.ds(n * width, width)], gathered.at[n]) for n in range(CHUNKS)
     ]
-    loads = []
-    for core in range(NC):
-        for k in range(NY):
-            chunk, first = in_buf.at[core * NY + k], core * 7 + 2 * k
-            if k == 0:
-                loads.append([begin(in_refs[first], chunk)])
-            else:
-                loads.append(
-                    [
-                        begin(in_refs[first - 1], chunk.at[pl.ds(0, half)]),
-                        begin(in_refs[first], chunk.at[pl.ds(half, half)]),
-                    ]
-                )
-    downs = [begin(down_hbm.at[t], down_buf.at[t]) for t in range(N_TP)]
+
+    def load(slot):
+        chunk, first = in_buf.at[slot], slot // NY * 7 + 2 * (slot % NY)
+        if slot % NY == 0:
+            return [begin(in_refs[first], chunk)]
+        return [
+            begin(in_refs[first - 1], chunk.at[pl.ds(0, half)]),
+            begin(in_refs[first], chunk.at[pl.ds(half, half)]),
+        ]
+
+    loads = [load(0)]
     for n in range(CHUNKS):
         parts[n].wait()
         rows[:, n * width : (n + 1) * width] = jnp.dot(
             take_ref[...], gathered[n], preferred_element_type=jnp.float32
         ).astype(jnp.bfloat16)
+        if n == 1:
+            loads.append(load(1))
+    loads.append(load(2))
+    downs = []
     for k in range(N_TP):
+        if k + 3 < N_TP:
+            loads.append(load(k + 3))
+        downs.append(begin(down_hbm.at[k], down_buf.at[k]))
         for copy in loads[k]:
             copy.wait()
         both = jnp.dot(rows[...], in_buf[k], preferred_element_type=jnp.float32)
@@ -179,12 +183,10 @@
     return lax.ppermute(value, "c", [(0, 1), (1, 0)])
 
 
-def gather_pieces(own):
+def gather_pieces(own, below_top, above_bottom):
     half = own.shape[0] // 2
-    top, bottom = own[:half], own[half:]
-    below_top, above_bottom = by_y(top, 1), by_y(bottom, -1)
-    below_bottom, above_top = by_y(bottom, 1), by_y(top, -1)
     far_top, far_bottom = by_y(below_top, 1), by_y(above_bottom, -1)
+    below_bottom, above_top = by_y(own[half:], 1), by_y(own[:half], -1)
     pieces = [own, below_top, below_bottom, above_top, above_bottom, far_top, far_bottom]
     return pieces + [other_core(piece) for piece in pieces]
 
@@ -224,6 +226,8 @@
         [queries.reshape(-1, N_TP, 512), fresh_kv.reshape(-1, N_TP, 256)], axis=2
     )
     heads = lax.all_to_all(mixed, TP, split_axis=1, concat_axis=0, tiled=True)[:, 0]
+    heads, in_own = lax.optimization_barrier((heads, in_own))
+    below_top, above_bottom = by_y(in_own[: D // 2], 1), by_y(in_own[D // 2 :], -1)
     query_heads, kv_rows = heads[:, :512], heads[:, 512:]
     resid_slots = residual.reshape(REQ, FRESH, -1)
     resid_came = lax.ppermute(
@@ -276,9 +280,11 @@
     packed = jnp.dot(placing, payload, preferred_element_type=jnp.float32).astype(jnp.bfloat16)
     received = lax.all_to_all(packed.reshape(NX * N_TP, PIECE, WIDE), SPREAD, 0, 0)
     normed = norm_rows(received.reshape(NX * N_TP, PIECE, WIDE))
-    normed, in_own, weights_down = lax.optimization_barrier((normed, in_own, weights_down))
+    normed, in_own, weights_down, below_top, above_bottom = lax.optimization_barrier(
+        (normed, in_own, weights_down, below_top, above_bottom)
+    )
     all_rows = lax.all_gather(normed, "z", tiled=True)
-    weights_in = gather_pieces(in_own)
+    weights_in = gather_pieces(in_own, below_top, above_bottom)
     my_y, my_core = lax.axis_index("y"), lax.axis_index("c")
     piece = jnp.arange(N_TP, dtype=jnp.int32)
     step = piece % 4

time: 308 us -> 322 us (1.045)
  blocking collectives: 18.6 us -> 55.2 us
  waiting for transfers between devices: 158 us -> 132 us
    all_to_all x1, blocking collectives: 18.6 us -> 55.2 us  [per_device(): lax.all_to_all(packed.reshape(NX * N_TP, PIECE, WIDE), SPREAD, 0, 0)]
    all_gather x1, waiting for transfers between devices: 17.3 us -> 0.98 us  [per_device(): weights_down = lax.all_gather(down_proj[0], TP)]
    ppermute x6, waiting for transfers between devices: 44.2 us -> 28.9 us  [by_y(): return lax.ppermute(value, 'y', [(i, (i + step) % NY) for i in range(NY)])]
    all_gather x1, waiting for transfers between devices: 0.01 us -> 11.1 us  [per_device(): all_rows = lax.all_gather(normed, 'z', tiled=True)]
    ppermute x1, waiting for transfers between devices: 7.81 us -> 0.01 us  [per_device(): lax.ppermute(lax.dynamic_index_in_dim(attention, leave_slot, 0, keepdims=...]
    slice x1 -> x2, local copies, waits for them, and re-layouts: 1.68 us -> 5.02 us  [the longest x1 3.34 us: per_device(): in_own[D // 2:]]
  transfers between devices with their start and end apart: 20 -> 20, of which waited for: 8 -> 7; matrix products, arithmetic and copies ran while one was open for 4% -> 5% of each run, Pallas kernels for 1% -> 1%
where the time goes in v7:
time: 322 us; the launch traced here: 321 us
  waiting for transfers between devices  132 us (41%)
  starting transfers between devices  67.7 us (21%)
  blocking collectives  55.2 us (17%)
  Pallas kernels  28.2 us (9%)
  between operations  15.6 us (5%)
  local copies, waits for them, and re-layouts  14.6 us (5%)
  matrix products  5.08 us (2%)
    reduce_scatter x1, waiting for transfers between devices, per_device(): lax.psum_scatter(partial_rows, 'z', scatter_dimension=0, tiled=True)  76.2 us
    all_to_all x1, blocking collectives, per_device(): lax.all_to_all(packed.reshape(NX * N_TP, PIECE, WIDE), SPREAD, 0, 0)  55.2 us
    ppermute x6, waiting for transfers between devices, by_y(): return lax.ppermute(value, 'y', [(i, (i + step) % NY) for i in range(NY)])  28.9 us
    pallas_call x1, Pallas kernels, run_experts(): pl.pallas_call(expert_kernel, out_shape=jax.ShapeDtypeStruct((ALL_ROWS, D...  26.2 us
    ppermute x6, starting transfers between devices, by_y(): return lax.ppermute(value, 'y', [(i, (i + step) % NY) for i in range(NY)])  19.5 us
    ppermute x7, starting transfers between devices, other_core(): return lax.ppermute(value, 'c', [(0, 1), (1, 0)])  17.5 us
    all_to_all x1, starting transfers between devices, per_device(): returned = lax.all_to_all(back.reshape(NX * N_TP, PIECE, 512), SPREAD, 0, 0)  16.4 us
    all_to_all x1, waiting for transfers between devices, per_device(): returned = lax.all_to_all(back.reshape(NX * N_TP, PIECE, 512), SPREAD, 0, 0)  11.6 us
  transfers between devices with their start and end apart: 20, of which 7 were waited for; matrix products, arithmetic and copies ran while one was open for 5% of the time, Pallas kernels for 1%

profile of v7, /device:TPU:1, one launch (start us, length us, event | category | flops | bytes accessed | tf_op | source)
XLA Modules:
  0.0 320.9 jit_solution(6312831133458981026)
XLA Ops:
  6.6 0.7 all-gather.3.cloned.1.call-update
  7.3 0.9 copy.43
  8.3 0.7 copy.33
  9.0 10.3 %all-to-all-start = ((bf16[16,8,768]{2,0,1:T(8,128)(2,1)}), bf16[16,8,768]{2,0,1:T(8,128)(2,1)S(1)}, u32[]{:S(2)}, u32[]{:S(2)}) async-start(bf16[16,8,768]{2,0,1:T(8,128)(2,1)} %copy.33), calls=%async_computation | async-start | bytes 393216 | tf_op jit(solution)/shard_map/all_to_all | solution.py:228
  19.3 0.6 dynamic_slice.16
  21.9 1.9 collective-permute-start
  24.0 0.5 broadcast.378
  24.5 0.6 reduce.3
  25.4 0.7 iota_compare_fusion.17
  26.3 0.6 gather_fusion
  27.5 1.8 fusion.89
  29.3 1.7 fusion.11
  31.1 2.0 collective-permute-start.1
  33.1 3.3 %fusion.88 = (bf16[2048,256]{1,0:T(8,128)(2,1)}, bf16[2048,256]{1,0:T(8,128)(2,1)}) fusion(bf16[4096,256]{1,0:T(8,128)(2,1)} %bitcast.8.refs_0_), kind=kLoop, calls=%fused_computation.155 | loop fusion | bytes 4194304 | tf_op jit(solution)/shard_map/slice | solution.py:230
  36.5 3.3 %collective-permute-start.2 = (bf16[2048,256]{1,0:T(8,128)(2,1)}, bf16[2048,256]{1,0:T(8,128)(2,1)S(1)}, u32[]{:S(2)}, u32[]{:S(2)}) collective-permute-start(bf16[2048,256]{1,0:T(8,128)(2,1)} %get-tuple-element.25), channel_id=1, source_target_pairs={{0,2},{2,4},{4,6},{6,0},{1,3},{3,5},{5,7},{7,1},{8,10},{10,12},{12... | collective-permute-start | bytes 3145736 | tf_op jit(solution)/shard_map/ppermute | solution.py:179
  39.8 3.2 %collective-permute-start.3 = (bf16[2048,256]{1,0:T(8,128)(2,1)}, bf16[2048,256]{1,0:T(8,128)(2,1)}, u32[]{:S(2)}, u32[]{:S(2)}) collective-permute-start(bf16[2048,256]{1,0:T(8,128)(2,1)} %get-tuple-element.24), channel_id=1, source_target_pairs={{0,6},{2,0},{4,2},{6,4},{1,7},{3,1},{5,3},{7,5},{8,14},{10,8},{12,... | collective-permute-start | bytes 3145736 | tf_op jit(solution)/shard_map/ppermute | solution.py:179
  43.1 0.2 multiply_convert_fusion
  43.6 0.3 convolution_convert_fusion
  44.0 55.2 %all_to_all.25.recv_ref = bf16[32,10,640]{2,1,0:T(8,128)(2,1)} all-to-all(bf16[32,10,640]{2,1,0:T(8,128)(2,1)S(1)} %reshape.317), channel_id=1, replica_groups=mesh['x'=4,'z'=16,'y'=4,'c'=2] {'x','y','c'}, dimensions={0} | all-to-all | bytes 819200 | tf_op jit(solution)/shard_map/all_to_all | solution.py:281
  99.2 2.0 norm_rows.1
  101.2 1.0 all-gather.3.cloned.1.call-done.refs_14_
  102.3 1.7 fusion.87
  103.9 2.3 collective-permute-start.4
  106.3 4.2 %collective-permute-start.5 = (bf16[2048,256]{1,0:T(8,128)(2,1)S(1)}, bf16[2048,256]{1,0:T(8,128)(2,1)}, u32[]{:S(2)}, u32[]{:S(2)}) collective-permute-start(bf16[2048,256]{1,0:T(8,128)(2,1)S(1)} %get-tuple-element.22), channel_id=1, source_target_pairs={{0,6},{2,0},{4,2},{6,4},{1,7},{3,1},{5,3},{7,5},{8,14},{10,8},{12,... | collective-permute-start | bytes 3145736 | tf_op jit(solution)/shard_map/ppermute | solution.py:179
  110.5 2.7 collective-permute-start.8
  113.2 1.9 collective-permute-start.6
  115.1 4.6 %collective-permute-start.7 = (bf16[2048,256]{1,0:T(8,128)(2,1)}, bf16[2048,256]{1,0:T(8,128)(2,1)}, u32[]{:S(2)}, u32[]{:S(2)}) collective-permute-start(bf16[2048,256]{1,0:T(8,128)(2,1)} %collective-permute-done.3.refs_4_), channel_id=1, source_target_pairs={{0,6},{2,0},{4,2},{6,4},{1,7},{3,1},{5,3},{7,5},{8,14},{10,8},{12,... | collective-permute-start | bytes 3145736 | tf_op jit(solution)/shard_map/ppermute | solution.py:179
  119.7 12.0 %collective-permute-done.4.refs_2_ = bf16[2048,256]{1,0:T(8,128)(2,1)} collective-permute-done((bf16[2048,256]{1,0:T(8,128)(2,1)S(1)}, bf16[2048,256]{1,0:T(8,128)(2,1)}, u32[]{:S(2)}, u32[]{:S(2)}) %collective-permute-start.4) | collective-permute-done | bytes 1048608 | tf_op jit(solution)/shard_map/ppermute | solution.py:179
  131.7 3.6 %collective-permute-start.12 = (bf16[2048,256]{1,0:T(8,128)(2,1)}, bf16[2048,256]{1,0:T(8,128)(2,1)S(1)}, u32[]{:S(2)}, u32[]{:S(2)}) collective-permute-start(bf16[2048,256]{1,0:T(8,128)(2,1)} %collective-permute-done.3.refs_4_), channel_id=1, source_target_pairs={{0,1},{1,0},{2,3},{3,2},{4,5},{5,4},{6,7},{7,6},{8,9},{9,8},{10,11... | collective-permute-start | bytes 3145736 | tf_op jit(solution)/shard_map/ppermute | solution.py:183
  135.3 1.9 collective-permute-start.9
  137.2 16.9 %collective-permute-done.6.refs_5_ = bf16[2048,256]{1,0:T(8,128)(2,1)} collective-permute-done((bf16[2048,256]{1,0:T(8,128)(2,1)S(1)}, bf16[2048,256]{1,0:T(8,128)(2,1)}, u32[]{:S(2)}, u32[]{:S(2)}) %collective-permute-start.6) | collective-permute-done | bytes 1048608 | tf_op jit(solution)/shard_map/ppermute | solution.py:179
  154.1 3.0 collective-permute-start.10
  157.1 1.9 collective-permute-start.11
  159.1 2.4 collective-permute-start.13
  161.5 1.0 copy-done.1
  162.5 1.9 collective-permute-start.14
  164.8 2.6 collective-permute-done.14.refs_13_
  167.4 11.1 %all-gather.5.cloned.1.call-done.all_ref = bf16[640,4096]{1,0:T(8,128)(2,1)} async-done(((bf16[40,4096]{1,0:T(8,128)(2,1)}), bf16[640,4096]{1,0:T(8,128)(2,1)}) %all-gather.5.cloned.1.call-update) | async-done | bytes 5242896 | tf_op jit(solution)/shard_map/all_gather | solution.py:286
  178.5 1.2 copy-done.2
  179.7 26.2 %experts.1 = bf16[640,4096]{1,0:T(8,128)(2,1)} custom-call(s32[8]{0:T(128)S(1)} %fusion.69.order_ref, bf16[640,4096]{1,0:T(8,128)(2,1)} %all-gather.5.cloned.1.call-done.all_ref, bf16[320,640]{1,0:T(8,128)(2,1)S(1)} %fusion.10.take_ref, bf16[640,320]{1,0:T(8,128)(2,1)S(1)} %fusion.9.put_ref, bf16[4096,256]{1,0:T(8,128)(2,1)} %bitcast.8.refs_0_, ...), custom_call_target="tpu_custom_call" | custom-call | tf_op jit(solution)/shard_map/experts/pallas_call | solution.py:159
  206.0 0.6 copy-done.7
  206.7 76.2 %reduce-scatter.2.cloned.1.call-done = bf16[40,4096]{1,0:T(8,128)(2,1)} async-done(((bf16[640,4096]{1,0:T(8,128)(2,1)}), bf16[40,4096]{1,0:T(8,128)(2,1)}) %reduce-scatter.2.cloned.1.call-update) | async-done | bytes 327696 | tf_op jit(solution)/shard_map/reduce_scatter | solution.py:301
  282.9 1.1 copy.46
  284.0 1.0 copy.39
  285.0 16.4 %all-to-all-start.2 = ((bf16[32,10,512]{2,1,0:T(8,128)(2,1)}), bf16[32,10,512]{2,1,0:T(8,128)(2,1)S(1)}, u32[]{:S(2)}, u32[]{:S(2)}) async-start(bf16[32,10,512]{2,1,0:T(8,128)(2,1)} %copy.39), calls=%async_computation.3 | async-start | bytes 1048576 | tf_op jit(solution)/shard_map/all_to_all | solution.py:303
  301.4 11.6 %all-to-all-done.2 = bf16[32,10,512]{2,1,0:T(8,128)(2,1)S(1)} async-done(((bf16[32,10,512]{2,1,0:T(8,128)(2,1)}), bf16[32,10,512]{2,1,0:T(8,128)(2,1)S(1)}, u32[]{:S(2)}, u32[]{:S(2)}) %all-to-all-start.2) | async-done | bytes 327712 | tf_op jit(solution)/shard_map/all_to_all | solution.py:303
  313.1 0.3 convolution_multiply_fusion.2
  313.4 0.9 fusion.8
  (87 shorter events, 2.5 us)
Async XLA Ops:
  6.5 19.7 %copy-start = (bf16[128,16,256]{2,1,0:T(8,128)(2,1)S(1)}, bf16[128,16,256]{2,1,0:T(8,128)(2,1)}, u32[]{:S(2)}) copy-start(bf16[128,16,256]{2,1,0:T(8,128)(2,1)} %param.15) | copy-start | bytes 3145732
  6.5 1.7 copy-start.5
  6.5 12.8 %copy-start.11 = (s32[64]{0:T(128)S(1)}, s32[64]{0:T(128)}, u32[]{:S(2)}) copy-start(s32[64]{0:T(128)} %param.23) | copy-start | bytes 772
  6.5 15.3 %copy-start.4 = (bf16[128,512]{1,0:T(8,128)(2,1)S(1)}, bf16[128,512]{1,0:T(8,128)(2,1)}, u32[]{:S(2)}) copy-start(bf16[128,512]{1,0:T(8,128)(2,1)} %param.16) | copy-start | bytes 393220
  6.5 17.3 %copy-start.9 = (s32[256]{0:T(256)S(1)}, s32[256]{0:T(256)}, u32[]{:S(2)}) copy-start(s32[256]{0:T(256)} %param.21) | copy-start | bytes 3076
  6.5 17.4 %copy-start.10 = (s32[256]{0:T(256)S(1)}, s32[256]{0:T(256)}, u32[]{:S(2)}) copy-start(s32[256]{0:T(256)} %param.20) | copy-start | bytes 3076
  6.6 17.9 %copy-start.12 = (s32[1,128]{1,0:T(1,128)S(1)}, s32[1,128]{1,0:T(1,128)}, u32[]{:S(2)}) copy-start(s32[1,128]{1,0:T(1,128)} %param.22) | copy-start | bytes 1540
  6.6 95.6 %all-gather.3.cloned.1.call-start = ((), (), s32[]{:S(2)}) async-start(), calls=%async_computation.4 | async-start | bytes 9437184 | tf_op jit(solution)/shard_map/all_gather | solution.py:224
  9.0 18.0 %copy-start.6 = (s32[128,2]{0,1:T(2,128)S(1)}, s32[128,2]{0,1:T(2,128)}, u32[]{:S(2)}) copy-start(s32[128,2]{0,1:T(2,128)} %param.24) | copy-start | bytes 3076
  9.0 18.4 %all-to-all-start = ((bf16[16,8,768]{2,0,1:T(8,128)(2,1)}), bf16[16,8,768]{2,0,1:T(8,128)(2,1)S(1)}, u32[]{:S(2)}, u32[]{:S(2)}) async-start(bf16[16,8,768]{2,0,1:T(8,128)(2,1)} %copy.33), calls=%async_computation | async-start | bytes 393216 | tf_op jit(solution)/shard_map/all_to_all | solution.py:228
  19.3 159.2 %all-gather.5.cloned.1.call-start = ((), (), s32[]{:S(2)}) async-start(), calls=%async_computation.5 | async-start | bytes 5570560 | tf_op jit(solution)/shard_map/all_gather | solution.py:286
  21.9 21.2 %collective-permute-start = (bf16[32,512]{1,0:T(8,128)(2,1)S(1)}, bf16[32,512]{1,0:T(8,128)(2,1)S(1)}, u32[]{:S(2)}, u32[]{:S(2)}) collective-permute-start(bf16[32,512]{1,0:T(8,128)(2,1)S(1)} %dynamic-slice_bitcast_fusion), channel_id=1, source_target_pairs={{0,8},{8,16},{16,24},{24,32},{32,40},{40,48},{48,56},{56,64},{64,7... | collective-permute-start | bytes 98312 | tf_op jit(solution)/shard_map/ppermute | solution.py:233
  31.1 12.0 %copy-start.8 = (f32[512]{0:T(512)S(1)}, f32[512]{0:T(512)}, u32[]{:S(2)}) copy-start(f32[512]{0:T(512)} %param.17) | copy-start | bytes 6148
  31.1 12.0 %collective-permute-start.1 = (bf16[32,512]{1,0:T(8,128)(2,1)S(1)}, bf16[32,512]{1,0:T(8,128)(2,1)S(1)}, u32[]{:S(2)}, u32[]{:S(2)}) collective-permute-start(bf16[32,512]{1,0:T(8,128)(2,1)S(1)} %fusion.45), channel_id=1, source_target_pairs={{0,8},{8,16},{16,24},{24,32},{32,40},{40,48},{48,56},{56,64},{64,7... | collective-permute-start | bytes 98312 | tf_op jit(solution)/shard_map/ppermute | solution.py:247
  36.5 64.7 %collective-permute-start.2 = (bf16[2048,256]{1,0:T(8,128)(2,1)}, bf16[2048,256]{1,0:T(8,128)(2,1)S(1)}, u32[]{:S(2)}, u32[]{:S(2)}) collective-permute-start(bf16[2048,256]{1,0:T(8,128)(2,1)} %get-tuple-element.25), channel_id=1, source_target_pairs={{0,2},{2,4},{4,6},{6,0},{1,3},{3,5},{5,7},{7,1},{8,10},{10,12},{12... | collective-permute-start | bytes 3145736 | tf_op jit(solution)/shard_map/ppermute | solution.py:179
  39.8 61.4 %collective-permute-start.3 = (bf16[2048,256]{1,0:T(8,128)(2,1)}, bf16[2048,256]{1,0:T(8,128)(2,1)}, u32[]{:S(2)}, u32[]{:S(2)}) collective-permute-start(bf16[2048,256]{1,0:T(8,128)(2,1)} %get-tuple-element.24), channel_id=1, source_target_pairs={{0,6},{2,0},{4,2},{6,4},{1,7},{3,1},{5,3},{7,5},{8,14},{10,8},{12,... | collective-permute-start | bytes 3145736 | tf_op jit(solution)/shard_map/ppermute | solution.py:179
  102.2 180.7 %reduce-scatter.2.cloned.1.call-start = ((), (), s32[]{:S(2)}) async-start(), calls=%async_computation.6 | async-start | bytes 5570560 | tf_op jit(solution)/shard_map/reduce_scatter | solution.py:301
  103.9 27.7 %collective-permute-start.4 = (bf16[2048,256]{1,0:T(8,128)(2,1)S(1)}, bf16[2048,256]{1,0:T(8,128)(2,1)}, u32[]{:S(2)}, u32[]{:S(2)}) collective-permute-start(bf16[2048,256]{1,0:T(8,128)(2,1)S(1)} %get-tuple-element.23), channel_id=1, source_target_pairs={{0,2},{2,4},{4,6},{6,0},{1,3},{3,5},{5,7},{7,1},{8,10},{10,12},{12... | collective-permute-start | bytes 3145736 | tf_op jit(solution)/shard_map/ppermute | solution.py:179
  106.3 29.0 %collective-permute-start.5 = (bf16[2048,256]{1,0:T(8,128)(2,1)S(1)}, bf16[2048,256]{1,0:T(8,128)(2,1)}, u32[]{:S(2)}, u32[]{:S(2)}) collective-permute-start(bf16[2048,256]{1,0:T(8,128)(2,1)S(1)} %get-tuple-element.22), channel_id=1, source_target_pairs={{0,6},{2,0},{4,2},{6,4},{1,7},{3,1},{5,3},{7,5},{8,14},{10,8},{12,... | collective-permute-start | bytes 3145736 | tf_op jit(solution)/shard_map/ppermute | solution.py:179
  110.5 54.3 %collective-permute-start.8 = (bf16[4096,256]{1,0:T(8,128)(2,1)}, bf16[4096,256]{1,0:T(8,128)(2,1)}, u32[]{:S(2)}, u32[]{:S(2)}) collective-permute-start(bf16[4096,256]{1,0:T(8,128)(2,1)} %bitcast.8.refs_0_), channel_id=1, source_target_pairs={{0,1},{1,0},{2,3},{3,2},{4,5},{5,4},{6,7},{7,6},{8,9},{9,8},{10,11... | collective-permute-start | bytes 6291464 | tf_op jit(solution)/shard_map/ppermute | solution.py:183
  113.2 41.0 %collective-permute-start.6 = (bf16[2048,256]{1,0:T(8,128)(2,1)S(1)}, bf16[2048,256]{1,0:T(8,128)(2,1)}, u32[]{:S(2)}, u32[]{:S(2)}) collective-permute-start(bf16[2048,256]{1,0:T(8,128)(2,1)S(1)} %collective-permute-done.2.refs_1_), channel_id=1, source_target_pairs={{0,2},{2,4},{4,6},{6,0},{1,3},{3,5},{5,7},{7,1},{8,10},{10,12},{12... | collective-permute-start | bytes 3145736 | tf_op jit(solution)/shard_map/ppermute | solution.py:179
  115.1 42.0 %collective-permute-start.7 = (bf16[2048,256]{1,0:T(8,128)(2,1)}, bf16[2048,256]{1,0:T(8,128)(2,1)}, u32[]{:S(2)}, u32[]{:S(2)}) collective-permute-start(bf16[2048,256]{1,0:T(8,128)(2,1)} %collective-permute-done.3.refs_4_), channel_id=1, source_target_pairs={{0,6},{2,0},{4,2},{6,4},{1,7},{3,1},{5,3},{7,5},{8,14},{10,8},{12,... | collective-permute-start | bytes 3145736 | tf_op jit(solution)/shard_map/ppermute | solution.py:179
  131.7 27.4 %collective-permute-start.12 = (bf16[2048,256]{1,0:T(8,128)(2,1)}, bf16[2048,256]{1,0:T(8,128)(2,1)S(1)}, u32[]{:S(2)}, u32[]{:S(2)}) collective-permute-start(bf16[2048,256]{1,0:T(8,128)(2,1)} %collective-permute-done.3.refs_4_), channel_id=1, source_target_pairs={{0,1},{1,0},{2,3},{3,2},{4,5},{5,4},{6,7},{7,6},{8,9},{9,8},{10,11... | collective-permute-start | bytes 3145736 | tf_op jit(solution)/shard_map/ppermute | solution.py:183
  135.3 26.2 %collective-permute-start.9 = (bf16[2048,256]{1,0:T(8,128)(2,1)S(1)}, bf16[2048,256]{1,0:T(8,128)(2,1)S(1)}, u32[]{:S(2)}, u32[]{:S(2)}) collective-permute-start(bf16[2048,256]{1,0:T(8,128)(2,1)S(1)} %collective-permute-done.2.refs_1_), channel_id=1, source_target_pairs={{0,1},{1,0},{2,3},{3,2},{4,5},{5,4},{6,7},{7,6},{8,9},{9,8},{10,11... | collective-permute-start | bytes 3145736 | tf_op jit(solution)/shard_map/ppermute | solution.py:183
  154.1 10.6 %collective-permute-start.10 = (bf16[2048,256]{1,0:T(8,128)(2,1)}, bf16[2048,256]{1,0:T(8,128)(2,1)}, u32[]{:S(2)}, u32[]{:S(2)}) collective-permute-start(bf16[2048,256]{1,0:T(8,128)(2,1)} %collective-permute-done.4.refs_2_), channel_id=1, source_target_pairs={{0,1},{1,0},{2,3},{3,2},{4,5},{5,4},{6,7},{7,6},{8,9},{9,8},{10,11... | collective-permute-start | bytes 3145736 | tf_op jit(solution)/shard_map/ppermute | solution.py:183
  157.1 7.6 %collective-permute-start.11 = (bf16[2048,256]{1,0:T(8,128)(2,1)}, bf16[2048,256]{1,0:T(8,128)(2,1)}, u32[]{:S(2)}, u32[]{:S(2)}) collective-permute-start(bf16[2048,256]{1,0:T(8,128)(2,1)} %collective-permute-done.5.refs_3_), channel_id=1, source_target_pairs={{0,1},{1,0},{2,3},{3,2},{4,5},{5,4},{6,7},{7,6},{8,9},{9,8},{10,11... | collective-permute-start | bytes 3145736 | tf_op jit(solution)/shard_map/ppermute | solution.py:183
  159.1 2.4 copy-start.3
  159.1 5.7 %collective-permute-start.13 = (bf16[2048,256]{1,0:T(8,128)(2,1)}, bf16[2048,256]{1,0:T(8,128)(2,1)}, u32[]{:S(2)}, u32[]{:S(2)}) collective-permute-start(bf16[2048,256]{1,0:T(8,128)(2,1)} %collective-permute-done.6.refs_5_), channel_id=1, source_target_pairs={{0,1},{1,0},{2,3},{3,2},{4,5},{5,4},{6,7},{7,6},{8,9},{9,8},{10,11... | collective-permute-start | bytes 3145736 | tf_op jit(solution)/shard_map/ppermute | solution.py:183
  161.5 1.0 copy-start.1
  162.5 4.9 %collective-permute-start.14 = (bf16[2048,256]{1,0:T(8,128)(2,1)}, bf16[2048,256]{1,0:T(8,128)(2,1)}, u32[]{:S(2)}, u32[]{:S(2)}) collective-permute-start(bf16[2048,256]{1,0:T(8,128)(2,1)} %collective-permute-done.7.refs_6_), channel_id=1, source_target_pairs={{0,1},{1,0},{2,3},{3,2},{4,5},{5,4},{6,7},{7,6},{8,9},{9,8},{10,11... | collective-permute-start | bytes 3145736 | tf_op jit(solution)/shard_map/ppermute | solution.py:183
  178.5 1.2 copy-start.2
  206.0 0.7 copy-start.7
  285.0 28.0 %all-to-all-start.2 = ((bf16[32,10,512]{2,1,0:T(8,128)(2,1)}), bf16[32,10,512]{2,1,0:T(8,128)(2,1)S(1)}, u32[]{:S(2)}, u32[]{:S(2)}) async-start(bf16[32,10,512]{2,1,0:T(8,128)(2,1)} %copy.39), calls=%async_computation.3 | async-start | bytes 1048576 | tf_op jit(solution)/shard_map/all_to_all | solution.py:303
Sparse Core Ops, SparseCore 0:
  9.6 92.5 all-gather.2
  104.3 74.1 all-gather.4
  206.1 76.6 reduce-scatter.1
